TPU v7x, 32 devices: a whole 2x2x4 slice. The times are simulated.
32 devices in a mesh: grp: 2 (over y), seq: 4 (over z), head: 4 (over x, core).
Axes of the slice: x: 2, y: 2, z: 4, core: 2. Of those that a mesh axis runs over, the one named last changes fastest.
Arguments:
- queries: bfloat16 [8, 512, 2048], P('grp', 'seq', 'head'), parts along dimension 0, may hold values from -6 to 6
- keys: bfloat16 [8, 512, 2, 2048], P('grp', 'seq', None, 'head'), parts along dimension 0, may hold values from -6 to 6
- values: bfloat16 [8, 512, 2, 2048], P('grp', 'seq', None, 'head'), parts along dimension 0, may hold values from -6 to 6
- log_gate: float32 [8, 16, 512], P('grp', 'head', 'seq'), parts along dimension 0, may hold values from -1 to 0
- beta: float32 [8, 2, 16, 512], P('grp', None, 'head', 'seq'), parts along dimension 0, may hold values from 0 to 1
- resets: int32 [8, 3], P('grp'), parts along dimension 0, may hold values from 0 to 511
- w_out: bfloat16 [2048, 2048], P('head'), may hold values from -0.1875 to 0.1875
Outputs:
- layer_out: float32 [8, 512, 2048], P('grp', 'seq', 'head'), parts along dimension 0
There are 2 independent parts, one for each index of `grp`. A program takes and returns all parts, laid end to end along the dimension named above; an argument that names none is the same for every part. Nothing has to cross between parts.
All inputs are finite; a program needn't handle non-finite values.
Results may differ from a plain program's by a relative error of at most 0.0029.
Values sent between devices are 32-bit elements; how exact they have to be, the bound alone decides.
No kernel may reach another device: no remote copies, remote signals or barrier semaphores. Data moves between devices by JAX's collectives and lax.ppermute only.
A program may use at most 128 MiB of HBM per device.

v0:
```python
import functools

import jax
import jax.numpy as jnp
from jax import lax
from jax.experimental import pallas as pl
from jax.experimental.pallas import tpu as pltpu
from jax.sharding import PartitionSpec as P

epsilon = 1e-06
f32 = jnp.float32
bf16 = jnp.bfloat16


def mm(a, b):
    return lax.dot_general(a, b, (((1,), (0,)), ((), ())), preferred_element_type=f32)


def mm_nt(a, b):
    return lax.dot_general(a, b, (((1,), (1,)), ((), ())), preferred_element_type=f32)


def mm_tn(a, b):
    return lax.dot_general(a, b, (((0,), (0,)), ((), ())), preferred_element_type=f32)


def split(x):
    high = x.astype(bf16)
    return high, (x - high.astype(f32)).astype(bf16)


def split3(x):
    high, rest = x.astype(bf16), None
    rest = x - high.astype(f32)
    middle = rest.astype(bf16)
    return high, middle, (rest - middle.astype(f32)).astype(bf16)


def dot3(a, b):
    a_high, a_low = split(a)
    b_high, b_low = split(b)
    return mm(a_high, b_high) + (mm(a_low, b_high) + mm(a_high, b_low))


def iota(shape, axis):
    return lax.broadcasted_iota(jnp.int32, shape, axis)


def local_kernel(head_count, seq, offset_ref, resets_ref, q_ref, k_ref, v_ref, gate_ref, beta_ref,
                 transit_ref, filled_ref, reach_ref, own_ref):
    tok = q_ref.shape[1]
    size = q_ref.shape[2] // head_count
    keys = 2 * tok
    half = keys // 2
    heads = range(head_count)
    offset = offset_ref[0]
    reset = [resets_ref[seq, i] for i in range(resets_ref.shape[1])]

    def doc_of(position):
        total = jnp.zeros_like(position)
        for r in reset:
            total = total + (r <= position).astype(jnp.int32)
        return total

    start_doc = sum(((r < offset).astype(jnp.int32) for r in reset), jnp.int32(0))
    last_doc = sum(((r <= offset + tok - 1).astype(jnp.int32) for r in reset), jnp.int32(0))
    doc_row = doc_of(offset + (iota((1, keys), 1) >> 1))
    doc_col = doc_of(offset + (iota((keys, 1), 0) >> 1))
    doc_tok = doc_of(offset + iota((tok, 1), 0))

    gate3 = jnp.concatenate([p.astype(f32) for p in split3(gate_ref[0])], axis=0).astype(bf16)
    beta3 = [
        jnp.concatenate([p.astype(f32) for p in split3(beta_ref[0, j])], axis=0).astype(bf16)
        for j in range(2)
    ]
    key_i, tok_i = iota((keys, tok), 0), iota((keys, tok), 1)
    running = (tok_i <= (key_i >> 1)).astype(f32).astype(bf16)
    picks = [(key_i == 2 * tok_i + j).astype(f32).astype(bf16) for j in range(2)]
    running_tok = (iota((tok, tok), 1) <= iota((tok, tok), 0)).astype(f32).astype(bf16)

    def fold_col(m):
        n = head_count
        return m[:, :n] + m[:, n:2 * n] + m[:, 2 * n:3 * n]

    def fold_row(m):
        n = head_count
        return m[:n] + m[n:2 * n] + m[2 * n:3 * n]

    gs_col = fold_col(mm_nt(running, gate3))
    gs_row = fold_row(mm_nt(gate3, running))
    gs_tok = fold_col(mm_nt(running_tok, gate3))
    beta_col = fold_col(mm_nt(picks[0], beta3[0]) + mm_nt(picks[1], beta3[1]))
    beta_row = fold_row(mm_nt(beta3[0], picks[0]) + mm_nt(beta3[1], picks[1]))

    row_i, col_i = iota((keys, keys), 0), iota((keys, keys), 1)
    below = jnp.logical_and(row_i > col_i, doc_col == doc_row)
    eye_keys = row_i == col_i
    tok_linked = jnp.logical_and(
        (iota((tok, keys), 1) >> 1) <= iota((tok, keys), 0), doc_tok == doc_row
    )
    h_i, h_j = iota((half, half), 0), iota((half, half), 1)
    apart = jnp.where(h_i > h_j, h_i ^ h_j, 0)
    eye_half = (h_i == h_j).astype(f32)
    eye_size = (iota((size, size), 0) == iota((size, size), 1)).astype(f32)

    q = [q_ref[0, :, h * size:(h + 1) * size] for h in heads]
    k = [k_ref[0, :, h * size:(h + 1) * size] for h in heads]
    v = [v_ref[0, :, h * size:(h + 1) * size] for h in heads]

    gram = [mm_nt(k[h], k[h]) for h in heads]
    q_norm = []
    for h in heads:
        q32 = q[h].astype(f32)
        q_norm.append(lax.rsqrt(jnp.sum(q32 * q32, axis=1, keepdims=True) + epsilon))
    k_col, k_row, low = [], [], []
    for h in heads:
        diag = jnp.where(eye_keys, gram[h], 0.0)
        k_col.append(lax.rsqrt(jnp.sum(diag, axis=1, keepdims=True) + epsilon))
        k_row.append(lax.rsqrt(jnp.sum(diag, axis=0, keepdims=True) + epsilon))
        spread = gs_col[:, h:h + 1] - gs_row[h:h + 1]
        left = beta_col[:, h:h + 1] * k_col[h]
        low.append(jnp.where(below, gram[h] * jnp.exp(spread) * k_row[h] * left, 0.0))

    low16 = [split(low[h]) for h in heads]
    blocks = [(h, b) for h in heads for b in range(2)]
    part = {
        (h, b): low16[h][0][b * half:(b + 1) * half, b * half:(b + 1) * half] for h, b in blocks
    }
    inv = {}
    for key in blocks:
        inv[key] = (eye_half - jnp.where(apart == 1, part[key].astype(f32), 0.0)).astype(bf16)
    width = 2
    while width < half:
        mask = jnp.logical_and(apart >= width, apart < 2 * width)
        inner = {
            key: mm(jnp.where(mask, part[key].astype(f32), 0.0).astype(bf16), inv[key]).astype(bf16)
            for key in blocks
        }
        inv = {
            key: (inv[key].astype(f32) - mm(inv[key], inner[key])).astype(bf16) for key in blocks
        }
        width *= 2
    zeros = jnp.zeros((half, half), bf16)
    first = []
    for h in heads:
        inner = mm(low16[h][0][half:, :half], inv[h, 0]).astype(bf16)
        corner = (-mm(inv[h, 1], inner)).astype(bf16)
        first.append(
            jnp.concatenate(
                [
                    jnp.concatenate([inv[h, 0], zeros], axis=1),
                    jnp.concatenate([corner, inv[h, 1]], axis=1),
                ],
                axis=0,
            )
        )
    eye32 = eye_keys.astype(f32)
    solve = []
    for h in heads:
        rest = eye32 - first[h].astype(f32) - (mm(low16[h][0], first[h]) + mm(low16[h][1], first[h]))
        solve.append(first[h].astype(f32) + mm(first[h], rest.astype(bf16)))

    for h in heads:
        gr, gc, gt = gs_row[h:h + 1], gs_col[:, h:h + 1], gs_tok[:, h:h + 1]
        carried_row = jnp.where(doc_row == start_doc, jnp.exp(gr), 0.0)
        carried_tok = jnp.where(doc_tok == start_doc, jnp.exp(gt), 0.0)
        closing = jnp.where(doc_col == last_doc, jnp.exp(gr[:, keys - 1:] - gc), 0.0)
        b_row = beta_row[h:h + 1]
        w_high, w_low = split(solve[h] * (b_row * carried_row * k_row[h]))
        u_high, u_low = split(solve[h] * b_row)
        both = jnp.concatenate(
            [mm(w_high, k[h]) + mm(w_low, k[h]), mm(u_high, v[h]) + mm(u_low, v[h])], axis=1
        )
        end_high, end_low = split(both * (closing * k_col[h]))
        ends = mm_tn(k[h], end_high) + mm_tn(k[h], end_low)
        keep = carried_row[:, keys - 1:]
        transit_ref[h] = keep * eye_size - ends[:, :size]
        filled_ref[h] = ends[:, size:]
        probes = jnp.where(
            tok_linked, mm_nt(q[h], k[h]) * jnp.exp(gt - gr) * k_row[h] * q_norm[h], 0.0
        )
        outs = dot3(probes, both)
        reach_ref[h] = (carried_tok * q_norm[h]) * q[h].astype(f32) - outs[:, :size]
        own_ref[h] = outs[:, size:]


def local_terms(seq, offset, resets, queries, keys, values, log_gate, beta):
    _, tok, packed = queries.shape
    head_count = log_gate.shape[1]
    size = packed // head_count

    def block(shape):
        return pl.BlockSpec((1,) + shape, lambda i, o, r: (seq,) + (0,) * len(shape))

    whole = pl.BlockSpec((head_count, size, size), lambda i, o, r: (0, 0, 0))
    tall = pl.BlockSpec((head_count, tok, size), lambda i, o, r: (0, 0, 0))
    return pl.pallas_call(
        functools.partial(local_kernel, head_count, seq),
        grid_spec=pltpu.PrefetchScalarGridSpec(
            num_scalar_prefetch=2,
            grid=(1,),
            in_specs=[
                block((tok, packed)),
                block((2 * tok, packed)),
                block((2 * tok, packed)),
                block((head_count, tok)),
                block((2, head_count, tok)),
            ],
            out_specs=[whole, whole, tall, tall],
        ),
        out_shape=[
            jax.ShapeDtypeStruct((head_count, size, size), f32),
            jax.ShapeDtypeStruct((head_count, size, size), f32),
            jax.ShapeDtypeStruct((head_count, tok, size), f32),
            jax.ShapeDtypeStruct((head_count, tok, size), f32),
        ],
        compiler_params=pltpu.CompilerParams(vmem_limit_bytes=48 << 20),
        name="local_terms",
    )(offset, resets, queries, keys, values, log_gate, beta)


def step_kernel(map_ref, fill_ref, state_ref, out_ref):
    for h in range(map_ref.shape[0]):
        out_ref[h] = dot3(map_ref[h], state_ref[h]) + fill_ref[h]


def step(step_map, step_fill, state):
    return pl.pallas_call(
        step_kernel,
        out_shape=jax.ShapeDtypeStruct(state.shape, f32),
        name="state_step",
    )(step_map, step_fill, state)


def project_kernel(place_ref, reach_ref, own_ref, state_ref, w_ref, send_ref, keep_ref, head_ref):
    slot = pl.program_id(0)
    heads, _, size = reach_ref.shape

    @pl.when(slot == 0)
    def _():
        for h in range(heads):
            mixed = own_ref[h] + dot3(reach_ref[h], state_ref[h])
            head_ref[:, h * size:(h + 1) * size] = mixed.astype(bf16)

    share = mm(head_ref[...], w_ref[...])

    @pl.when(slot < pl.num_programs(0) // 2)
    def _():
        send_ref[0] = share

    @pl.when(slot >= pl.num_programs(0) // 2)
    def _():
        keep_ref[0] = share


def project(groups, place, reach, own, state, w_out):
    heads, tok, size = reach.shape
    rows, width = w_out.shape
    part = width // groups
    mid = groups // 2

    def of_slot(i, p):
        r = jnp.where(i < mid, 2 * i + 1, 2 * (i - mid))
        return (0, p[0] ^ r)

    whole = pl.BlockSpec((heads, tok, size), lambda i, p: (0, 0, 0))
    square = pl.BlockSpec((heads, size, size), lambda i, p: (0, 0, 0))
    return pl.pallas_call(
        project_kernel,
        grid_spec=pltpu.PrefetchScalarGridSpec(
            num_scalar_prefetch=1,
            grid=(groups,),
            in_specs=[whole, whole, square, pl.BlockSpec((rows, part), of_slot)],
            out_specs=[
                pl.BlockSpec((1, tok, part), lambda i, p: (jnp.minimum(i, mid - 1), 0, 0)),
                pl.BlockSpec((1, tok, part), lambda i, p: (jnp.maximum(i - mid, 0), 0, 0)),
            ],
            scratch_shapes=[pltpu.VMEM((tok, heads * size), bf16)],
        ),
        out_shape=[jax.ShapeDtypeStruct((mid, tok, part), f32)] * 2,
        name="project",
    )(place, reach, own, state, w_out)


def swapped(x, axis, bit):
    size = lax.axis_size(axis)
    return lax.ppermute(x, axis, [(i, i ^ bit) for i in range(size)])


def hop(x, source):
    return lax.ppermute(x, "seq", [(source, source + 1)])


def chain(step_map, step_fill):
    devices = lax.axis_size("seq")
    if devices <= 8:
        arrived = hop(step_fill, 0)
        total = arrived
        for source in range(1, devices - 1):
            arrived = hop(step(step_map, step_fill, arrived), source)
            total = total + arrived
        return total

    def turn(_, incoming):
        return lax.ppermute(
            step(step_map, step_fill, incoming), "seq", [(i, i + 1) for i in range(devices - 1)]
        )

    return lax.fori_loop(0, devices - 1, turn, jnp.zeros_like(step_fill))


def gathered(send, keep):
    bit = 1
    while True:
        keep = keep + swapped(send, "head", bit)
        if keep.shape[0] == 1:
            return keep[0]
        send, keep = keep[1::2], keep[0::2]
        bit *= 2


def shards(queries, keys, values, log_gate, beta, resets, w_out):
    seq_count, tok, packed = queries.shape
    groups = lax.axis_size("head")
    offset = (lax.axis_index("seq") * tok).astype(jnp.int32).reshape(1)
    place = lax.axis_index("head").astype(jnp.int32).reshape(1)
    key_rows = keys.reshape(seq_count, 2 * tok, packed)
    value_rows = values.reshape(seq_count, 2 * tok, packed)
    local = [
        local_terms(s, offset, resets, queries, key_rows, value_rows, log_gate, beta)
        for s in range(seq_count)
    ]
    states = [chain(local[s][0], local[s][1]) for s in range(seq_count)]
    outs = []
    for s in range(seq_count):
        send, keep = project(groups, place, local[s][2], local[s][3], states[s], w_out)
        outs.append(gathered(send, keep))
    return jnp.stack(outs)


def solution(mesh):
    placed = (
        P("grp", "seq", "head"),
        P("grp", "seq", None, "head"),
        P("grp", "seq", None, "head"),
        P("grp", "head", "seq"),
        P("grp", None, "head", "seq"),
        P("grp", None),
        P("head", None),
    )
    return jax.shard_map(
        shards, mesh=mesh, in_specs=placed, out_specs=P("grp", "seq", "head"), check_vma=False
    )
```

profile of v0, /device:TPU:22, one launch (start us, length us, event | category | flops | bytes accessed | tf_op | source)
XLA Modules:
  0.0 127.8 jit_solution(9218990773747504808)
XLA Ops:
  0.0 1.5 %reshape.14.k_ref = bf16[4,256,512]{2,1,0:T(8,128)(2,1)S(1)} reshape(bf16[4,128,2,512]{3,2,1,0:T(2,128)(2,1)} %param.8) | data formatting | bytes 2097152 | tf_op jit(solution)/shard_map/reshape | solution.py:327
  1.6 1.5 %reshape.15.v_ref = bf16[4,256,512]{2,1,0:T(8,128)(2,1)S(1)} reshape(bf16[4,128,2,512]{3,2,1,0:T(2,128)(2,1)} %param.9) | data formatting | bytes 2097152 | tf_op jit(solution)/shard_map/reshape | solution.py:328
  3.1 6.8 %local_terms.7 = (f32[4,128,128]{2,1,0:T(8,128)S(1)}, f32[4,128,128]{2,1,0:T(8,128)S(1)}, f32[4,128,128]{2,1,0:T(8,128)S(1)}, f32[4,128,128]{2,1,0:T(8,128)S(1)}) custom-call(s32[1]{0:T(128)} %bitcast.1.offset_ref, s32[4,3]{1,0:T(4,128)S(1)} %copy-done.19, bf16[4,128,512]{2,1,0:T(8,128)(2,1)S(1)} %copy-done, bf16[4,256,512]{2,1,0:T(8,128)(2,1)S(1)} %reshape.14.k_ref, ...), custom_call_target="tpu_custom_call" | custom-call | tf_op jit(solution)/shard_map/local_terms/pallas_call | solution.py:197
  10.5 0.7 copy-done.16
  11.3 0.7 copy-done.17
  12.7 6.8 %local_terms.6 = (f32[4,128,128]{2,1,0:T(8,128)S(1)}, f32[4,128,128]{2,1,0:T(8,128)S(1)}, f32[4,128,128]{2,1,0:T(8,128)S(1)}, f32[4,128,128]{2,1,0:T(8,128)S(1)}) custom-call(s32[1]{0:T(128)} %bitcast.1.offset_ref, s32[4,3]{1,0:T(4,128)S(1)} %copy-done.19, bf16[4,128,512]{2,1,0:T(8,128)(2,1)S(1)} %copy-done, bf16[4,256,512]{2,1,0:T(8,128)(2,1)S(1)} %reshape.14.k_ref, ...), custom_call_target="tpu_custom_call" | custom-call | tf_op jit(solution)/shard_map/local_terms/pallas_call | solution.py:197
  20.1 0.7 copy-done.14
  21.5 1.4 %collective-permute-start.10 = (f32[4,128,128]{2,1,0:T(8,128)S(1)}, f32[4,128,128]{2,1,0:T(8,128)}, u32[]{:S(2)}, u32[]{:S(2)}) collective-permute-start(f32[4,128,128]{2,1,0:T(8,128)S(1)} %get-tuple-element.43.fill_ref), channel_id=1, source_target_pairs={{0,4},{1,5},{2,6},{3,7},{16,20},{17,21},{18,22},{19,23}} | collective-permute-start | bytes 786440 | tf_op jit(solution)/shard_map/ppermute | solution.py:291
  22.9 6.8 %local_terms.5 = (f32[4,128,128]{2,1,0:T(8,128)S(1)}, f32[4,128,128]{2,1,0:T(8,128)S(1)}, f32[4,128,128]{2,1,0:T(8,128)S(1)}, f32[4,128,128]{2,1,0:T(8,128)S(1)}) custom-call(s32[1]{0:T(128)} %bitcast.1.offset_ref, s32[4,3]{1,0:T(4,128)S(1)} %copy-done.19, bf16[4,128,512]{2,1,0:T(8,128)(2,1)S(1)} %copy-done, bf16[4,256,512]{2,1,0:T(8,128)(2,1)S(1)} %reshape.14.k_ref, ...), custom_call_target="tpu_custom_call" | custom-call | tf_op jit(solution)/shard_map/local_terms/pallas_call | solution.py:197
  31.8 1.4 %collective-permute-start.5 = (f32[4,128,128]{2,1,0:T(8,128)S(1)}, f32[4,128,128]{2,1,0:T(8,128)}, u32[]{:S(2)}, u32[]{:S(2)}) collective-permute-start(f32[4,128,128]{2,1,0:T(8,128)S(1)} %get-tuple-element.37.fill_ref), channel_id=1, source_target_pairs={{0,4},{1,5},{2,6},{3,7},{16,20},{17,21},{18,22},{19,23}} | collective-permute-start | bytes 786440 | tf_op jit(solution)/shard_map/ppermute | solution.py:291
  33.2 6.7 %local_terms.4 = (f32[4,128,128]{2,1,0:T(8,128)S(1)}, f32[4,128,128]{2,1,0:T(8,128)S(1)}, f32[4,128,128]{2,1,0:T(8,128)S(1)}, f32[4,128,128]{2,1,0:T(8,128)S(1)}) custom-call(s32[1]{0:T(128)} %bitcast.1.offset_ref, s32[4,3]{1,0:T(4,128)S(1)} %copy-done.19, bf16[4,128,512]{2,1,0:T(8,128)(2,1)S(1)} %copy-done, bf16[4,256,512]{2,1,0:T(8,128)(2,1)S(1)} %reshape.14.k_ref, ...), custom_call_target="tpu_custom_call" | custom-call | tf_op jit(solution)/shard_map/local_terms/pallas_call | solution.py:197
  40.6 0.7 copy-done.10
  41.3 0.7 copy-done.11
  43.5 2.1 %state_step.14 = f32[4,128,128]{2,1,0:T(8,128)} custom-call(f32[4,128,128]{2,1,0:T(8,128)} %copy-done.7, f32[4,128,128]{2,1,0:T(8,128)} %copy-done.8, f32[4,128,128]{2,1,0:T(8,128)} %copy-done.22), custom_call_target="tpu_custom_call" | custom-call | tf_op jit(solution)/shard_map/state_step/pallas_call | solution.py:228
  45.5 1.3 %collective-permute-start.16 = (f32[4,128,128]{2,1,0:T(8,128)}, f32[4,128,128]{2,1,0:T(8,128)S(1)}, u32[]{:S(2)}, u32[]{:S(2)}) collective-permute-start(f32[4,128,128]{2,1,0:T(8,128)} %state_step.14), channel_id=1, source_target_pairs={{4,8},{5,9},{6,10},{7,11},{20,24},{21,25},{22,26},{23,27}} | collective-permute-start | bytes 786440 | tf_op jit(solution)/shard_map/ppermute | solution.py:291
  46.8 2.1 %state_step.12 = f32[4,128,128]{2,1,0:T(8,128)} custom-call(f32[4,128,128]{2,1,0:T(8,128)} %copy-done.5, f32[4,128,128]{2,1,0:T(8,128)} %copy-done.6, f32[4,128,128]{2,1,0:T(8,128)} %collective-permute-done.10.state_ref), custom_call_target="tpu_custom_call" | custom-call | tf_op jit(solution)/shard_map/state_step/pallas_call | solution.py:228
  48.9 1.3 %collective-permute-start.11 = (f32[4,128,128]{2,1,0:T(8,128)}, f32[4,128,128]{2,1,0:T(8,128)S(1)}, u32[]{:S(2)}, u32[]{:S(2)}) collective-permute-start(f32[4,128,128]{2,1,0:T(8,128)} %state_step.12), channel_id=1, source_target_pairs={{4,8},{5,9},{6,10},{7,11},{20,24},{21,25},{22,26},{23,27}} | collective-permute-start | bytes 786440 | tf_op jit(solution)/shard_map/ppermute | solution.py:291
  50.2 2.1 %state_step.10 = f32[4,128,128]{2,1,0:T(8,128)} custom-call(f32[4,128,128]{2,1,0:T(8,128)} %copy-done.3, f32[4,128,128]{2,1,0:T(8,128)} %copy-done.4, f32[4,128,128]{2,1,0:T(8,128)} %collective-permute-done.5.state_ref), custom_call_target="tpu_custom_call" | custom-call | tf_op jit(solution)/shard_map/state_step/pallas_call | solution.py:228
  52.3 1.3 %collective-permute-start.6 = (f32[4,128,128]{2,1,0:T(8,128)}, f32[4,128,128]{2,1,0:T(8,128)S(1)}, u32[]{:S(2)}, u32[]{:S(2)}) collective-permute-start(f32[4,128,128]{2,1,0:T(8,128)} %state_step.10), channel_id=1, source_target_pairs={{4,8},{5,9},{6,10},{7,11},{20,24},{21,25},{22,26},{23,27}} | collective-permute-start | bytes 786440 | tf_op jit(solution)/shard_map/ppermute | solution.py:291
  54.3 2.1 %state_step.8 = f32[4,128,128]{2,1,0:T(8,128)} custom-call(f32[4,128,128]{2,1,0:T(8,128)} %copy-done.1, f32[4,128,128]{2,1,0:T(8,128)} %copy-done.2, f32[4,128,128]{2,1,0:T(8,128)} %copy-done.20), custom_call_target="tpu_custom_call" | custom-call | tf_op jit(solution)/shard_map/state_step/pallas_call | solution.py:228
  56.4 1.4 %collective-permute-start.1 = (f32[4,128,128]{2,1,0:T(8,128)}, f32[4,128,128]{2,1,0:T(8,128)S(1)}, u32[]{:S(2)}, u32[]{:S(2)}) collective-permute-start(f32[4,128,128]{2,1,0:T(8,128)} %state_step.8), channel_id=1, source_target_pairs={{4,8},{5,9},{6,10},{7,11},{20,24},{21,25},{22,26},{23,27}} | collective-permute-start | bytes 786440 | tf_op jit(solution)/shard_map/ppermute | solution.py:291
  57.9 0.7 copy-done.30
  58.6 2.1 %state_step.15 = f32[4,128,128]{2,1,0:T(8,128)} custom-call(f32[4,128,128]{2,1,0:T(8,128)} %copy-done.7, f32[4,128,128]{2,1,0:T(8,128)} %copy-done.8, f32[4,128,128]{2,1,0:T(8,128)} %copy-done.30), custom_call_target="tpu_custom_call" | custom-call | tf_op jit(solution)/shard_map/state_step/pallas_call | solution.py:228
  60.7 1.4 %collective-permute-start.17 = (f32[4,128,128]{2,1,0:T(8,128)}, f32[4,128,128]{2,1,0:T(8,128)S(1)}, u32[]{:S(2)}, u32[]{:S(2)}) collective-permute-start(f32[4,128,128]{2,1,0:T(8,128)} %state_step.15), channel_id=1, source_target_pairs={{8,12},{9,13},{10,14},{11,15},{24,28},{25,29},{26,30},{27,31}} | collective-permute-start | bytes 786440 | tf_op jit(solution)/shard_map/ppermute | solution.py:291
  62.5 0.7 copy-done.28
  63.2 2.1 %state_step.13 = f32[4,128,128]{2,1,0:T(8,128)} custom-call(f32[4,128,128]{2,1,0:T(8,128)} %copy-done.5, f32[4,128,128]{2,1,0:T(8,128)} %copy-done.6, f32[4,128,128]{2,1,0:T(8,128)} %copy-done.28), custom_call_target="tpu_custom_call" | custom-call | tf_op jit(solution)/shard_map/state_step/pallas_call | solution.py:228
  65.2 1.5 %collective-permute-start.12 = (f32[4,128,128]{2,1,0:T(8,128)}, f32[4,128,128]{2,1,0:T(8,128)S(1)}, u32[]{:S(2)}, u32[]{:S(2)}) collective-permute-start(f32[4,128,128]{2,1,0:T(8,128)} %state_step.13), channel_id=1, source_target_pairs={{8,12},{9,13},{10,14},{11,15},{24,28},{25,29},{26,30},{27,31}} | collective-permute-start | bytes 786440 | tf_op jit(solution)/shard_map/ppermute | solution.py:291
  66.8 1.3 %collective-permute-done.6.state_ref = f32[4,128,128]{2,1,0:T(8,128)S(1)} collective-permute-done((f32[4,128,128]{2,1,0:T(8,128)}, f32[4,128,128]{2,1,0:T(8,128)S(1)}, u32[]{:S(2)}, u32[]{:S(2)}) %collective-permute-start.6) | collective-permute-done | bytes 262176 | tf_op jit(solution)/shard_map/ppermute | solution.py:291
  68.1 0.7 copy-done.26
  68.8 2.1 %state_step.11 = f32[4,128,128]{2,1,0:T(8,128)} custom-call(f32[4,128,128]{2,1,0:T(8,128)} %copy-done.3, f32[4,128,128]{2,1,0:T(8,128)} %copy-done.4, f32[4,128,128]{2,1,0:T(8,128)} %copy-done.26), custom_call_target="tpu_custom_call" | custom-call | tf_op jit(solution)/shard_map/state_step/pallas_call | solution.py:228
  70.9 1.3 %collective-permute-start.7 = (f32[4,128,128]{2,1,0:T(8,128)}, f32[4,128,128]{2,1,0:T(8,128)S(1)}, u32[]{:S(2)}, u32[]{:S(2)}) collective-permute-start(f32[4,128,128]{2,1,0:T(8,128)} %state_step.11), channel_id=1, source_target_pairs={{8,12},{9,13},{10,14},{11,15},{24,28},{25,29},{26,30},{27,31}} | collective-permute-start | bytes 786440 | tf_op jit(solution)/shard_map/ppermute | solution.py:291
  73.2 2.1 %state_step.9 = f32[4,128,128]{2,1,0:T(8,128)} custom-call(f32[4,128,128]{2,1,0:T(8,128)} %copy-done.1, f32[4,128,128]{2,1,0:T(8,128)} %copy-done.2, f32[4,128,128]{2,1,0:T(8,128)} %copy-done.24), custom_call_target="tpu_custom_call" | custom-call | tf_op jit(solution)/shard_map/state_step/pallas_call | solution.py:228
  75.3 1.4 %collective-permute-start.2 = (f32[4,128,128]{2,1,0:T(8,128)}, f32[4,128,128]{2,1,0:T(8,128)S(1)}, u32[]{:S(2)}, u32[]{:S(2)}) collective-permute-start(f32[4,128,128]{2,1,0:T(8,128)} %state_step.9), channel_id=1, source_target_pairs={{8,12},{9,13},{10,14},{11,15},{24,28},{25,29},{26,30},{27,31}} | collective-permute-start | bytes 786440 | tf_op jit(solution)/shard_map/ppermute | solution.py:291
  76.8 0.8 add_add_fusion.state_ref
  77.6 4.6 %project.7 = (f32[2,128,512]{2,1,0:T(8,128)}, f32[2,128,512]{2,1,0:T(8,128)}) custom-call(s32[1]{0:T(128)} %bitcast.place_ref, f32[4,128,128]{2,1,0:T(8,128)} %copy-done.16, f32[4,128,128]{2,1,0:T(8,128)} %copy-done.17, f32[4,128,128]{2,1,0:T(8,128)} %add_add_fusion.state_ref, bf16[512,2048]{1,0:T(8,128)(2,1)} %w_ref.7), custom_call_target="tpu_custom_call" | custom-call | tf_op jit(solution)/shard_map/project/pallas_call | solution.py:268
  82.2 1.8 %add_add_fusion.1.state_ref = f32[4,128,128]{2,1,0:T(8,128)} fusion(f32[4,128,128]{2,1,0:T(8,128)S(1)} %collective-permute-done.12, f32[4,128,128]{2,1,0:T(8,128)} %collective-permute-done.10.state_ref, f32[4,128,128]{2,1,0:T(8,128)S(1)} %copy-done.29), kind=kLoop, calls=%fused_computation.6 | loop fusion | flops 131072 | bytes 1048576 | tf_op jit(solution)/shard_map/add | solution.py:301
  83.9 4.7 %project.6 = (f32[2,128,512]{2,1,0:T(8,128)}, f32[2,128,512]{2,1,0:T(8,128)}) custom-call(s32[1]{0:T(128)} %bitcast.place_ref, f32[4,128,128]{2,1,0:T(8,128)} %copy-done.14, f32[4,128,128]{2,1,0:T(8,128)} %copy-done.15, f32[4,128,128]{2,1,0:T(8,128)} %add_add_fusion.1.state_ref, bf16[512,2048]{1,0:T(8,128)(2,1)} %w_ref.7), custom_call_target="tpu_custom_call" | custom-call | tf_op jit(solution)/shard_map/project/pallas_call | solution.py:268
  89.1 1.7 %add_add_fusion.2.state_ref = f32[4,128,128]{2,1,0:T(8,128)} fusion(f32[4,128,128]{2,1,0:T(8,128)S(1)} %collective-permute-done.7, f32[4,128,128]{2,1,0:T(8,128)} %collective-permute-done.5.state_ref, f32[4,128,128]{2,1,0:T(8,128)S(1)} %copy-done.27), kind=kLoop, calls=%fused_computation.7 | loop fusion | flops 131072 | bytes 1048576 | tf_op jit(solution)/shard_map/add | solution.py:301
  90.8 4.6 %project.5 = (f32[2,128,512]{2,1,0:T(8,128)}, f32[2,128,512]{2,1,0:T(8,128)}) custom-call(s32[1]{0:T(128)} %bitcast.place_ref, f32[4,128,128]{2,1,0:T(8,128)} %copy-done.12, f32[4,128,128]{2,1,0:T(8,128)} %copy-done.13, f32[4,128,128]{2,1,0:T(8,128)} %add_add_fusion.2.state_ref, bf16[512,2048]{1,0:T(8,128)(2,1)} %w_ref.7), custom_call_target="tpu_custom_call" | custom-call | tf_op jit(solution)/shard_map/project/pallas_call | solution.py:268
  95.5 0.7 add_add_fusion.3.state_ref
  96.3 4.7 %project.4 = (f32[2,128,512]{2,1,0:T(8,128)}, f32[2,128,512]{2,1,0:T(8,128)}) custom-call(s32[1]{0:T(128)} %bitcast.place_ref, f32[4,128,128]{2,1,0:T(8,128)} %copy-done.10, f32[4,128,128]{2,1,0:T(8,128)} %copy-done.11, f32[4,128,128]{2,1,0:T(8,128)} %add_add_fusion.3.state_ref, bf16[512,2048]{1,0:T(8,128)(2,1)} %w_ref.7), custom_call_target="tpu_custom_call" | custom-call | tf_op jit(solution)/shard_map/project/pallas_call | solution.py:268
  102.2 1.6 %collective-permute-start.14 = (f32[1,128,512]{2,1,0:T(8,128)S(1)}, f32[1,128,512]{2,1,0:T(8,128)S(1)}, u32[]{:S(2)}, u32[]{:S(2)}) collective-permute-start(f32[1,128,512]{2,1,0:T(8,128)S(1)} %slice.45), channel_id=1, source_target_pairs={{0,2},{1,3},{2,0},{3,1},{4,6},{5,7},{6,4},{7,5},{8,10},{9,11},{10,... | collective-permute-start | bytes 786440 | tf_op jit(solution)/shard_map/ppermute | solution.py:287
  104.6 1.6 %collective-permute-start.4 = (f32[1,128,512]{2,1,0:T(8,128)S(1)}, f32[1,128,512]{2,1,0:T(8,128)S(1)}, u32[]{:S(2)}, u32[]{:S(2)}) collective-permute-start(f32[1,128,512]{2,1,0:T(8,128)S(1)} %slice.41), channel_id=1, source_target_pairs={{0,2},{1,3},{2,0},{3,1},{4,6},{5,7},{6,4},{7,5},{8,10},{9,11},{10,... | collective-permute-start | bytes 786440 | tf_op jit(solution)/shard_map/ppermute | solution.py:287
  106.2 4.6 %collective-permute-done.19 = f32[1,128,512]{2,1,0:T(8,128)S(1)} collective-permute-done((f32[1,128,512]{2,1,0:T(8,128)S(1)}, f32[1,128,512]{2,1,0:T(8,128)S(1)}, u32[]{:S(2)}, u32[]{:S(2)}) %collective-permute-start.19) | collective-permute-done | bytes 262176 | tf_op jit(solution)/shard_map/ppermute | solution.py:287
  110.8 5.6 %collective-permute-done.14 = f32[1,128,512]{2,1,0:T(8,128)S(1)} collective-permute-done((f32[1,128,512]{2,1,0:T(8,128)S(1)}, f32[1,128,512]{2,1,0:T(8,128)S(1)}, u32[]{:S(2)}, u32[]{:S(2)}) %collective-permute-start.14) | collective-permute-done | bytes 262176 | tf_op jit(solution)/shard_map/ppermute | solution.py:287
  116.4 5.6 %collective-permute-done.9 = f32[1,128,512]{2,1,0:T(8,128)S(1)} collective-permute-done((f32[1,128,512]{2,1,0:T(8,128)S(1)}, f32[1,128,512]{2,1,0:T(8,128)S(1)}, u32[]{:S(2)}, u32[]{:S(2)}) %collective-permute-start.9) | collective-permute-done | bytes 262176 | tf_op jit(solution)/shard_map/ppermute | solution.py:287
  122.0 4.7 %collective-permute-done.4 = f32[1,128,512]{2,1,0:T(8,128)S(1)} collective-permute-done((f32[1,128,512]{2,1,0:T(8,128)S(1)}, f32[1,128,512]{2,1,0:T(8,128)S(1)}, u32[]{:S(2)}, u32[]{:S(2)}) %collective-permute-start.4) | collective-permute-done | bytes 262176 | tf_op jit(solution)/shard_map/ppermute | solution.py:287
  126.7 1.1 pad_maximum_fusion
  (99 shorter events, 11.9 us)
Async XLA Ops:
  0.0 3.0 %copy-start = (bf16[4,128,512]{2,1,0:T(8,128)(2,1)S(1)}, bf16[4,128,512]{2,1,0:T(8,128)(2,1)}, u32[]{:S(2)}) copy-start(bf16[4,128,512]{2,1,0:T(8,128)(2,1)} %q_ref.7) | copy-start | bytes 1572868
  0.0 3.0 %copy-start.9 = (f32[4,2,4,128]{3,2,1,0:T(4,128)S(1)}, f32[4,2,4,128]{3,2,1,0:T(4,128)}, u32[]{:S(2)}) copy-start(f32[4,2,4,128]{3,2,1,0:T(4,128)} %beta_ref.7) | copy-start | bytes 49156
  0.0 3.1 %copy-start.18 = (f32[4,4,128]{2,1,0:T(4,128)S(1)}, f32[4,4,128]{2,1,0:T(4,128)}, u32[]{:S(2)}) copy-start(f32[4,4,128]{2,1,0:T(4,128)} %gate_ref.7) | copy-start | bytes 24580
  0.0 3.1 %copy-start.19 = (s32[4,3]{1,0:T(4,128)S(1)}, s32[4,3]{1,0:T(4,128)}, u32[]{:S(2)}) copy-start(s32[4,3]{1,0:T(4,128)} %resets_ref.7) | copy-start | bytes 148
  10.5 0.7 copy-start.16
  11.3 0.7 copy-start.17
  12.0 17.7 %copy-start.8 = (f32[4,128,128]{2,1,0:T(8,128)}, f32[4,128,128]{2,1,0:T(8,128)S(1)}, u32[]{:S(2)}) copy-start(f32[4,128,128]{2,1,0:T(8,128)S(1)} %get-tuple-element.49.fill_ref) | copy-start | bytes 786436
  12.0 30.8 %collective-permute-start.15 = (f32[4,128,128]{2,1,0:T(8,128)S(1)}, f32[4,128,128]{2,1,0:T(8,128)S(1)}, u32[]{:S(2)}, u32[]{:S(2)}) collective-permute-start(f32[4,128,128]{2,1,0:T(8,128)S(1)} %get-tuple-element.49.fill_ref), channel_id=1, source_target_pairs={{0,4},{1,5},{2,6},{3,7},{16,20},{17,21},{18,22},{19,23}} | collective-permute-start | bytes 786440 | tf_op jit(solution)/shard_map/ppermute | solution.py:291
  20.1 0.7 copy-start.14
  21.5 18.4 %copy-start.6 = (f32[4,128,128]{2,1,0:T(8,128)}, f32[4,128,128]{2,1,0:T(8,128)S(1)}, u32[]{:S(2)}) copy-start(f32[4,128,128]{2,1,0:T(8,128)S(1)} %get-tuple-element.43.fill_ref) | copy-start | bytes 786436
  21.5 25.3 %collective-permute-start.10 = (f32[4,128,128]{2,1,0:T(8,128)S(1)}, f32[4,128,128]{2,1,0:T(8,128)}, u32[]{:S(2)}, u32[]{:S(2)}) collective-permute-start(f32[4,128,128]{2,1,0:T(8,128)S(1)} %get-tuple-element.43.fill_ref), channel_id=1, source_target_pairs={{0,4},{1,5},{2,6},{3,7},{16,20},{17,21},{18,22},{19,23}} | collective-permute-start | bytes 786440 | tf_op jit(solution)/shard_map/ppermute | solution.py:291
  31.8 17.1 %copy-start.4 = (f32[4,128,128]{2,1,0:T(8,128)}, f32[4,128,128]{2,1,0:T(8,128)S(1)}, u32[]{:S(2)}) copy-start(f32[4,128,128]{2,1,0:T(8,128)S(1)} %get-tuple-element.37.fill_ref) | copy-start | bytes 786436
  31.8 18.4 %collective-permute-start.5 = (f32[4,128,128]{2,1,0:T(8,128)S(1)}, f32[4,128,128]{2,1,0:T(8,128)}, u32[]{:S(2)}, u32[]{:S(2)}) collective-permute-start(f32[4,128,128]{2,1,0:T(8,128)S(1)} %get-tuple-element.37.fill_ref), channel_id=1, source_target_pairs={{0,4},{1,5},{2,6},{3,7},{16,20},{17,21},{18,22},{19,23}} | collective-permute-start | bytes 786440 | tf_op jit(solution)/shard_map/ppermute | solution.py:291
  39.9 0.7 copy-start.1
  40.6 0.7 copy-start.10
  41.3 0.7 copy-start.11
  42.1 11.6 %copy-start.2 = (f32[4,128,128]{2,1,0:T(8,128)}, f32[4,128,128]{2,1,0:T(8,128)S(1)}, u32[]{:S(2)}) copy-start(f32[4,128,128]{2,1,0:T(8,128)S(1)} %get-tuple-element.31.fill_ref) | copy-start | bytes 786436
  42.1 11.6 %collective-permute-start = (f32[4,128,128]{2,1,0:T(8,128)S(1)}, f32[4,128,128]{2,1,0:T(8,128)S(1)}, u32[]{:S(2)}, u32[]{:S(2)}) collective-permute-start(f32[4,128,128]{2,1,0:T(8,128)S(1)} %get-tuple-element.31.fill_ref), channel_id=1, source_target_pairs={{0,4},{1,5},{2,6},{3,7},{16,20},{17,21},{18,22},{19,23}} | collective-permute-start | bytes 786440 | tf_op jit(solution)/shard_map/ppermute | solution.py:291
  42.7 0.7 copy-start.22
  45.5 12.3 %collective-permute-start.16 = (f32[4,128,128]{2,1,0:T(8,128)}, f32[4,128,128]{2,1,0:T(8,128)S(1)}, u32[]{:S(2)}, u32[]{:S(2)}) collective-permute-start(f32[4,128,128]{2,1,0:T(8,128)} %state_step.14), channel_id=1, source_target_pairs={{4,8},{5,9},{6,10},{7,11},{20,24},{21,25},{22,26},{23,27}} | collective-permute-start | bytes 786440 | tf_op jit(solution)/shard_map/ppermute | solution.py:291
  48.9 13.5 %collective-permute-start.11 = (f32[4,128,128]{2,1,0:T(8,128)}, f32[4,128,128]{2,1,0:T(8,128)S(1)}, u32[]{:S(2)}, u32[]{:S(2)}) collective-permute-start(f32[4,128,128]{2,1,0:T(8,128)} %state_step.12), channel_id=1, source_target_pairs={{4,8},{5,9},{6,10},{7,11},{20,24},{21,25},{22,26},{23,27}} | collective-permute-start | bytes 786440 | tf_op jit(solution)/shard_map/ppermute | solution.py:291
  52.3 15.7 %collective-permute-start.6 = (f32[4,128,128]{2,1,0:T(8,128)}, f32[4,128,128]{2,1,0:T(8,128)S(1)}, u32[]{:S(2)}, u32[]{:S(2)}) collective-permute-start(f32[4,128,128]{2,1,0:T(8,128)} %state_step.10), channel_id=1, source_target_pairs={{4,8},{5,9},{6,10},{7,11},{20,24},{21,25},{22,26},{23,27}} | collective-permute-start | bytes 786440 | tf_op jit(solution)/shard_map/ppermute | solution.py:291
  56.4 20.4 %copy-start.23 = (f32[4,128,128]{2,1,0:T(8,128)S(1)}, f32[4,128,128]{2,1,0:T(8,128)}, u32[]{:S(2)}) copy-start(f32[4,128,128]{2,1,0:T(8,128)} %copy-done.22) | copy-start | bytes 786436
  56.4 16.1 %collective-permute-start.1 = (f32[4,128,128]{2,1,0:T(8,128)}, f32[4,128,128]{2,1,0:T(8,128)S(1)}, u32[]{:S(2)}, u32[]{:S(2)}) collective-permute-start(f32[4,128,128]{2,1,0:T(8,128)} %state_step.8), channel_id=1, source_target_pairs={{4,8},{5,9},{6,10},{7,11},{20,24},{21,25},{22,26},{23,27}} | collective-permute-start | bytes 786440 | tf_op jit(solution)/shard_map/ppermute | solution.py:291
  57.8 0.7 copy-start.30
  60.7 16.1 %copy-start.31 = (f32[4,128,128]{2,1,0:T(8,128)S(1)}, f32[4,128,128]{2,1,0:T(8,128)}, u32[]{:S(2)}) copy-start(f32[4,128,128]{2,1,0:T(8,128)} %copy-done.30) | copy-start | bytes 786436
  60.7 16.1 %collective-permute-start.17 = (f32[4,128,128]{2,1,0:T(8,128)}, f32[4,128,128]{2,1,0:T(8,128)S(1)}, u32[]{:S(2)}, u32[]{:S(2)}) collective-permute-start(f32[4,128,128]{2,1,0:T(8,128)} %state_step.15), channel_id=1, source_target_pairs={{8,12},{9,13},{10,14},{11,15},{24,28},{25,29},{26,30},{27,31}} | collective-permute-start | bytes 786440 | tf_op jit(solution)/shard_map/ppermute | solution.py:291
  62.4 0.7 copy-start.28
  65.2 16.9 %collective-permute-start.12 = (f32[4,128,128]{2,1,0:T(8,128)}, f32[4,128,128]{2,1,0:T(8,128)S(1)}, u32[]{:S(2)}, u32[]{:S(2)}) collective-permute-start(f32[4,128,128]{2,1,0:T(8,128)} %state_step.13), channel_id=1, source_target_pairs={{8,12},{9,13},{10,14},{11,15},{24,28},{25,29},{26,30},{27,31}} | collective-permute-start | bytes 786440 | tf_op jit(solution)/shard_map/ppermute | solution.py:291
  68.1 0.7 copy-start.26
  70.9 18.2 %collective-permute-start.7 = (f32[4,128,128]{2,1,0:T(8,128)}, f32[4,128,128]{2,1,0:T(8,128)S(1)}, u32[]{:S(2)}, u32[]{:S(2)}) collective-permute-start(f32[4,128,128]{2,1,0:T(8,128)} %state_step.11), channel_id=1, source_target_pairs={{8,12},{9,13},{10,14},{11,15},{24,28},{25,29},{26,30},{27,31}} | collective-permute-start | bytes 786440 | tf_op jit(solution)/shard_map/ppermute | solution.py:291
  75.3 6.8 %copy-start.29 = (f32[4,128,128]{2,1,0:T(8,128)S(1)}, f32[4,128,128]{2,1,0:T(8,128)}, u32[]{:S(2)}) copy-start(f32[4,128,128]{2,1,0:T(8,128)} %copy-done.28) | copy-start | bytes 786436
  75.3 20.2 %collective-permute-start.2 = (f32[4,128,128]{2,1,0:T(8,128)}, f32[4,128,128]{2,1,0:T(8,128)S(1)}, u32[]{:S(2)}, u32[]{:S(2)}) collective-permute-start(f32[4,128,128]{2,1,0:T(8,128)} %state_step.9), channel_id=1, source_target_pairs={{8,12},{9,13},{10,14},{11,15},{24,28},{25,29},{26,30},{27,31}} | collective-permute-start | bytes 786440 | tf_op jit(solution)/shard_map/ppermute | solution.py:291
  82.1 7.0 %copy-start.27 = (f32[4,128,128]{2,1,0:T(8,128)S(1)}, f32[4,128,128]{2,1,0:T(8,128)}, u32[]{:S(2)}) copy-start(f32[4,128,128]{2,1,0:T(8,128)} %copy-done.26) | copy-start | bytes 786436
  82.1 19.2 %collective-permute-start.18 = (f32[2,128,512]{2,1,0:T(8,128)}, f32[2,128,512]{2,1,0:T(8,128)S(1)}, u32[]{:S(2)}, u32[]{:S(2)}) collective-permute-start(f32[2,128,512]{2,1,0:T(8,128)} %get-tuple-element.52), channel_id=1, source_target_pairs={{0,1},{1,0},{2,3},{3,2},{4,5},{5,4},{6,7},{7,6},{8,9},{9,8},{10,11... | collective-permute-start | bytes 1572872 | tf_op jit(solution)/shard_map/ppermute | solution.py:287
  88.6 6.9 %copy-start.21 = (f32[4,128,128]{2,1,0:T(8,128)S(1)}, f32[4,128,128]{2,1,0:T(8,128)}, u32[]{:S(2)}) copy-start(f32[4,128,128]{2,1,0:T(8,128)} %copy-done.20) | copy-start | bytes 786436
  88.6 6.9 %copy-start.25 = (f32[4,128,128]{2,1,0:T(8,128)S(1)}, f32[4,128,128]{2,1,0:T(8,128)}, u32[]{:S(2)}) copy-start(f32[4,128,128]{2,1,0:T(8,128)} %copy-done.24) | copy-start | bytes 786436
  88.6 13.5 %collective-permute-start.13 = (f32[2,128,512]{2,1,0:T(8,128)}, f32[2,128,512]{2,1,0:T(8,128)S(1)}, u32[]{:S(2)}, u32[]{:S(2)}) collective-permute-start(f32[2,128,512]{2,1,0:T(8,128)} %get-tuple-element.46), channel_id=1, source_target_pairs={{0,1},{1,0},{2,3},{3,2},{4,5},{5,4},{6,7},{7,6},{8,9},{9,8},{10,11... | collective-permute-start | bytes 1572872 | tf_op jit(solution)/shard_map/ppermute | solution.py:287
  95.4 5.9 %copy-start.32 = (f32[2,128,512]{2,1,0:T(8,128)S(1)}, f32[2,128,512]{2,1,0:T(8,128)}, u32[]{:S(2)}) copy-start(f32[2,128,512]{2,1,0:T(8,128)} %get-tuple-element.51) | copy-start | bytes 1572868
  95.4 8.3 %collective-permute-start.8 = (f32[2,128,512]{2,1,0:T(8,128)}, f32[2,128,512]{2,1,0:T(8,128)S(1)}, u32[]{:S(2)}, u32[]{:S(2)}) collective-permute-start(f32[2,128,512]{2,1,0:T(8,128)} %get-tuple-element.40), channel_id=1, source_target_pairs={{0,1},{1,0},{2,3},{3,2},{4,5},{5,4},{6,7},{7,6},{8,9},{9,8},{10,11... | collective-permute-start | bytes 1572872 | tf_op jit(solution)/shard_map/ppermute | solution.py:287
  96.3 5.8 %copy-start.33 = (f32[2,128,512]{2,1,0:T(8,128)S(1)}, f32[2,128,512]{2,1,0:T(8,128)}, u32[]{:S(2)}) copy-start(f32[2,128,512]{2,1,0:T(8,128)} %get-tuple-element.45) | copy-start | bytes 1572868
  100.9 3.5 %collective-permute-start.3 = (f32[2,128,512]{2,1,0:T(8,128)}, f32[2,128,512]{2,1,0:T(8,128)S(1)}, u32[]{:S(2)}, u32[]{:S(2)}) collective-permute-start(f32[2,128,512]{2,1,0:T(8,128)} %get-tuple-element.34), channel_id=1, source_target_pairs={{0,1},{1,0},{2,3},{3,2},{4,5},{5,4},{6,7},{7,6},{8,9},{9,8},{10,11... | collective-permute-start | bytes 1572872 | tf_op jit(solution)/shard_map/ppermute | solution.py:287
  101.4 2.4 %copy-start.34 = (f32[2,128,512]{2,1,0:T(8,128)S(1)}, f32[2,128,512]{2,1,0:T(8,128)}, u32[]{:S(2)}) copy-start(f32[2,128,512]{2,1,0:T(8,128)} %get-tuple-element.39) | copy-start | bytes 1572868
  101.5 9.2 %collective-permute-start.19 = (f32[1,128,512]{2,1,0:T(8,128)S(1)}, f32[1,128,512]{2,1,0:T(8,128)S(1)}, u32[]{:S(2)}, u32[]{:S(2)}) collective-permute-start(f32[1,128,512]{2,1,0:T(8,128)S(1)} %slice.47), channel_id=1, source_target_pairs={{0,2},{1,3},{2,0},{3,1},{4,6},{5,7},{6,4},{7,5},{8,10},{9,11},{10,... | collective-permute-start | bytes 786440 | tf_op jit(solution)/shard_map/ppermute | solution.py:287
  102.1 2.4 %copy-start.35 = (f32[2,128,512]{2,1,0:T(8,128)S(1)}, f32[2,128,512]{2,1,0:T(8,128)}, u32[]{:S(2)}) copy-start(f32[2,128,512]{2,1,0:T(8,128)} %get-tuple-element.33) | copy-start | bytes 1572868
  102.2 14.1 %collective-permute-start.14 = (f32[1,128,512]{2,1,0:T(8,128)S(1)}, f32[1,128,512]{2,1,0:T(8,128)S(1)}, u32[]{:S(2)}, u32[]{:S(2)}) collective-permute-start(f32[1,128,512]{2,1,0:T(8,128)S(1)} %slice.45), channel_id=1, source_target_pairs={{0,2},{1,3},{2,0},{3,1},{4,6},{5,7},{6,4},{7,5},{8,10},{9,11},{10,... | collective-permute-start | bytes 786440 | tf_op jit(solution)/shard_map/ppermute | solution.py:287
  103.9 18.1 %collective-permute-start.9 = (f32[1,128,512]{2,1,0:T(8,128)S(1)}, f32[1,128,512]{2,1,0:T(8,128)S(1)}, u32[]{:S(2)}, u32[]{:S(2)}) collective-permute-start(f32[1,128,512]{2,1,0:T(8,128)S(1)} %slice.43), channel_id=1, source_target_pairs={{0,2},{1,3},{2,0},{3,1},{4,6},{5,7},{6,4},{7,5},{8,10},{9,11},{10,... | collective-permute-start | bytes 786440 | tf_op jit(solution)/shard_map/ppermute | solution.py:287
  104.6 22.1 %collective-permute-start.4 = (f32[1,128,512]{2,1,0:T(8,128)S(1)}, f32[1,128,512]{2,1,0:T(8,128)S(1)}, u32[]{:S(2)}, u32[]{:S(2)}) collective-permute-start(f32[1,128,512]{2,1,0:T(8,128)S(1)} %slice.41), channel_id=1, source_target_pairs={{0,2},{1,3},{2,0},{3,1},{4,6},{5,7},{6,4},{7,5},{8,10},{9,11},{10,... | collective-permute-start | bytes 786440 | tf_op jit(solution)/shard_map/ppermute | solution.py:287
  (8 other events, 5.6 us)
where the time goes:
time: 129 us; the launch traced here: 128 us
  Pallas kernels  62.2 us (48%)
  waiting for transfers between devices  22.5 us (17%)
  starting transfers between devices  20.3 us (16%)
  local copies, waits for them, and re-layouts  15.9 us (12%)
  other arithmetic  6.5 us (5%)
    pallas_call x4, Pallas kernels, local_terms(): pl.pallas_call(functools.partial(local_kernel, head_count, seq), grid_spe...  27 us
    ppermute x8, waiting for transfers between devices, swapped(): return lax.ppermute(x, axis, [(i, i ^ bit) for i in range(size)])  20.4 us
    pallas_call x4, Pallas kernels, project(): pl.pallas_call(project_kernel, grid_spec=pltpu.PrefetchScalarGridSpec(num...  18.5 us
    pallas_call x8, Pallas kernels, step(): pl.pallas_call(step_kernel, out_shape=jax.ShapeDtypeStruct(state.shape, f...  16.7 us
    ppermute x12, starting transfers between devices, hop(): return lax.ppermute(x, 'seq', [(source, source + 1)])  15 us
    unnamed x72, local copies, waits for them, and re-layouts  12.8 us
    ppermute x8, starting transfers between devices, swapped(): return lax.ppermute(x, axis, [(i, i ^ bit) for i in range(size)])  5.34 us
    add x4, other arithmetic, chain(): total = total + arrived  4.95 us
  transfers between devices with their start and end apart: 20, of which 7 were waited for; matrix products, arithmetic and copies ran while one was open for 4% of the time, Pallas kernels for 43%

commit v1 on v0

--- a/solution.py
+++ b/solution.py
@@ -214,72 +214,95 @@
             jax.ShapeDtypeStruct((head_count, tok, size), f32),
             jax.ShapeDtypeStruct((head_count, tok, size), f32),
         ],
-        compiler_params=pltpu.CompilerParams(vmem_limit_bytes=48 << 20),
+        compiler_params=pltpu.CompilerParams(vmem_limit_bytes=16 << 20),
         name="local_terms",
     )(offset, resets, queries, keys, values, log_gate, beta)
 
 
-def step_kernel(map_ref, fill_ref, state_ref, out_ref):
-    for h in range(map_ref.shape[0]):
-        out_ref[h] = dot3(map_ref[h], state_ref[h]) + fill_ref[h]
-
-
-def step(step_map, step_fill, state):
+def vmem(count):
+    return [pl.BlockSpec(memory_space=pltpu.VMEM)] * count
+
+
+def step_kernel(choices, here_ref, *refs):
+    maps, fills = refs[:choices], refs[choices:2 * choices]
+    state_ref, out_ref = refs[2 * choices:]
+    here = here_ref[0]
+    for n in range(choices):
+
+        @pl.when(here == n)
+        def _(n=n):
+            for h in range(state_ref.shape[0]):
+                out_ref[h] = dot3(maps[n][h], state_ref[h]) + fills[n][h]
+
+    @pl.when(jnp.logical_or(here < 0, here >= choices))
+    def _():
+        out_ref[...] = fills[0][...]
+
+
+def step(here, maps, fills, state):
     return pl.pallas_call(
-        step_kernel,
+        functools.partial(step_kernel, len(maps)),
+        in_specs=[pl.BlockSpec(memory_space=pltpu.SMEM)] + vmem(2 * len(maps) + 1),
+        out_specs=pl.BlockSpec(memory_space=pltpu.VMEM),
         out_shape=jax.ShapeDtypeStruct(state.shape, f32),
+        compiler_params=pltpu.CompilerParams(vmem_limit_bytes=8 << 20),
         name="state_step",
-    )(step_map, step_fill, state)
-
-
-def project_kernel(place_ref, reach_ref, own_ref, state_ref, w_ref, send_ref, keep_ref, head_ref):
-    slot = pl.program_id(0)
+    )(here, *maps, *fills, state)
+
+
+def project_kernel(choices, groups, here_ref, place_ref, reach_ref, own_ref, *refs):
+    states = refs[:choices]
+    w_ref, send_ref, keep_ref, head_ref, state_ref = refs[choices:]
     heads, _, size = reach_ref.shape
-
-    @pl.when(slot == 0)
+    here, place = here_ref[0], place_ref[0]
+    part = w_ref.shape[1] // groups
+
+    @pl.when(here == 0)
     def _():
+        for h in range(heads):
+            head_ref[:, h * size:(h + 1) * size] = own_ref[h].astype(bf16)
+
+    @pl.when(here > 0)
+    def _():
+        for n in range(choices):
+
+            @pl.when(here == n + 1)
+            def _(n=n):
+                state_ref[...] = states[n][...]
+
         for h in range(heads):
             mixed = own_ref[h] + dot3(reach_ref[h], state_ref[h])
             head_ref[:, h * size:(h + 1) * size] = mixed.astype(bf16)
 
-    share = mm(head_ref[...], w_ref[...])
-
-    @pl.when(slot < pl.num_programs(0) // 2)
-    def _():
-        send_ref[0] = share
-
-    @pl.when(slot >= pl.num_programs(0) // 2)
-    def _():
-        keep_ref[0] = share
-
-
-def project(groups, place, reach, own, state, w_out):
+    for r in range(groups):
+        start = pl.multiple_of((place ^ r) * part, part)
+        share = mm(head_ref[...], w_ref[:, pl.ds(start, part)])
+        if r % 2:
+            send_ref[r // 2] = share
+        else:
+            keep_ref[r // 2] = share
+
+
+def project(groups, here, place, reach, own, states, w_out):
     heads, tok, size = reach.shape
-    rows, width = w_out.shape
-    part = width // groups
-    mid = groups // 2
-
-    def of_slot(i, p):
-        r = jnp.where(i < mid, 2 * i + 1, 2 * (i - mid))
-        return (0, p[0] ^ r)
-
-    whole = pl.BlockSpec((heads, tok, size), lambda i, p: (0, 0, 0))
-    square = pl.BlockSpec((heads, size, size), lambda i, p: (0, 0, 0))
+    part = w_out.shape[1] // groups
+    smem = pl.BlockSpec(memory_space=pltpu.SMEM)
     return pl.pallas_call(
-        project_kernel,
-        grid_spec=pltpu.PrefetchScalarGridSpec(
-            num_scalar_prefetch=1,
-            grid=(groups,),
-            in_specs=[whole, whole, square, pl.BlockSpec((rows, part), of_slot)],
-            out_specs=[
-                pl.BlockSpec((1, tok, part), lambda i, p: (jnp.minimum(i, mid - 1), 0, 0)),
-                pl.BlockSpec((1, tok, part), lambda i, p: (jnp.maximum(i - mid, 0), 0, 0)),
-            ],
-            scratch_shapes=[pltpu.VMEM((tok, heads * size), bf16)],
-        ),
-        out_shape=[jax.ShapeDtypeStruct((mid, tok, part), f32)] * 2,
+        functools.partial(project_kernel, len(states), groups),
+        in_specs=[smem, smem] + vmem(3 + len(states)),
+        out_specs=vmem(2),
+        out_shape=[jax.ShapeDtypeStruct((groups // 2, tok, part), f32)] * 2,
+        scratch_shapes=[
+            pltpu.VMEM((tok, heads * size), bf16),
+            pltpu.VMEM((heads, size, size), f32),
+        ],
+        compiler_params=pltpu.CompilerParams(vmem_limit_bytes=16 << 20),
         name="project",
-    )(place, reach, own, state, w_out)
+    )(here, place, reach, own, *states, w_out)
+
+
+def after(small, *arrays):
+    return lax.optimization_barrier((small,) + arrays)[0]
 
 
 def swapped(x, axis, bit):
@@ -287,54 +310,84 @@
     return lax.ppermute(x, axis, [(i, i ^ bit) for i in range(size)])
 
 
-def hop(x, source):
-    return lax.ppermute(x, "seq", [(source, source + 1)])
-
-
-def chain(step_map, step_fill):
+def carry_on(devices, x, round_index, chunks):
+    pairs = [(i, i + 1) for i in range(devices - 1) if 0 <= round_index - i < chunks]
+    return lax.ppermute(x, "seq", pairs)
+
+
+def gathered(keep, received):
+    keep = keep + received
+    bit = 2
+    while keep.shape[0] > 1:
+        keep = keep[0::2] + swapped(keep[1::2], "head", bit)
+        bit *= 2
+    return keep[0]
+
+
+def shards(queries, keys, values, log_gate, beta, resets, w_out):
+    chunks, tok, packed = queries.shape
+    groups = lax.axis_size("head")
     devices = lax.axis_size("seq")
-    if devices <= 8:
-        arrived = hop(step_fill, 0)
-        total = arrived
-        for source in range(1, devices - 1):
-            arrived = hop(step(step_map, step_fill, arrived), source)
-            total = total + arrived
-        return total
-
-    def turn(_, incoming):
-        return lax.ppermute(
-            step(step_map, step_fill, incoming), "seq", [(i, i + 1) for i in range(devices - 1)]
-        )
-
-    return lax.fori_loop(0, devices - 1, turn, jnp.zeros_like(step_fill))
-
-
-def gathered(send, keep):
-    bit = 1
-    while True:
-        keep = keep + swapped(send, "head", bit)
-        if keep.shape[0] == 1:
-            return keep[0]
-        send, keep = keep[1::2], keep[0::2]
-        bit *= 2
-
-
-def shards(queries, keys, values, log_gate, beta, resets, w_out):
-    seq_count, tok, packed = queries.shape
-    groups = lax.axis_size("head")
-    offset = (lax.axis_index("seq") * tok).astype(jnp.int32).reshape(1)
+    here = lax.axis_index("seq").astype(jnp.int32).reshape(1)
+    offset = here * tok
     place = lax.axis_index("head").astype(jnp.int32).reshape(1)
-    key_rows = keys.reshape(seq_count, 2 * tok, packed)
-    value_rows = values.reshape(seq_count, 2 * tok, packed)
-    local = [
-        local_terms(s, offset, resets, queries, key_rows, value_rows, log_gate, beta)
-        for s in range(seq_count)
-    ]
-    states = [chain(local[s][0], local[s][1]) for s in range(seq_count)]
-    outs = []
-    for s in range(seq_count):
-        send, keep = project(groups, place, local[s][2], local[s][3], states[s], w_out)
-        outs.append(gathered(send, keep))
+    key_rows = keys.reshape(chunks, 2 * tok, packed)
+    value_rows = values.reshape(chunks, 2 * tok, packed)
+
+    def local(s, offset):
+        return local_terms(s, offset, resets, queries, key_rows, value_rows, log_gate, beta)
+
+    if devices > 8:
+        terms = [local(s, offset) for s in range(chunks)]
+        pairs = [(i, i + 1) for i in range(devices - 1)]
+        no_choice = jnp.zeros((1,), jnp.int32)
+
+        def turn(_, incoming):
+            return tuple(
+                lax.ppermute(
+                    step(no_choice, [terms[s][0]], [terms[s][1]], incoming[s]), "seq", pairs
+                )
+                for s in range(chunks)
+            )
+
+        zero = tuple(jnp.zeros_like(terms[s][1]) for s in range(chunks))
+        states = lax.fori_loop(0, devices - 1, turn, zero)
+        outs = []
+        for s in range(chunks):
+            one = jnp.ones((1,), jnp.int32)
+            send, keep = project(groups, one, place, terms[s][2], terms[s][3], [states[s]], w_out)
+            outs.append(gathered(keep, swapped(send, "head", 1)))
+        return jnp.stack(outs)
+
+    last_round = chunks + devices - 3
+    terms, arrived, outs = [], [], []
+    token = None
+    for r in range(last_round + devices):
+        if r < chunks:
+            terms.append(local(r, offset if token is None else after(offset, token)))
+            token = terms[r][1]
+        done = r - devices + 1
+        if r <= last_round:
+            if r == 0:
+                sent = terms[0][1]
+            else:
+                valid = [r - i for i in range(devices - 1) if 0 <= r - i < chunks]
+                first = r - valid[0]
+                sent = step(
+                    after(here - first, token),
+                    [terms[c][0] for c in valid],
+                    [terms[c][1] for c in valid],
+                    arrived[r - 1],
+                )
+                token = sent
+            arrived.append(carry_on(devices, sent, r, chunks))
+        if 0 <= done < chunks:
+            send, keep = project(
+                groups, after(here, token), place, terms[done][2], terms[done][3],
+                [arrived[done + i] for i in range(devices - 1)], w_out,
+            )
+            token = keep
+            outs.append(gathered(keep, swapped(send, "head", 1)))
     return jnp.stack(outs)
 
 

time: 129 us -> 95 us (0.74)
  Pallas kernels: 62.2 us -> 31.9 us
  waiting for transfers between devices: 22.5 us -> 34.9 us
  local copies, waits for them, and re-layouts: 15.9 us -> 10.2 us
  starting transfers between devices: 20.3 us -> 14.7 us
  other arithmetic: 6.5 us -> 1.51 us
    pallas_call x12 -> x9, Pallas kernels: 35.2 us -> 4.95 us  [the longest x4 3.17 us: project(): pl.pallas_call(functools.partial(project_kernel, len(states), groups), in...]
    ppermute x12 -> x6, waiting for transfers between devices: 2.04 us -> 13.1 us  [carry_on(): return lax.ppermute(x, 'seq', pairs)]
    unnamed x72, local copies, waits for them, and re-layouts: 12.8 us -> 7.15 us
    add x12 -> x8, other arithmetic: 5.43 us -> 0.47 us  [the longest x4 0.33 us: gathered(): keep = keep + received]
    ppermute x12 -> x6, starting transfers between devices: 15 us -> 10.6 us  [carry_on(): return lax.ppermute(x, 'seq', pairs)]
    ppermute x8, waiting for transfers between devices: 20.4 us -> 21.8 us  [swapped(): return lax.ppermute(x, axis, [(i, i ^ bit) for i in range(size)])]
  transfers between devices with their start and end apart: 20 -> 14, of which waited for: 7 -> 9; matrix products, arithmetic and copies ran while one was open for 4% -> 1% of each run, Pallas kernels for 43% -> 25%
where the time goes in v1:
time: 95 us; the launch traced here: 93.8 us
  waiting for transfers between devices  34.9 us (37%)
  Pallas kernels  31.9 us (34%)
  starting transfers between devices  14.7 us (15%)
  local copies, waits for them, and re-layouts  10.2 us (11%)
  other arithmetic  1.51 us (2%)
    pallas_call x4, Pallas kernels, local_terms(): pl.pallas_call(functools.partial(local_kernel, head_count, seq), grid_spe...  26.9 us
    ppermute x8, waiting for transfers between devices, swapped(): return lax.ppermute(x, axis, [(i, i ^ bit) for i in range(size)])  21.8 us
    ppermute x6, waiting for transfers between devices, carry_on(): return lax.ppermute(x, 'seq', pairs)  13.1 us
    ppermute x6, starting transfers between devices, carry_on(): return lax.ppermute(x, 'seq', pairs)  10.6 us
    unnamed x72, local copies, waits for them, and re-layouts  7.15 us
    ppermute x8, starting transfers between devices, swapped(): return lax.ppermute(x, axis, [(i, i ^ bit) for i in range(size)])  4.09 us
    pallas_call x4, Pallas kernels, project(): pl.pallas_call(functools.partial(project_kernel, len(states), groups), in...  3.17 us
  transfers between devices with their start and end apart: 14, of which 9 were waited for; matrix products, arithmetic and copies ran while one was open for 1% of the time, Pallas kernels for 25%

profile of v1, /device:TPU:22, one launch (start us, length us, event | category | flops | bytes accessed | tf_op | source)
XLA Modules:
  0.0 93.8 jit_solution(7921315869857737590)
XLA Ops:
  0.0 1.5 %reshape.13.k_ref = bf16[4,256,512]{2,1,0:T(8,128)(2,1)S(1)} reshape(bf16[4,128,2,512]{3,2,1,0:T(2,128)(2,1)} %param.8) | data formatting | bytes 2097152 | tf_op jit(solution)/shard_map/reshape | solution.py:334
  1.6 1.5 %reshape.14.v_ref = bf16[4,256,512]{2,1,0:T(8,128)(2,1)S(1)} reshape(bf16[4,128,2,512]{3,2,1,0:T(2,128)(2,1)} %param.9) | data formatting | bytes 2097152 | tf_op jit(solution)/shard_map/reshape | solution.py:335
  3.1 6.7 %local_terms.4 = (f32[4,128,128]{2,1,0:T(8,128)S(1)}, f32[4,128,128]{2,1,0:T(8,128)S(1)}, f32[4,128,128]{2,1,0:T(8,128)S(1)}, f32[4,128,128]{2,1,0:T(8,128)S(1)}) custom-call(s32[1]{0:T(128)S(6)} %mul.3.offset_ref, s32[4,3]{1,0:T(4,128)S(1)} %copy-done.35, bf16[4,128,512]{2,1,0:T(8,128)(2,1)S(1)} %copy-done.3, bf16[4,256,512]{2,1,0:T(8,128)(2,1)S(1)} %reshape.13.k_ref, ...), custom_call_target="tpu_custom_call" | custom-call | tf_op jit(solution)/shard_map/local_terms/pallas_call | solution.py:197
  9.8 0.7 copy-done.30
  10.5 0.7 copy-done.32
  11.2 0.7 collective-permute-start
  11.9 6.7 %local_terms.5 = (f32[4,128,128]{2,1,0:T(8,128)S(1)}, f32[4,128,128]{2,1,0:T(8,128)S(1)}, f32[4,128,128]{2,1,0:T(8,128)S(1)}, f32[4,128,128]{2,1,0:T(8,128)S(1)}) custom-call(s32[1]{0:T(128)S(6)} %mul.3.offset_ref, s32[4,3]{1,0:T(4,128)S(1)} %copy-done.35, bf16[4,128,512]{2,1,0:T(8,128)(2,1)S(1)} %copy-done.3, bf16[4,256,512]{2,1,0:T(8,128)(2,1)S(1)} %reshape.13.k_ref, ...), custom_call_target="tpu_custom_call" | custom-call | tf_op jit(solution)/shard_map/local_terms/pallas_call | solution.py:197
  18.6 0.7 copy-done.28
  19.4 0.7 copy-done.26
  20.0 1.6 %collective-permute-start.1 = (f32[4,128,128]{2,1,0:T(8,128)S(1)}, f32[4,128,128]{2,1,0:T(8,128)S(1)}, u32[]{:S(2)}, u32[]{:S(2)}) collective-permute-start(f32[4,128,128]{2,1,0:T(8,128)S(1)} %state_step.5), channel_id=1, source_target_pairs={{0,4},{4,8},{1,5},{5,9},{2,6},{6,10},{3,7},{7,11},{16,20},{20,24},... | collective-permute-start | bytes 786440 | tf_op jit(solution)/shard_map/ppermute | solution.py:315
  21.6 6.7 %local_terms.6 = (f32[4,128,128]{2,1,0:T(8,128)S(1)}, f32[4,128,128]{2,1,0:T(8,128)S(1)}, f32[4,128,128]{2,1,0:T(8,128)S(1)}, f32[4,128,128]{2,1,0:T(8,128)S(1)}) custom-call(s32[1]{0:T(128)S(6)} %mul.3.offset_ref, s32[4,3]{1,0:T(4,128)S(1)} %copy-done.35, bf16[4,128,512]{2,1,0:T(8,128)(2,1)S(1)} %copy-done.3, bf16[4,256,512]{2,1,0:T(8,128)(2,1)S(1)} %reshape.13.k_ref, ...), custom_call_target="tpu_custom_call" | custom-call | tf_op jit(solution)/shard_map/local_terms/pallas_call | solution.py:197
  28.4 0.7 copy-done.24
  29.1 1.0 %collective-permute-done.1.refs_6_.refs_1_.refs_0_ = f32[4,128,128]{2,1,0:T(8,128)S(1)} collective-permute-done((f32[4,128,128]{2,1,0:T(8,128)S(1)}, f32[4,128,128]{2,1,0:T(8,128)S(1)}, u32[]{:S(2)}, u32[]{:S(2)}) %collective-permute-start.1) | collective-permute-done | bytes 262176 | tf_op jit(solution)/shard_map/ppermute | solution.py:315
  30.1 0.3 state_step.6
  30.4 0.7 copy-done.5
  31.1 2.4 %collective-permute-start.2 = (f32[4,128,128]{2,1,0:T(8,128)S(1)}, f32[4,128,128]{2,1,0:T(8,128)S(1)}, u32[]{:S(2)}, u32[]{:S(2)}) collective-permute-start(f32[4,128,128]{2,1,0:T(8,128)S(1)} %state_step.6), channel_id=1, source_target_pairs={{0,4},{4,8},{8,12},{1,5},{5,9},{9,13},{2,6},{6,10},{10,14},{3,7},{... | collective-permute-start | bytes 786440 | tf_op jit(solution)/shard_map/ppermute | solution.py:315
  33.5 6.7 %local_terms.7 = (f32[4,128,128]{2,1,0:T(8,128)S(1)}, f32[4,128,128]{2,1,0:T(8,128)S(1)}, f32[4,128,128]{2,1,0:T(8,128)S(1)}, f32[4,128,128]{2,1,0:T(8,128)S(1)}) custom-call(s32[1]{0:T(128)S(6)} %mul.3.offset_ref, s32[4,3]{1,0:T(4,128)S(1)} %copy-done.35, bf16[4,128,512]{2,1,0:T(8,128)(2,1)S(1)} %copy-done.4, bf16[4,256,512]{2,1,0:T(8,128)(2,1)S(1)} %reshape.13.k_ref, ...), custom_call_target="tpu_custom_call" | custom-call | tf_op jit(solution)/shard_map/local_terms/pallas_call | solution.py:197
  40.3 0.9 collective-permute-done.2.refs_6_.refs_2_.refs_1_.refs_0_
  41.2 1.0 %state_step.7 = f32[4,128,128]{2,1,0:T(8,128)} custom-call(s32[1]{0:T(128)} %bitcast.here_ref, f32[4,128,128]{2,1,0:T(8,128)S(1)} %get-tuple-element.54.refs_0_, f32[4,128,128]{2,1,0:T(8,128)S(1)} %get-tuple-element.50.refs_0_.refs_1_, f32[4,128,128]{2,1,0:T(8,128)S(1)} %get-tuple-element.45.refs_0_.refs_1_.refs_2_, ...), custom_call_target="tpu_custom_call" | custom-call | tf_op jit(solution)/shard_map/state_step/pallas_call | solution.py:243
  42.2 2.1 %collective-permute-start.5 = (f32[4,128,128]{2,1,0:T(8,128)}, f32[4,128,128]{2,1,0:T(8,128)S(1)}, u32[]{:S(2)}, u32[]{:S(2)}) collective-permute-start(f32[4,128,128]{2,1,0:T(8,128)} %state_step.7), channel_id=1, source_target_pairs={{0,4},{4,8},{8,12},{1,5},{5,9},{9,13},{2,6},{6,10},{10,14},{3,7},{... | collective-permute-start | bytes 786440 | tf_op jit(solution)/shard_map/ppermute | solution.py:315
  44.4 1.0 %copy-done.16 = f32[4,128,128]{2,1,0:T(8,128)S(1)} copy-done((f32[4,128,128]{2,1,0:T(8,128)S(1)}, f32[4,128,128]{2,1,0:T(8,128)}, u32[]{:S(2)}) %copy-start.16) | copy-done | bytes 262168
  45.4 0.9 %copy-done.31 = f32[4,128,128]{2,1,0:T(8,128)S(1)} copy-done((f32[4,128,128]{2,1,0:T(8,128)S(1)}, f32[4,128,128]{2,1,0:T(8,128)}, u32[]{:S(2)}) %copy-start.31) | copy-done | bytes 262168
  46.3 0.9 %copy-done.33 = f32[4,128,128]{2,1,0:T(8,128)S(1)} copy-done((f32[4,128,128]{2,1,0:T(8,128)S(1)}, f32[4,128,128]{2,1,0:T(8,128)}, u32[]{:S(2)}) %copy-start.33) | copy-done | bytes 262168
  47.3 0.9 %project.4 = (f32[2,128,512]{2,1,0:T(8,128)S(1)}, f32[2,128,512]{2,1,0:T(8,128)S(1)}) custom-call(s32[1]{0:T(128)} %bitcast.here_ref, s32[1]{0:T(128)} %bitcast.1.place_ref, f32[4,128,128]{2,1,0:T(8,128)S(1)} %copy-done.31, f32[4,128,128]{2,1,0:T(8,128)S(1)} %copy-done.33, f32[4,128,128]{2,1,0:T(8,128)S(1)} %copy-done.16, f32[4,128,128]{2,1,0:T(8,128)S(1)} %copy-done.6, ...), custom_call_target="tpu_custom_call" | custom-call | tf_op jit(solution)/shard_map/project/pallas_call | solution.py:290
  48.2 3.4 %collective-permute-done.5.refs_4_.refs_2_.refs_1_.refs_0_ = f32[4,128,128]{2,1,0:T(8,128)S(1)} collective-permute-done((f32[4,128,128]{2,1,0:T(8,128)}, f32[4,128,128]{2,1,0:T(8,128)S(1)}, u32[]{:S(2)}, u32[]{:S(2)}) %collective-permute-start.5) | collective-permute-done | bytes 262176 | tf_op jit(solution)/shard_map/ppermute | solution.py:315
  51.6 0.3 state_step.8
  51.9 2.0 %collective-permute-start.8 = (f32[4,128,128]{2,1,0:T(8,128)S(1)}, f32[4,128,128]{2,1,0:T(8,128)S(1)}, u32[]{:S(2)}, u32[]{:S(2)}) collective-permute-start(f32[4,128,128]{2,1,0:T(8,128)S(1)} %state_step.8), channel_id=1, source_target_pairs={{4,8},{8,12},{5,9},{9,13},{6,10},{10,14},{7,11},{11,15},{20,24},{2... | collective-permute-start | bytes 786440 | tf_op jit(solution)/shard_map/ppermute | solution.py:315
  54.0 0.8 project.5
  54.8 5.4 %collective-permute-done.8.refs_2_.refs_1_ = f32[4,128,128]{2,1,0:T(8,128)S(1)} collective-permute-done((f32[4,128,128]{2,1,0:T(8,128)S(1)}, f32[4,128,128]{2,1,0:T(8,128)S(1)}, u32[]{:S(2)}, u32[]{:S(2)}) %collective-permute-start.8) | collective-permute-done | bytes 262176 | tf_op jit(solution)/shard_map/ppermute | solution.py:315
  60.2 0.3 state_step.9
  60.4 1.8 %collective-permute-start.11 = (f32[4,128,128]{2,1,0:T(8,128)S(1)}, f32[4,128,128]{2,1,0:T(8,128)S(1)}, u32[]{:S(2)}, u32[]{:S(2)}) collective-permute-start(f32[4,128,128]{2,1,0:T(8,128)S(1)} %state_step.9), channel_id=1, source_target_pairs={{8,12},{9,13},{10,14},{11,15},{24,28},{25,29},{26,30},{27,31}} | collective-permute-start | bytes 786440 | tf_op jit(solution)/shard_map/ppermute | solution.py:315
  62.4 0.7 project.6
  63.1 0.5 collective-permute-start.9
  63.7 2.5 %collective-permute-done.11.refs_2_ = f32[4,128,128]{2,1,0:T(8,128)S(1)} collective-permute-done((f32[4,128,128]{2,1,0:T(8,128)S(1)}, f32[4,128,128]{2,1,0:T(8,128)S(1)}, u32[]{:S(2)}, u32[]{:S(2)}) %collective-permute-start.11) | collective-permute-done | bytes 262176 | tf_op jit(solution)/shard_map/ppermute | solution.py:315
  66.2 0.7 project.7
  67.0 0.1 add.26
  67.1 0.6 collective-permute-start.4
  67.7 0.1 add.28
  67.8 1.6 %collective-permute-start.7 = (f32[1,128,512]{2,1,0:T(8,128)S(1)}, f32[1,128,512]{2,1,0:T(8,128)S(1)}, u32[]{:S(2)}, u32[]{:S(2)}) collective-permute-start(f32[1,128,512]{2,1,0:T(8,128)S(1)} %slice.43), channel_id=1, source_target_pairs={{0,2},{1,3},{2,0},{3,1},{4,6},{5,7},{6,4},{7,5},{8,10},{9,11},{10,... | collective-permute-start | bytes 786440 | tf_op jit(solution)/shard_map/ppermute | solution.py:310
  69.4 0.1 add.30
  69.5 0.6 collective-permute-start.10
  70.1 6.2 %collective-permute-done.4 = f32[1,128,512]{2,1,0:T(8,128)S(1)} collective-permute-done((f32[1,128,512]{2,1,0:T(8,128)S(1)}, f32[1,128,512]{2,1,0:T(8,128)S(1)}, u32[]{:S(2)}, u32[]{:S(2)}) %collective-permute-start.4) | collective-permute-done | bytes 262176 | tf_op jit(solution)/shard_map/ppermute | solution.py:310
  76.3 0.1 add.32
  76.4 0.6 collective-permute-start.13
  77.0 4.9 %collective-permute-done.7 = f32[1,128,512]{2,1,0:T(8,128)S(1)} collective-permute-done((f32[1,128,512]{2,1,0:T(8,128)S(1)}, f32[1,128,512]{2,1,0:T(8,128)S(1)}, u32[]{:S(2)}, u32[]{:S(2)}) %collective-permute-start.7) | collective-permute-done | bytes 262176 | tf_op jit(solution)/shard_map/ppermute | solution.py:310
  81.9 5.6 %collective-permute-done.10 = f32[1,128,512]{2,1,0:T(8,128)S(1)} collective-permute-done((f32[1,128,512]{2,1,0:T(8,128)S(1)}, f32[1,128,512]{2,1,0:T(8,128)S(1)}, u32[]{:S(2)}, u32[]{:S(2)}) %collective-permute-start.10) | collective-permute-done | bytes 262176 | tf_op jit(solution)/shard_map/ppermute | solution.py:310
  87.5 5.2 %collective-permute-done.13 = f32[1,128,512]{2,1,0:T(8,128)S(1)} collective-permute-done((f32[1,128,512]{2,1,0:T(8,128)S(1)}, f32[1,128,512]{2,1,0:T(8,128)S(1)}, u32[]{:S(2)}, u32[]{:S(2)}) %collective-permute-start.13) | collective-permute-done | bytes 262176 | tf_op jit(solution)/shard_map/ppermute | solution.py:310
  92.7 1.0 %pad_maximum_fusion = f32[4,128,512]{2,1,0:T(8,128)} fusion(f32[1,128,512]{2,1,0:T(8,128)S(1)} %slice_add_fusion, f32[1,128,512]{2,1,0:T(8,128)S(1)} %slice_add_fusion.1, f32[1,128,512]{2,1,0:T(8,128)S(1)} %slice_add_fusion.2, f32[1,128,512]{2,1,0:T(8,128)S(1)} %slice_add_fusion.3), kind=kLoop, calls=%fused_computation | loop fusion | flops 786432 | bytes 2097152 | tf_op jit(solution)/shard_map/stack | solution.py:391
  (80 shorter events, 0.6 us)
Async XLA Ops:
  0.0 3.0 %copy-start.3 = (bf16[4,128,512]{2,1,0:T(8,128)(2,1)S(1)}, bf16[4,128,512]{2,1,0:T(8,128)(2,1)}, u32[]{:S(2)}) copy-start(bf16[4,128,512]{2,1,0:T(8,128)(2,1)} %q_ref.7) | copy-start | bytes 1572868
  0.0 3.1 %copy-start.17 = (f32[4,2,4,128]{3,2,1,0:T(4,128)S(1)}, f32[4,2,4,128]{3,2,1,0:T(4,128)}, u32[]{:S(2)}) copy-start(f32[4,2,4,128]{3,2,1,0:T(4,128)} %beta_ref.7) | copy-start | bytes 49156
  0.0 3.1 %copy-start.34 = (f32[4,4,128]{2,1,0:T(4,128)S(1)}, f32[4,4,128]{2,1,0:T(4,128)}, u32[]{:S(2)}) copy-start(f32[4,4,128]{2,1,0:T(4,128)} %gate_ref.7) | copy-start | bytes 24580
  0.0 3.1 %copy-start.35 = (s32[4,3]{1,0:T(4,128)S(1)}, s32[4,3]{1,0:T(4,128)}, u32[]{:S(2)}) copy-start(s32[4,3]{1,0:T(4,128)} %resets_ref.7) | copy-start | bytes 148
  3.0 18.6 %copy-start.1 = (bf16[4,256,512]{2,1,0:T(8,128)(2,1)}, bf16[4,256,512]{2,1,0:T(8,128)(2,1)S(1)}, u32[]{:S(2)}) copy-start(bf16[4,256,512]{2,1,0:T(8,128)(2,1)S(1)} %reshape.14.v_ref) | copy-start | bytes 3145732
  9.8 0.7 copy-start.30
  10.5 0.7 copy-start.32
  11.2 8.1 %collective-permute-start = (f32[4,128,128]{2,1,0:T(8,128)S(1)}, f32[4,128,128]{2,1,0:T(8,128)S(1)}, u32[]{:S(2)}, u32[]{:S(2)}) collective-permute-start(f32[4,128,128]{2,1,0:T(8,128)S(1)} %get-tuple-element.41.refs_3_.refs_5_), channel_id=1, source_target_pairs={{0,4},{1,5},{2,6},{3,7},{16,20},{17,21},{18,22},{19,23}} | collective-permute-start | bytes 786440 | tf_op jit(solution)/shard_map/ppermute | solution.py:315
  19.3 9.0 %copy-start.15 = (f32[4,128,128]{2,1,0:T(8,128)}, f32[4,128,128]{2,1,0:T(8,128)S(1)}, u32[]{:S(2)}) copy-start(f32[4,128,128]{2,1,0:T(8,128)S(1)} %collective-permute-done.refs_4_.refs_0_) | copy-start | bytes 786436
  20.0 13.5 %copy-start.4 = (bf16[4,128,512]{2,1,0:T(8,128)(2,1)S(1)}, bf16[4,128,512]{2,1,0:T(8,128)(2,1)}, u32[]{:S(2)}) copy-start(bf16[4,128,512]{2,1,0:T(8,128)(2,1)} %q_ref.7) | copy-start | bytes 1572868
  20.0 10.1 %collective-permute-start.1 = (f32[4,128,128]{2,1,0:T(8,128)S(1)}, f32[4,128,128]{2,1,0:T(8,128)S(1)}, u32[]{:S(2)}, u32[]{:S(2)}) collective-permute-start(f32[4,128,128]{2,1,0:T(8,128)S(1)} %state_step.5), channel_id=1, source_target_pairs={{0,4},{4,8},{1,5},{5,9},{2,6},{6,10},{3,7},{7,11},{16,20},{20,24},... | collective-permute-start | bytes 786440 | tf_op jit(solution)/shard_map/ppermute | solution.py:315
  28.4 0.7 copy-start.24
  29.1 1.3 %copy-start.22 = (f32[4,128,128]{2,1,0:T(8,128)}, f32[4,128,128]{2,1,0:T(8,128)S(1)}, u32[]{:S(2)}) copy-start(f32[4,128,128]{2,1,0:T(8,128)S(1)} %get-tuple-element.68.reach_ref) | copy-start | bytes 786436
  29.1 12.1 %copy-start.7 = (f32[4,128,128]{2,1,0:T(8,128)}, f32[4,128,128]{2,1,0:T(8,128)S(1)}, u32[]{:S(2)}) copy-start(f32[4,128,128]{2,1,0:T(8,128)S(1)} %get-tuple-element.50.refs_0_.refs_1_) | copy-start | bytes 786436
  29.1 12.1 %copy-start.9 = (f32[4,128,128]{2,1,0:T(8,128)}, f32[4,128,128]{2,1,0:T(8,128)S(1)}, u32[]{:S(2)}) copy-start(f32[4,128,128]{2,1,0:T(8,128)S(1)} %get-tuple-element.48.refs_3_.refs_4_) | copy-start | bytes 786436
  29.1 4.4 %copy-start.2 = (bf16[4,256,512]{2,1,0:T(8,128)(2,1)S(1)}, bf16[4,256,512]{2,1,0:T(8,128)(2,1)}, u32[]{:S(2)}) copy-start(bf16[4,256,512]{2,1,0:T(8,128)(2,1)} %copy-done.1) | copy-start | bytes 3145732
  30.4 0.7 copy-start.5
  31.1 13.3 %copy-start = (bf16[512,2048]{1,0:T(8,128)(2,1)S(1)}, bf16[512,2048]{1,0:T(8,128)(2,1)}, u32[]{:S(2)}) copy-start(bf16[512,2048]{1,0:T(8,128)(2,1)} %refs_3_.7) | copy-start | bytes 6291460
  31.1 10.1 %collective-permute-start.2 = (f32[4,128,128]{2,1,0:T(8,128)S(1)}, f32[4,128,128]{2,1,0:T(8,128)S(1)}, u32[]{:S(2)}, u32[]{:S(2)}) collective-permute-start(f32[4,128,128]{2,1,0:T(8,128)S(1)} %state_step.6), channel_id=1, source_target_pairs={{0,4},{4,8},{8,12},{1,5},{5,9},{9,13},{2,6},{6,10},{10,14},{3,7},{... | collective-permute-start | bytes 786440 | tf_op jit(solution)/shard_map/ppermute | solution.py:315
  40.3 1.9 %copy-start.11 = (f32[4,128,128]{2,1,0:T(8,128)}, f32[4,128,128]{2,1,0:T(8,128)S(1)}, u32[]{:S(2)}) copy-start(f32[4,128,128]{2,1,0:T(8,128)S(1)} %get-tuple-element.54.refs_0_) | copy-start | bytes 786436
  40.3 1.9 %copy-start.13 = (f32[4,128,128]{2,1,0:T(8,128)}, f32[4,128,128]{2,1,0:T(8,128)S(1)}, u32[]{:S(2)}) copy-start(f32[4,128,128]{2,1,0:T(8,128)S(1)} %get-tuple-element.52.refs_3_.refs_2_.refs_1_) | copy-start | bytes 786436
  40.3 1.9 %copy-start.18 = (f32[4,128,128]{2,1,0:T(8,128)}, f32[4,128,128]{2,1,0:T(8,128)S(1)}, u32[]{:S(2)}) copy-start(f32[4,128,128]{2,1,0:T(8,128)S(1)} %get-tuple-element.73.reach_ref) | copy-start | bytes 786436
  40.3 1.9 %copy-start.20 = (f32[4,128,128]{2,1,0:T(8,128)}, f32[4,128,128]{2,1,0:T(8,128)S(1)}, u32[]{:S(2)}) copy-start(f32[4,128,128]{2,1,0:T(8,128)S(1)} %get-tuple-element.74.own_ref) | copy-start | bytes 786436
  40.3 4.1 %copy-start.6 = (f32[4,128,128]{2,1,0:T(8,128)S(1)}, f32[4,128,128]{2,1,0:T(8,128)}, u32[]{:S(2)}) copy-start(f32[4,128,128]{2,1,0:T(8,128)} %copy-done.5) | copy-start | bytes 786436
  42.2 9.4 %copy-start.8 = (f32[4,128,128]{2,1,0:T(8,128)S(1)}, f32[4,128,128]{2,1,0:T(8,128)}, u32[]{:S(2)}) copy-start(f32[4,128,128]{2,1,0:T(8,128)} %copy-done.7) | copy-start | bytes 786436
  42.2 9.4 %copy-start.10 = (f32[4,128,128]{2,1,0:T(8,128)S(1)}, f32[4,128,128]{2,1,0:T(8,128)}, u32[]{:S(2)}) copy-start(f32[4,128,128]{2,1,0:T(8,128)} %copy-done.9) | copy-start | bytes 786436
  42.2 9.4 %collective-permute-start.5 = (f32[4,128,128]{2,1,0:T(8,128)}, f32[4,128,128]{2,1,0:T(8,128)S(1)}, u32[]{:S(2)}, u32[]{:S(2)}) collective-permute-start(f32[4,128,128]{2,1,0:T(8,128)} %state_step.7), channel_id=1, source_target_pairs={{0,4},{4,8},{8,12},{1,5},{5,9},{9,13},{2,6},{6,10},{10,14},{3,7},{... | collective-permute-start | bytes 786440 | tf_op jit(solution)/shard_map/ppermute | solution.py:315
  44.3 7.3 %copy-start.12 = (f32[4,128,128]{2,1,0:T(8,128)S(1)}, f32[4,128,128]{2,1,0:T(8,128)}, u32[]{:S(2)}) copy-start(f32[4,128,128]{2,1,0:T(8,128)} %copy-done.11) | copy-start | bytes 786436
  44.3 7.3 %copy-start.14 = (f32[4,128,128]{2,1,0:T(8,128)S(1)}, f32[4,128,128]{2,1,0:T(8,128)}, u32[]{:S(2)}) copy-start(f32[4,128,128]{2,1,0:T(8,128)} %copy-done.13) | copy-start | bytes 786436
  44.4 1.0 %copy-start.16 = (f32[4,128,128]{2,1,0:T(8,128)S(1)}, f32[4,128,128]{2,1,0:T(8,128)}, u32[]{:S(2)}) copy-start(f32[4,128,128]{2,1,0:T(8,128)} %copy-done.15) | copy-start | bytes 786436
  45.4 0.9 %copy-start.31 = (f32[4,128,128]{2,1,0:T(8,128)S(1)}, f32[4,128,128]{2,1,0:T(8,128)}, u32[]{:S(2)}) copy-start(f32[4,128,128]{2,1,0:T(8,128)} %copy-done.30) | copy-start | bytes 786436
  46.3 0.9 %copy-start.33 = (f32[4,128,128]{2,1,0:T(8,128)S(1)}, f32[4,128,128]{2,1,0:T(8,128)}, u32[]{:S(2)}) copy-start(f32[4,128,128]{2,1,0:T(8,128)} %copy-done.32) | copy-start | bytes 786436
  47.3 6.7 %copy-start.27 = (f32[4,128,128]{2,1,0:T(8,128)S(1)}, f32[4,128,128]{2,1,0:T(8,128)}, u32[]{:S(2)}) copy-start(f32[4,128,128]{2,1,0:T(8,128)} %copy-done.26) | copy-start | bytes 786436
  47.3 6.7 %copy-start.29 = (f32[4,128,128]{2,1,0:T(8,128)S(1)}, f32[4,128,128]{2,1,0:T(8,128)}, u32[]{:S(2)}) copy-start(f32[4,128,128]{2,1,0:T(8,128)} %copy-done.28) | copy-start | bytes 786436
  51.9 8.3 %collective-permute-start.8 = (f32[4,128,128]{2,1,0:T(8,128)S(1)}, f32[4,128,128]{2,1,0:T(8,128)S(1)}, u32[]{:S(2)}, u32[]{:S(2)}) collective-permute-start(f32[4,128,128]{2,1,0:T(8,128)S(1)} %state_step.8), channel_id=1, source_target_pairs={{4,8},{8,12},{5,9},{9,13},{6,10},{10,14},{7,11},{11,15},{20,24},{2... | collective-permute-start | bytes 786440 | tf_op jit(solution)/shard_map/ppermute | solution.py:315
  53.9 13.1 %collective-permute-start.3 = (f32[2,128,512]{2,1,0:T(8,128)S(1)}, f32[2,128,512]{2,1,0:T(8,128)S(1)}, u32[]{:S(2)}, u32[]{:S(2)}) collective-permute-start(f32[2,128,512]{2,1,0:T(8,128)S(1)} %get-tuple-element.59), channel_id=1, source_target_pairs={{0,1},{1,0},{2,3},{3,2},{4,5},{5,4},{6,7},{7,6},{8,9},{9,8},{10,11... | collective-permute-start | bytes 1572872 | tf_op jit(solution)/shard_map/ppermute | solution.py:310
  54.0 8.4 %copy-start.23 = (f32[4,128,128]{2,1,0:T(8,128)S(1)}, f32[4,128,128]{2,1,0:T(8,128)}, u32[]{:S(2)}) copy-start(f32[4,128,128]{2,1,0:T(8,128)} %copy-done.22) | copy-start | bytes 786436
  54.0 8.4 %copy-start.25 = (f32[4,128,128]{2,1,0:T(8,128)S(1)}, f32[4,128,128]{2,1,0:T(8,128)}, u32[]{:S(2)}) copy-start(f32[4,128,128]{2,1,0:T(8,128)} %copy-done.24) | copy-start | bytes 786436
  54.7 11.4 %copy-start.19 = (f32[4,128,128]{2,1,0:T(8,128)S(1)}, f32[4,128,128]{2,1,0:T(8,128)}, u32[]{:S(2)}) copy-start(f32[4,128,128]{2,1,0:T(8,128)} %copy-done.18) | copy-start | bytes 786436
  54.8 11.4 %copy-start.21 = (f32[4,128,128]{2,1,0:T(8,128)S(1)}, f32[4,128,128]{2,1,0:T(8,128)}, u32[]{:S(2)}) copy-start(f32[4,128,128]{2,1,0:T(8,128)} %copy-done.20) | copy-start | bytes 786436
  60.4 5.7 %collective-permute-start.11 = (f32[4,128,128]{2,1,0:T(8,128)S(1)}, f32[4,128,128]{2,1,0:T(8,128)S(1)}, u32[]{:S(2)}, u32[]{:S(2)}) collective-permute-start(f32[4,128,128]{2,1,0:T(8,128)S(1)} %state_step.9), channel_id=1, source_target_pairs={{8,12},{9,13},{10,14},{11,15},{24,28},{25,29},{26,30},{27,31}} | collective-permute-start | bytes 786440 | tf_op jit(solution)/shard_map/ppermute | solution.py:315
  62.3 5.4 %collective-permute-start.6 = (f32[2,128,512]{2,1,0:T(8,128)S(1)}, f32[2,128,512]{2,1,0:T(8,128)S(1)}, u32[]{:S(2)}, u32[]{:S(2)}) collective-permute-start(f32[2,128,512]{2,1,0:T(8,128)S(1)} %get-tuple-element.65), channel_id=1, source_target_pairs={{0,1},{1,0},{2,3},{3,2},{4,5},{5,4},{6,7},{7,6},{8,9},{9,8},{10,11... | collective-permute-start | bytes 1572872 | tf_op jit(solution)/shard_map/ppermute | solution.py:310
  63.1 6.2 %collective-permute-start.9 = (f32[2,128,512]{2,1,0:T(8,128)S(1)}, f32[2,128,512]{2,1,0:T(8,128)S(1)}, u32[]{:S(2)}, u32[]{:S(2)}) collective-permute-start(f32[2,128,512]{2,1,0:T(8,128)S(1)} %get-tuple-element.71), channel_id=1, source_target_pairs={{0,1},{1,0},{2,3},{3,2},{4,5},{5,4},{6,7},{7,6},{8,9},{9,8},{10,11... | collective-permute-start | bytes 1572872 | tf_op jit(solution)/shard_map/ppermute | solution.py:310
  66.9 9.4 %collective-permute-start.12 = (f32[2,128,512]{2,1,0:T(8,128)S(1)}, f32[2,128,512]{2,1,0:T(8,128)S(1)}, u32[]{:S(2)}, u32[]{:S(2)}) collective-permute-start(f32[2,128,512]{2,1,0:T(8,128)S(1)} %get-tuple-element.76), channel_id=1, source_target_pairs={{0,1},{1,0},{2,3},{3,2},{4,5},{5,4},{6,7},{7,6},{8,9},{9,8},{10,11... | collective-permute-start | bytes 1572872 | tf_op jit(solution)/shard_map/ppermute | solution.py:310
  67.1 9.2 %collective-permute-start.4 = (f32[1,128,512]{2,1,0:T(8,128)S(1)}, f32[1,128,512]{2,1,0:T(8,128)S(1)}, u32[]{:S(2)}, u32[]{:S(2)}) collective-permute-start(f32[1,128,512]{2,1,0:T(8,128)S(1)} %slice.41), channel_id=1, source_target_pairs={{0,2},{1,3},{2,0},{3,1},{4,6},{5,7},{6,4},{7,5},{8,10},{9,11},{10,... | collective-permute-start | bytes 786440 | tf_op jit(solution)/shard_map/ppermute | solution.py:310
  67.8 14.1 %collective-permute-start.7 = (f32[1,128,512]{2,1,0:T(8,128)S(1)}, f32[1,128,512]{2,1,0:T(8,128)S(1)}, u32[]{:S(2)}, u32[]{:S(2)}) collective-permute-start(f32[1,128,512]{2,1,0:T(8,128)S(1)} %slice.43), channel_id=1, source_target_pairs={{0,2},{1,3},{2,0},{3,1},{4,6},{5,7},{6,4},{7,5},{8,10},{9,11},{10,... | collective-permute-start | bytes 786440 | tf_op jit(solution)/shard_map/ppermute | solution.py:310
  69.5 18.0 %collective-permute-start.10 = (f32[1,128,512]{2,1,0:T(8,128)S(1)}, f32[1,128,512]{2,1,0:T(8,128)S(1)}, u32[]{:S(2)}, u32[]{:S(2)}) collective-permute-start(f32[1,128,512]{2,1,0:T(8,128)S(1)} %slice.45), channel_id=1, source_target_pairs={{0,2},{1,3},{2,0},{3,1},{4,6},{5,7},{6,4},{7,5},{8,10},{9,11},{10,... | collective-permute-start | bytes 786440 | tf_op jit(solution)/shard_map/ppermute | solution.py:310
  76.4 16.3 %collective-permute-start.13 = (f32[1,128,512]{2,1,0:T(8,128)S(1)}, f32[1,128,512]{2,1,0:T(8,128)S(1)}, u32[]{:S(2)}, u32[]{:S(2)}) collective-permute-start(f32[1,128,512]{2,1,0:T(8,128)S(1)} %slice.47), channel_id=1, source_target_pairs={{0,2},{1,3},{2,0},{3,1},{4,6},{5,7},{6,4},{7,5},{8,10},{9,11},{10,... | collective-permute-start | bytes 786440 | tf_op jit(solution)/shard_map/ppermute | solution.py:310
  (2 other events, 1.4 us)

commit v2 on v1

v2 whole, which is shorter than its diff:
```python
import functools

import jax
import jax.numpy as jnp
from jax import lax
from jax.experimental import pallas as pl
from jax.experimental.pallas import tpu as pltpu
from jax.sharding import PartitionSpec as P

epsilon = 1e-06
small_cost = pl.CostEstimate(flops=1 << 20, transcendentals=0, bytes_accessed=1 << 10)
f32 = jnp.float32
bf16 = jnp.bfloat16


def mm(a, b):
    return lax.dot_general(a, b, (((1,), (0,)), ((), ())), preferred_element_type=f32)


def mm_nt(a, b):
    return lax.dot_general(a, b, (((1,), (1,)), ((), ())), preferred_element_type=f32)


def mm_tn(a, b):
    return lax.dot_general(a, b, (((0,), (0,)), ((), ())), preferred_element_type=f32)


def split(x):
    high = x.astype(bf16)
    return high, (x - high.astype(f32)).astype(bf16)


def split3(x):
    high, rest = x.astype(bf16), None
    rest = x - high.astype(f32)
    middle = rest.astype(bf16)
    return high, middle, (rest - middle.astype(f32)).astype(bf16)


def dot3(a, b):
    a_high, a_low = split(a)
    b_high, b_low = split(b)
    return mm(a_high, b_high) + (mm(a_low, b_high) + mm(a_high, b_low))


def iota(shape, axis):
    return lax.broadcasted_iota(jnp.int32, shape, axis)


def local_kernel(head_count, seq, offset_ref, resets_ref, q_ref, k_ref, v_ref, gate_ref, beta_ref,
                 *refs):
    transit_ref, filled_ref, reach_ref, own_ref = refs[-4:]
    tok = q_ref.shape[1]
    size = q_ref.shape[2] // head_count
    keys = 2 * tok
    half = keys // 2
    heads = range(head_count)
    offset = offset_ref[0]
    reset = [resets_ref[seq, i] for i in range(resets_ref.shape[1])]

    def doc_of(position):
        total = jnp.zeros_like(position)
        for r in reset:
            total = total + (r <= position).astype(jnp.int32)
        return total

    start_doc = sum(((r < offset).astype(jnp.int32) for r in reset), jnp.int32(0))
    last_doc = sum(((r <= offset + tok - 1).astype(jnp.int32) for r in reset), jnp.int32(0))
    doc_row = doc_of(offset + (iota((1, keys), 1) >> 1))
    doc_col = doc_of(offset + (iota((keys, 1), 0) >> 1))
    doc_tok = doc_of(offset + iota((tok, 1), 0))

    def stacked(x):
        return jnp.concatenate([p.astype(f32) for p in split3(x)], axis=0).astype(bf16)

    def folded(m):
        n = head_count
        return m[:n] + m[n:2 * n] + m[2 * n:3 * n]

    tok_i, key_i = iota((tok, keys), 0), iota((tok, keys), 1)
    gate3 = stacked(gate_ref[0])
    gs_row = folded(mm(gate3, (tok_i <= (key_i >> 1)).astype(f32).astype(bf16)))
    beta_row = folded(
        mm(stacked(beta_ref[0, 0]), (key_i == 2 * tok_i).astype(f32).astype(bf16))
        + mm(stacked(beta_ref[0, 1]), (key_i == 2 * tok_i + 1).astype(f32).astype(bf16))
    )
    gs_tok_row = folded(
        mm(gate3, (iota((tok, tok), 0) <= iota((tok, tok), 1)).astype(f32).astype(bf16))
    )
    gs_col, beta_col, gs_tok = gs_row.T, beta_row.T, gs_tok_row.T

    h_i, h_j = iota((half, half), 0), iota((half, half), 1)
    eye_half = h_i == h_j
    apart = jnp.where(h_i > h_j, h_i ^ h_j, 0)
    widths = [1 << n for n in range((half - 1).bit_length())]
    masks = [
        jnp.logical_and(apart >= w, apart < 2 * w).astype(f32).astype(bf16) for w in widths
    ]
    eye16 = eye_half.astype(f32).astype(bf16)
    eye_size = (iota((size, size), 0) == iota((size, size), 1)).astype(f32)
    top_mask = jnp.logical_and(h_i > h_j, doc_col[:half] == doc_row[:, :half])
    low_i, low_j = iota((half, keys), 0), iota((half, keys), 1)
    bottom_mask = jnp.logical_and(low_i + half > low_j, doc_col[half:] == doc_row)
    tok_linked = jnp.logical_and(
        (iota((tok, keys), 1) >> 1) <= iota((tok, keys), 0), doc_tok == doc_row
    )

    q = [q_ref[0, :, h * size:(h + 1) * size] for h in heads]
    k = [k_ref[0, :, h * size:(h + 1) * size] for h in heads]
    v = [v_ref[0, :, h * size:(h + 1) * size] for h in heads]

    def unit(x):
        return lax.rsqrt(jnp.sum(x * x, axis=1, keepdims=True) + epsilon)

    top, bottom, k_col, k_row, right = [], [], [], [], []
    for h in heads:
        gram_top = mm_nt(k[h][:half], k[h][:half])
        gram_bottom = mm_nt(k[h][half:], k[h])
        k32 = k[h].astype(f32)
        k_col.append(unit(k32))
        squares = jnp.concatenate(
            [
                jnp.sum(jnp.where(eye_half, g, 0.0), axis=0, keepdims=True)
                for g in (gram_top, gram_bottom[:, half:])
            ],
            axis=1,
        )
        k_row.append(lax.rsqrt(squares + epsilon))
        gr, gc = gs_row[h:h + 1], gs_col[:, h:h + 1]
        b_col = beta_col[:, h:h + 1]
        left = b_col * k_col[h]
        carried = jnp.where(doc_col == start_doc, jnp.exp(gc), 0.0)
        right.append(
            jnp.concatenate([k32 * (left * carried), v[h].astype(f32) * b_col], axis=1)
        )
        top.append(
            split(
                jnp.where(
                    top_mask,
                    gram_top * jnp.exp(gc[:half] - gr[:, :half]) * k_row[h][:, :half] * left[:half],
                    0.0,
                )
            )
        )
        bottom.append(
            split(
                jnp.where(
                    bottom_mask, gram_bottom * jnp.exp(gc[half:] - gr) * k_row[h] * left[half:], 0.0
                )
            )
        )

    blocks = [(h, b) for h in heads for b in range(2)]
    part = {(h, b): top[h][0] if b == 0 else bottom[h][0][:, half:] for h, b in blocks}
    inv = {key: eye16 - part[key] * masks[0] for key in blocks}
    for mask in masks[1:]:
        inner = {key: mm(part[key] * mask, inv[key]).astype(bf16) for key in blocks}
        inv = {key: inv[key] - mm(inv[key], inner[key]).astype(bf16) for key in blocks}
    lower = []
    for h in heads:
        inner = mm(bottom[h][0][:, :half], inv[h, 0]).astype(bf16)
        lower.append(
            jnp.concatenate([-mm(inv[h, 1], inner).astype(bf16), inv[h, 1]], axis=1)
        )

    both = []
    for h in heads:
        rough = right[h].astype(bf16)
        g_top = mm(inv[h, 0], rough[:half]).astype(bf16)
        g_bottom = mm(lower[h], rough).astype(bf16)
        guess = jnp.concatenate([g_top, g_bottom], axis=0)
        rest_top = right[h][:half] - g_top.astype(f32) - (
            mm(top[h][0], g_top) + mm(top[h][1], g_top)
        )
        rest_bottom = right[h][half:] - g_bottom.astype(f32) - (
            mm(bottom[h][0], guess) + mm(bottom[h][1], guess)
        )
        rest = jnp.concatenate([rest_top.astype(bf16), rest_bottom.astype(bf16)], axis=0)
        both.append(
            jnp.concatenate(
                [
                    g_top.astype(f32) + mm(inv[h, 0], rest[:half]),
                    g_bottom.astype(f32) + mm(lower[h], rest),
                ],
                axis=0,
            )
        )

    for h in heads:
        gr, gc, gt = gs_row[h:h + 1], gs_col[:, h:h + 1], gs_tok[:, h:h + 1]
        last = gr[:, keys - 1:]
        carried_tok = jnp.where(doc_tok == start_doc, jnp.exp(gt), 0.0)
        closing = jnp.where(doc_col == last_doc, jnp.exp(last - gc), 0.0)
        end_high, end_low = split(both[h] * (closing * k_col[h]))
        ends = mm_tn(k[h], end_high) + mm_tn(k[h], end_low)
        keep = jnp.where(last_doc == start_doc, jnp.exp(last), 0.0)
        transit_ref[h] = keep * eye_size - ends[:, :size]
        filled_ref[h] = ends[:, size:]
        q32 = q[h].astype(f32)
        q_norm = unit(q32)
        probes = jnp.where(
            tok_linked, mm_nt(q[h], k[h]) * jnp.exp(gt - gr) * k_row[h] * q_norm, 0.0
        )
        outs = dot3(probes, both[h])
        reach_ref[h] = (carried_tok * q_norm) * q32 - outs[:, :size]
        own_ref[h] = outs[:, size:]


def local_terms(seq, offset, resets, queries, keys, values, log_gate, beta, earlier=()):
    _, tok, packed = queries.shape
    head_count = log_gate.shape[1]
    size = packed // head_count

    def block(shape):
        return pl.BlockSpec((1,) + shape, lambda i, o, r: (seq,) + (0,) * len(shape))

    whole = pl.BlockSpec((head_count, size, size), lambda i, o, r: (0, 0, 0))
    tall = pl.BlockSpec((head_count, tok, size), lambda i, o, r: (0, 0, 0))
    return pl.pallas_call(
        functools.partial(local_kernel, head_count, seq),
        grid_spec=pltpu.PrefetchScalarGridSpec(
            num_scalar_prefetch=2,
            grid=(1,),
            in_specs=[
                block((tok, packed)),
                block((2 * tok, packed)),
                block((2 * tok, packed)),
                block((head_count, tok)),
                block((2, head_count, tok)),
            ]
            + untouched(earlier),
            out_specs=[whole, whole, tall, tall],
        ),
        out_shape=[
            jax.ShapeDtypeStruct((head_count, size, size), f32),
            jax.ShapeDtypeStruct((head_count, size, size), f32),
            jax.ShapeDtypeStruct((head_count, tok, size), f32),
            jax.ShapeDtypeStruct((head_count, tok, size), f32),
        ],
        compiler_params=pltpu.CompilerParams(vmem_limit_bytes=16 << 20),
        name="local_terms",
    )(offset, resets, queries, keys, values, log_gate, beta, *earlier)


def vmem(count):
    return [pl.BlockSpec(memory_space=pltpu.VMEM)] * count


def untouched(earlier):
    return [pl.BlockSpec(memory_space=pl.ANY)] * len(earlier)


def step_kernel(choices, here_ref, *refs):
    maps, fills, state_ref, out_ref = refs[:choices], refs[choices:2 * choices], refs[2 * choices], refs[-1]
    here = here_ref[0]
    for n in range(choices):

        @pl.when(here == n)
        def _(n=n):
            for h in range(state_ref.shape[0]):
                out_ref[h] = dot3(maps[n][h], state_ref[h]) + fills[n][h]

    @pl.when(jnp.logical_or(here < 0, here >= choices))
    def _():
        out_ref[...] = fills[0][...]


def step(here, maps, fills, state, earlier=()):
    return pl.pallas_call(
        functools.partial(step_kernel, len(maps)),
        in_specs=[pl.BlockSpec(memory_space=pltpu.SMEM)]
        + vmem(2 * len(maps) + 1)
        + untouched(earlier),
        out_specs=pl.BlockSpec(memory_space=pltpu.VMEM),
        out_shape=jax.ShapeDtypeStruct(state.shape, f32),
        compiler_params=pltpu.CompilerParams(vmem_limit_bytes=8 << 20),
        cost_estimate=small_cost,
        name="state_step",
    )(here, *maps, *fills, state, *earlier)


def project_kernel(choices, groups, here_ref, place_ref, reach_ref, own_ref, *refs):
    states, w_ref = refs[:choices], refs[choices]
    send_ref, keep_ref, head_ref, state_ref = refs[-4:]
    heads, _, size = reach_ref.shape
    here, place = here_ref[0], place_ref[0]
    part = w_ref.shape[1] // groups

    @pl.when(here == 0)
    def _():
        for h in range(heads):
            head_ref[:, h * size:(h + 1) * size] = own_ref[h].astype(bf16)

    @pl.when(here > 0)
    def _():
        for n in range(choices):

            @pl.when(here == n + 1)
            def _(n=n):
                state_ref[...] = states[n][...]

        for h in range(heads):
            mixed = own_ref[h] + dot3(reach_ref[h], state_ref[h])
            head_ref[:, h * size:(h + 1) * size] = mixed.astype(bf16)

    for r in range(groups):
        start = pl.multiple_of((place ^ r) * part, part)
        share = mm(head_ref[...], w_ref[:, pl.ds(start, part)])
        if r % 2:
            send_ref[r // 2] = share
        else:
            keep_ref[r // 2] = share


def project(groups, here, place, reach, own, states, w_out, earlier=()):
    heads, tok, size = reach.shape
    part = w_out.shape[1] // groups
    smem = pl.BlockSpec(memory_space=pltpu.SMEM)
    return pl.pallas_call(
        functools.partial(project_kernel, len(states), groups),
        in_specs=[smem, smem] + vmem(3 + len(states)) + untouched(earlier),
        out_specs=vmem(2),
        out_shape=[jax.ShapeDtypeStruct((groups // 2, tok, part), f32)] * 2,
        scratch_shapes=[
            pltpu.VMEM((tok, heads * size), bf16),
            pltpu.VMEM((heads, size, size), f32),
        ],
        compiler_params=pltpu.CompilerParams(vmem_limit_bytes=16 << 20),
        cost_estimate=small_cost,
        name="project",
    )(here, place, reach, own, *states, w_out, *earlier)


def swapped(x, axis, bit):
    size = lax.axis_size(axis)
    return lax.ppermute(x, axis, [(i, i ^ bit) for i in range(size)])


def carry_on(devices, x, round_index, chunks):
    pairs = [(i, i + 1) for i in range(devices - 1) if 0 <= round_index - i < chunks]
    return lax.ppermute(x, "seq", pairs)


def add_kernel(mine_ref, other_ref, *refs):
    leave_ref, stay_ref = refs[-2:]
    for r in range(mine_ref.shape[0]):
        out_ref = leave_ref if r % 2 else stay_ref
        out_ref[r // 2] = mine_ref[r] + other_ref[r]


def add_parts(mine, other, earlier=()):
    part = jax.ShapeDtypeStruct((mine.shape[0] // 2,) + mine.shape[1:], f32)
    return pl.pallas_call(
        add_kernel,
        in_specs=vmem(2) + untouched(earlier),
        out_specs=vmem(2),
        out_shape=[part] * 2,
        compiler_params=pltpu.CompilerParams(vmem_limit_bytes=4 << 20),
        cost_estimate=small_cost,
        name="add_parts",
    )(mine, other, *earlier)


def reduced(send, keep):
    bit = 2
    while True:
        other = swapped(send, "head", bit)
        if keep.shape[0] == 1:
            return keep[0], other[0]
        send, keep = add_parts(keep, other)
        bit *= 2


def shards(queries, keys, values, log_gate, beta, resets, w_out):
    chunks, tok, packed = queries.shape
    groups = lax.axis_size("head")
    devices = lax.axis_size("seq")
    here = lax.axis_index("seq").astype(jnp.int32).reshape(1)
    offset = here * tok
    place = lax.axis_index("head").astype(jnp.int32).reshape(1)
    key_rows = keys.reshape(chunks, 2 * tok, packed)
    value_rows = values.reshape(chunks, 2 * tok, packed)

    def local(s, earlier=()):
        return local_terms(
            s, offset, resets, queries, key_rows, value_rows, log_gate, beta, earlier
        )

    if devices > 8:
        terms = [local(s) for s in range(chunks)]
        pairs = [(i, i + 1) for i in range(devices - 1)]
        no_choice = jnp.zeros((1,), jnp.int32)

        def turn(_, incoming):
            return tuple(
                lax.ppermute(
                    step(no_choice, [terms[s][0]], [terms[s][1]], incoming[s]), "seq", pairs
                )
                for s in range(chunks)
            )

        zero = tuple(jnp.zeros_like(terms[s][1]) for s in range(chunks))
        states = lax.fori_loop(0, devices - 1, turn, zero)
        outs = []
        for s in range(chunks):
            one = jnp.ones((1,), jnp.int32)
            send, keep = project(groups, one, place, terms[s][2], terms[s][3], [states[s]], w_out)
            leave, stay = add_parts(keep, swapped(send, "head", 1))
            outs.append(reduced(leave, stay))
        return jnp.stack([mine + other for mine, other in outs])

    last_round = chunks + devices - 3
    terms, arrived, outs = [], [], []
    token = ()
    for r in range(last_round + devices):
        if r < chunks:
            terms.append(local(r, token))
            token = (terms[r][1],)
        done = r - devices + 1
        if r <= last_round:
            if r == 0:
                sent = terms[0][1]
            else:
                valid = [r - i for i in range(devices - 1) if 0 <= r - i < chunks]
                sent = step(
                    here - (r - valid[0]),
                    [terms[c][0] for c in valid],
                    [terms[c][1] for c in valid],
                    arrived[r - 1],
                    token,
                )
                token = (sent,)
            arrived.append(carry_on(devices, sent, r, chunks))
        if 0 <= done < chunks:
            settled = (outs[done - 2][1],) if done >= 2 else ()
            send, keep = project(
                groups, here, place, terms[done][2], terms[done][3],
                [arrived[done + i] for i in range(devices - 1)], w_out, token + settled,
            )
            leave, stay = add_parts(keep, swapped(send, "head", 1), token)
            token = (leave,)
            outs.append(reduced(leave, stay))
    return jnp.stack([mine + other for mine, other in outs])


def solution(mesh):
    placed = (
        P("grp", "seq", "head"),
        P("grp", "seq", None, "head"),
        P("grp", "seq", None, "head"),
        P("grp", "head", "seq"),
        P("grp", None, "head", "seq"),
        P("grp", None),
        P("head", None),
    )
    return jax.shard_map(
        shards, mesh=mesh, in_specs=placed, out_specs=P("grp", "seq", "head"), check_vma=False
    )
```

time: 95 us -> 91.2 us (0.960)
  the two profiles are of different devices: /device:TPU:22 before, /device:TPU:24 now
where the time goes in v2:
time: 91.2 us; the launch traced here: 91 us
  waiting for transfers between devices  42.5 us (47%)
  Pallas kernels  27.9 us (31%)
  starting transfers between devices  11.5 us (13%)
  local copies, waits for them, and re-layouts  7.39 us (8%)
  other arithmetic  1.2 us (1%)
    pallas_call x4, Pallas kernels, local_terms(): pl.pallas_call(functools.partial(local_kernel, head_count, seq), grid_spe...  23.7 us
    ppermute x6, waiting for transfers between devices, carry_on(): return lax.ppermute(x, 'seq', pairs)  23.2 us
    ppermute x8, waiting for transfers between devices, swapped(): return lax.ppermute(x, axis, [(i, i ^ bit) for i in range(size)])  19.2 us
    ppermute x6, starting transfers between devices, carry_on(): return lax.ppermute(x, 'seq', pairs)  6.92 us
    ppermute x8, starting transfers between devices, swapped(): return lax.ppermute(x, axis, [(i, i ^ bit) for i in range(size)])  4.6 us
    unnamed x50, local copies, waits for them, and re-layouts  4.4 us
    pallas_call x4, Pallas kernels, project(): pl.pallas_call(functools.partial(project_kernel, len(states), groups), in...  2.97 us
  transfers between devices with their start and end apart: 14, of which 9 were waited for; matrix products, arithmetic and copies ran while one was open for 0% of the time, Pallas kernels for 20%

profile of v2, /device:TPU:24, one launch (start us, length us, event | category | flops | bytes accessed | tf_op | source)
XLA Modules:
  0.0 91.0 jit_solution(8770647693278261506)
XLA Ops:
  0.0 1.5 %reshape.14.k_ref = bf16[4,256,512]{2,1,0:T(8,128)(2,1)S(1)} reshape(bf16[4,128,2,512]{3,2,1,0:T(2,128)(2,1)} %param.8) | data formatting | bytes 2097152 | tf_op jit(solution)/shard_map/reshape | solution.py:381
  1.6 1.5 %reshape.15.v_ref = bf16[4,256,512]{2,1,0:T(8,128)(2,1)S(1)} reshape(bf16[4,128,2,512]{3,2,1,0:T(2,128)(2,1)} %param.9) | data formatting | bytes 2097152 | tf_op jit(solution)/shard_map/reshape | solution.py:382
  3.1 5.9 %local_terms.4 = (f32[4,128,128]{2,1,0:T(8,128)S(1)}, f32[4,128,128]{2,1,0:T(8,128)S(1)}, f32[4,128,128]{2,1,0:T(8,128)S(1)}, f32[4,128,128]{2,1,0:T(8,128)S(1)}) custom-call(s32[1]{0:T(128)S(6)} %mul.3.offset_ref, s32[4,3]{1,0:T(4,128)S(1)} %copy-done.24, bf16[4,128,512]{2,1,0:T(8,128)(2,1)S(1)} %copy-done.1, bf16[4,256,512]{2,1,0:T(8,128)(2,1)S(1)} %reshape.14.k_ref, ...), custom_call_target="tpu_custom_call" | custom-call | tf_op jit(solution)/shard_map/local_terms/pallas_call | solution.py:219
  9.0 0.7 copy-done.19
  9.7 0.7 copy-done.21
  10.4 0.7 collective-permute-start
  11.1 5.9 %local_terms.5 = (f32[4,128,128]{2,1,0:T(8,128)S(1)}, f32[4,128,128]{2,1,0:T(8,128)S(1)}, f32[4,128,128]{2,1,0:T(8,128)S(1)}, f32[4,128,128]{2,1,0:T(8,128)S(1)}) custom-call(s32[1]{0:T(128)S(6)} %mul.3.offset_ref, s32[4,3]{1,0:T(4,128)S(1)} %copy-done.24, bf16[4,128,512]{2,1,0:T(8,128)(2,1)S(1)} %copy-done.1, bf16[4,256,512]{2,1,0:T(8,128)(2,1)S(1)} %reshape.14.k_ref, ...), custom_call_target="tpu_custom_call" | custom-call | tf_op jit(solution)/shard_map/local_terms/pallas_call | solution.py:219
  17.1 0.6 copy-done.15
  17.7 0.1 copy-done.17
  17.9 0.7 copy-done.8
  18.6 0.8 collective-permute-start.1
  19.4 5.9 %local_terms.6 = (f32[4,128,128]{2,1,0:T(8,128)S(1)}, f32[4,128,128]{2,1,0:T(8,128)S(1)}, f32[4,128,128]{2,1,0:T(8,128)S(1)}, f32[4,128,128]{2,1,0:T(8,128)S(1)}) custom-call(s32[1]{0:T(128)S(6)} %mul.3.offset_ref, s32[4,3]{1,0:T(4,128)S(1)} %copy-done.24, bf16[4,128,512]{2,1,0:T(8,128)(2,1)S(1)} %copy-done.1, bf16[4,256,512]{2,1,0:T(8,128)(2,1)S(1)} %reshape.14.k_ref, ...), custom_call_target="tpu_custom_call" | custom-call | tf_op jit(solution)/shard_map/local_terms/pallas_call | solution.py:219
  25.4 0.7 copy-done.13
  26.1 0.8 state_step.6.refs_0_
  26.9 0.1 copy-done.6
  27.0 0.7 copy-done.2
  27.7 1.3 %collective-permute-start.2 = (f32[4,128,128]{2,1,0:T(8,128)}, f32[4,128,128]{2,1,0:T(8,128)S(1)}, u32[]{:S(2)}, u32[]{:S(2)}) collective-permute-start(f32[4,128,128]{2,1,0:T(8,128)} %state_step.6.refs_0_), channel_id=1, source_target_pairs={{0,4},{4,8},{8,12},{1,5},{5,9},{9,13},{2,6},{6,10},{10,14},{3,7},{... | collective-permute-start | bytes 786440 | tf_op jit(solution)/shard_map/ppermute | solution.py:341
  29.0 0.0 copy-start
  29.0 5.9 %local_terms.7 = (f32[4,128,128]{2,1,0:T(8,128)S(1)}, f32[4,128,128]{2,1,0:T(8,128)S(1)}, f32[4,128,128]{2,1,0:T(8,128)S(1)}, f32[4,128,128]{2,1,0:T(8,128)S(1)}) custom-call(s32[1]{0:T(128)S(6)} %mul.3.offset_ref, s32[4,3]{1,0:T(4,128)S(1)} %copy-done.24, bf16[4,128,512]{2,1,0:T(8,128)(2,1)S(1)} %copy-done.1, bf16[4,256,512]{2,1,0:T(8,128)(2,1)S(1)} %reshape.14.k_ref, ...), custom_call_target="tpu_custom_call" | custom-call | tf_op jit(solution)/shard_map/local_terms/pallas_call | solution.py:219
  35.0 3.1 %collective-permute-done.2.refs_6_.refs_2_.refs_1_.refs_0_ = f32[4,128,128]{2,1,0:T(8,128)S(1)} collective-permute-done((f32[4,128,128]{2,1,0:T(8,128)}, f32[4,128,128]{2,1,0:T(8,128)S(1)}, u32[]{:S(2)}, u32[]{:S(2)}) %collective-permute-start.2) | collective-permute-done | bytes 262176 | tf_op jit(solution)/shard_map/ppermute | solution.py:341
  38.2 0.7 project.4
  39.0 0.1 collective-permute-start.3
  39.1 1.4 %collective-permute-start.5 = (f32[4,128,128]{2,1,0:T(8,128)S(1)}, f32[4,128,128]{2,1,0:T(8,128)S(1)}, u32[]{:S(2)}, u32[]{:S(2)}) collective-permute-start(f32[4,128,128]{2,1,0:T(8,128)S(1)} %state_step.7.refs_4_.refs_0_), channel_id=1, source_target_pairs={{0,4},{4,8},{8,12},{1,5},{5,9},{9,13},{2,6},{6,10},{10,14},{3,7},{... | collective-permute-start | bytes 786440 | tf_op jit(solution)/shard_map/ppermute | solution.py:341
  40.5 0.5 collective-permute-done.3.other_ref
  40.9 0.1 add_parts.4
  41.0 9.2 %collective-permute-done.5.refs_4_.refs_2_.refs_1_.refs_0_ = f32[4,128,128]{2,1,0:T(8,128)S(1)} collective-permute-done((f32[4,128,128]{2,1,0:T(8,128)S(1)}, f32[4,128,128]{2,1,0:T(8,128)S(1)}, u32[]{:S(2)}, u32[]{:S(2)}) %collective-permute-start.5) | collective-permute-done | bytes 262176 | tf_op jit(solution)/shard_map/ppermute | solution.py:341
  50.3 0.7 project.5
  51.1 0.1 collective-permute-start.6
  51.1 1.4 %collective-permute-start.8 = (f32[4,128,128]{2,1,0:T(8,128)S(1)}, f32[4,128,128]{2,1,0:T(8,128)S(1)}, u32[]{:S(2)}, u32[]{:S(2)}) collective-permute-start(f32[4,128,128]{2,1,0:T(8,128)S(1)} %state_step.8.refs_4_.refs_0_), channel_id=1, source_target_pairs={{4,8},{8,12},{5,9},{9,13},{6,10},{10,14},{7,11},{11,15},{20,24},{2... | collective-permute-start | bytes 786440 | tf_op jit(solution)/shard_map/ppermute | solution.py:341
  52.6 1.6 %collective-permute-start.4 = (f32[1,128,512]{2,1,0:T(8,128)S(1)}, f32[1,128,512]{2,1,0:T(8,128)S(1)}, u32[]{:S(2)}, u32[]{:S(2)}) collective-permute-start(f32[1,128,512]{2,1,0:T(8,128)S(1)} %get-tuple-element.50.refs_5_), channel_id=1, source_target_pairs={{0,2},{1,3},{2,0},{3,1},{4,6},{5,7},{6,4},{7,5},{8,10},{9,11},{10,... | collective-permute-start | bytes 786440 | tf_op jit(solution)/shard_map/ppermute | solution.py:336
  54.1 0.1 add_parts.5
  54.2 7.8 %collective-permute-done.8.refs_2_.refs_1_ = f32[4,128,128]{2,1,0:T(8,128)S(1)} collective-permute-done((f32[4,128,128]{2,1,0:T(8,128)S(1)}, f32[4,128,128]{2,1,0:T(8,128)S(1)}, u32[]{:S(2)}, u32[]{:S(2)}) %collective-permute-start.8) | collective-permute-done | bytes 262176 | tf_op jit(solution)/shard_map/ppermute | solution.py:341
  62.0 0.8 project.6
  62.8 0.1 collective-permute-start.9
  62.9 1.6 %collective-permute-start.7 = (f32[1,128,512]{2,1,0:T(8,128)S(1)}, f32[1,128,512]{2,1,0:T(8,128)S(1)}, u32[]{:S(2)}, u32[]{:S(2)}) collective-permute-start(f32[1,128,512]{2,1,0:T(8,128)S(1)} %get-tuple-element.56.refs_3_), channel_id=1, source_target_pairs={{0,2},{1,3},{2,0},{3,1},{4,6},{5,7},{6,4},{7,5},{8,10},{9,11},{10,... | collective-permute-start | bytes 786440 | tf_op jit(solution)/shard_map/ppermute | solution.py:336
  64.5 1.3 %collective-permute-start.11 = (f32[4,128,128]{2,1,0:T(8,128)S(1)}, f32[4,128,128]{2,1,0:T(8,128)S(1)}, u32[]{:S(2)}, u32[]{:S(2)}) collective-permute-start(f32[4,128,128]{2,1,0:T(8,128)S(1)} %state_step.9.refs_4_.refs_0_), channel_id=1, source_target_pairs={{8,12},{9,13},{10,14},{11,15},{24,28},{25,29},{26,30},{27,31}} | collective-permute-start | bytes 786440 | tf_op jit(solution)/shard_map/ppermute | solution.py:341
  65.8 0.1 add_parts.6
  65.8 5.8 %collective-permute-done.7 = f32[1,128,512]{2,1,0:T(8,128)S(1)} collective-permute-done((f32[1,128,512]{2,1,0:T(8,128)S(1)}, f32[1,128,512]{2,1,0:T(8,128)S(1)}, u32[]{:S(2)}, u32[]{:S(2)}) %collective-permute-start.7) | collective-permute-done | bytes 262176 | tf_op jit(solution)/shard_map/ppermute | solution.py:336
  71.6 3.1 %collective-permute-done.11.refs_2_ = f32[4,128,128]{2,1,0:T(8,128)S(1)} collective-permute-done((f32[4,128,128]{2,1,0:T(8,128)S(1)}, f32[4,128,128]{2,1,0:T(8,128)S(1)}, u32[]{:S(2)}, u32[]{:S(2)}) %collective-permute-start.11) | collective-permute-done | bytes 262176 | tf_op jit(solution)/shard_map/ppermute | solution.py:341
  74.7 0.7 project.7
  75.4 0.1 collective-permute-start.12
  75.5 0.6 collective-permute-start.10
  76.1 1.3 %collective-permute-done.12.other_ref = f32[2,128,512]{2,1,0:T(8,128)S(1)} collective-permute-done((f32[2,128,512]{2,1,0:T(8,128)S(1)}, f32[2,128,512]{2,1,0:T(8,128)S(1)}, u32[]{:S(2)}, u32[]{:S(2)}) %collective-permute-start.12) | collective-permute-done | bytes 524320 | tf_op jit(solution)/shard_map/ppermute | solution.py:336
  77.4 0.1 add_parts.7
  77.5 0.6 collective-permute-start.13
  78.1 6.6 %collective-permute-done.10 = f32[1,128,512]{2,1,0:T(8,128)S(1)} collective-permute-done((f32[1,128,512]{2,1,0:T(8,128)S(1)}, f32[1,128,512]{2,1,0:T(8,128)S(1)}, u32[]{:S(2)}, u32[]{:S(2)}) %collective-permute-start.10) | collective-permute-done | bytes 262176 | tf_op jit(solution)/shard_map/ppermute | solution.py:336
  84.7 5.1 %collective-permute-done.13 = f32[1,128,512]{2,1,0:T(8,128)S(1)} collective-permute-done((f32[1,128,512]{2,1,0:T(8,128)S(1)}, f32[1,128,512]{2,1,0:T(8,128)S(1)}, u32[]{:S(2)}, u32[]{:S(2)}) %collective-permute-start.13) | collective-permute-done | bytes 262176 | tf_op jit(solution)/shard_map/ppermute | solution.py:336
  89.9 1.0 %pad_maximum_fusion = f32[4,128,512]{2,1,0:T(8,128)} fusion(f32[1,128,512]{2,1,0:T(8,128)S(1)} %add.21, f32[1,128,512]{2,1,0:T(8,128)S(1)} %add.20, f32[1,128,512]{2,1,0:T(8,128)S(1)} %add.19, f32[1,128,512]{2,1,0:T(8,128)S(1)} %add.18), kind=kLoop, calls=%fused_computation | loop fusion | flops 786432 | bytes 2097152 | tf_op jit(solution)/shard_map/stack | solution.py:443
  (54 shorter events, 0.3 us)
Async XLA Ops:
  0.0 3.0 %copy-start.1 = (bf16[4,128,512]{2,1,0:T(8,128)(2,1)S(1)}, bf16[4,128,512]{2,1,0:T(8,128)(2,1)}, u32[]{:S(2)}) copy-start(bf16[4,128,512]{2,1,0:T(8,128)(2,1)} %q_ref.7) | copy-start | bytes 1572868
  0.0 3.0 %copy-start.10 = (f32[4,2,4,128]{3,2,1,0:T(4,128)S(1)}, f32[4,2,4,128]{3,2,1,0:T(4,128)}, u32[]{:S(2)}) copy-start(f32[4,2,4,128]{3,2,1,0:T(4,128)} %beta_ref.7) | copy-start | bytes 49156
  0.0 3.1 %copy-start.23 = (f32[4,4,128]{2,1,0:T(4,128)S(1)}, f32[4,4,128]{2,1,0:T(4,128)}, u32[]{:S(2)}) copy-start(f32[4,4,128]{2,1,0:T(4,128)} %gate_ref.7) | copy-start | bytes 24580
  0.0 3.1 %copy-start.24 = (s32[4,3]{1,0:T(4,128)S(1)}, s32[4,3]{1,0:T(4,128)}, u32[]{:S(2)}) copy-start(s32[4,3]{1,0:T(4,128)} %resets_ref.7) | copy-start | bytes 148
  9.0 0.7 copy-start.19
  9.7 0.7 copy-start.21
  10.4 6.7 %collective-permute-start = (f32[4,128,128]{2,1,0:T(8,128)S(1)}, f32[4,128,128]{2,1,0:T(8,128)S(1)}, u32[]{:S(2)}, u32[]{:S(2)}) collective-permute-start(f32[4,128,128]{2,1,0:T(8,128)S(1)} %get-tuple-element.39.refs_0_.refs_3_.refs_5_), channel_id=1, source_target_pairs={{0,4},{1,5},{2,6},{3,7},{16,20},{17,21},{18,22},{19,23}} | collective-permute-start | bytes 786440 | tf_op jit(solution)/shard_map/ppermute | solution.py:341
  17.0 0.7 copy-start.15
  17.0 0.8 copy-start.17
  17.1 9.0 %copy-start.4 = (f32[4,128,128]{2,1,0:T(8,128)}, f32[4,128,128]{2,1,0:T(8,128)S(1)}, u32[]{:S(2)}) copy-start(f32[4,128,128]{2,1,0:T(8,128)S(1)} %get-tuple-element.40.refs_0_.refs_1_.refs_2_) | copy-start | bytes 786436
  17.9 0.7 copy-start.8
  18.6 7.5 %collective-permute-start.1 = (f32[4,128,128]{2,1,0:T(8,128)S(1)}, f32[4,128,128]{2,1,0:T(8,128)S(1)}, u32[]{:S(2)}, u32[]{:S(2)}) collective-permute-start(f32[4,128,128]{2,1,0:T(8,128)S(1)} %state_step.5.refs_0_), channel_id=1, source_target_pairs={{0,4},{4,8},{1,5},{5,9},{2,6},{6,10},{3,7},{7,11},{16,20},{20,24},... | collective-permute-start | bytes 786440 | tf_op jit(solution)/shard_map/ppermute | solution.py:341
  25.4 0.7 copy-start.13
  26.1 0.8 copy-start.11
  26.1 0.9 copy-start.6
  27.0 0.7 copy-start.2
  27.7 10.5 %collective-permute-start.2 = (f32[4,128,128]{2,1,0:T(8,128)}, f32[4,128,128]{2,1,0:T(8,128)S(1)}, u32[]{:S(2)}, u32[]{:S(2)}) collective-permute-start(f32[4,128,128]{2,1,0:T(8,128)} %state_step.6.refs_0_), channel_id=1, source_target_pairs={{0,4},{4,8},{8,12},{1,5},{5,9},{9,13},{2,6},{6,10},{10,14},{3,7},{... | collective-permute-start | bytes 786440 | tf_op jit(solution)/shard_map/ppermute | solution.py:341
  29.0 9.2 %copy-start.3 = (f32[4,128,128]{2,1,0:T(8,128)S(1)}, f32[4,128,128]{2,1,0:T(8,128)}, u32[]{:S(2)}) copy-start(f32[4,128,128]{2,1,0:T(8,128)} %copy-done.2) | copy-start | bytes 786436
  29.0 9.2 %copy-start.5 = (f32[4,128,128]{2,1,0:T(8,128)S(1)}, f32[4,128,128]{2,1,0:T(8,128)}, u32[]{:S(2)}) copy-start(f32[4,128,128]{2,1,0:T(8,128)} %copy-done.4) | copy-start | bytes 786436
  29.0 9.2 %copy-start = (bf16[512,2048]{1,0:T(8,128)(2,1)S(1)}, bf16[512,2048]{1,0:T(8,128)(2,1)}, u32[]{:S(2)}) copy-start(bf16[512,2048]{1,0:T(8,128)(2,1)} %refs_3_.7) | copy-start | bytes 6291460
  29.0 9.2 %copy-start.7 = (f32[4,128,128]{2,1,0:T(8,128)S(1)}, f32[4,128,128]{2,1,0:T(8,128)}, u32[]{:S(2)}) copy-start(f32[4,128,128]{2,1,0:T(8,128)} %copy-done.6) | copy-start | bytes 786436
  29.0 9.2 %copy-start.9 = (f32[4,128,128]{2,1,0:T(8,128)S(1)}, f32[4,128,128]{2,1,0:T(8,128)}, u32[]{:S(2)}) copy-start(f32[4,128,128]{2,1,0:T(8,128)} %copy-done.8) | copy-start | bytes 786436
  29.0 9.2 %copy-start.20 = (f32[4,128,128]{2,1,0:T(8,128)S(1)}, f32[4,128,128]{2,1,0:T(8,128)}, u32[]{:S(2)}) copy-start(f32[4,128,128]{2,1,0:T(8,128)} %copy-done.19) | copy-start | bytes 786436
  29.0 9.2 %copy-start.22 = (f32[4,128,128]{2,1,0:T(8,128)S(1)}, f32[4,128,128]{2,1,0:T(8,128)}, u32[]{:S(2)}) copy-start(f32[4,128,128]{2,1,0:T(8,128)} %copy-done.21) | copy-start | bytes 786436
  39.0 11.3 %copy-start.16 = (f32[4,128,128]{2,1,0:T(8,128)S(1)}, f32[4,128,128]{2,1,0:T(8,128)}, u32[]{:S(2)}) copy-start(f32[4,128,128]{2,1,0:T(8,128)} %copy-done.15) | copy-start | bytes 786436
  39.0 11.3 %copy-start.18 = (f32[4,128,128]{2,1,0:T(8,128)S(1)}, f32[4,128,128]{2,1,0:T(8,128)}, u32[]{:S(2)}) copy-start(f32[4,128,128]{2,1,0:T(8,128)} %copy-done.17) | copy-start | bytes 786436
  39.0 2.0 %collective-permute-start.3 = (f32[2,128,512]{2,1,0:T(8,128)S(1)}, f32[2,128,512]{2,1,0:T(8,128)S(1)}, u32[]{:S(2)}, u32[]{:S(2)}) collective-permute-start(f32[2,128,512]{2,1,0:T(8,128)S(1)} %get-tuple-element.48), channel_id=1, source_target_pairs={{0,1},{1,0},{2,3},{3,2},{4,5},{5,4},{6,7},{7,6},{8,9},{9,8},{10,11... | collective-permute-start | bytes 1572872 | tf_op jit(solution)/shard_map/ppermute | solution.py:336
  39.1 11.2 %collective-permute-start.5 = (f32[4,128,128]{2,1,0:T(8,128)S(1)}, f32[4,128,128]{2,1,0:T(8,128)S(1)}, u32[]{:S(2)}, u32[]{:S(2)}) collective-permute-start(f32[4,128,128]{2,1,0:T(8,128)S(1)} %state_step.7.refs_4_.refs_0_), channel_id=1, source_target_pairs={{0,4},{4,8},{8,12},{1,5},{5,9},{9,13},{2,6},{6,10},{10,14},{3,7},{... | collective-permute-start | bytes 786440 | tf_op jit(solution)/shard_map/ppermute | solution.py:341
  51.0 11.0 %copy-start.12 = (f32[4,128,128]{2,1,0:T(8,128)S(1)}, f32[4,128,128]{2,1,0:T(8,128)}, u32[]{:S(2)}) copy-start(f32[4,128,128]{2,1,0:T(8,128)} %copy-done.11) | copy-start | bytes 786436
  51.0 11.0 %copy-start.14 = (f32[4,128,128]{2,1,0:T(8,128)S(1)}, f32[4,128,128]{2,1,0:T(8,128)}, u32[]{:S(2)}) copy-start(f32[4,128,128]{2,1,0:T(8,128)} %copy-done.13) | copy-start | bytes 786436
  51.1 3.1 %collective-permute-start.6 = (f32[2,128,512]{2,1,0:T(8,128)S(1)}, f32[2,128,512]{2,1,0:T(8,128)S(1)}, u32[]{:S(2)}, u32[]{:S(2)}) collective-permute-start(f32[2,128,512]{2,1,0:T(8,128)S(1)} %get-tuple-element.54), channel_id=1, source_target_pairs={{0,1},{1,0},{2,3},{3,2},{4,5},{5,4},{6,7},{7,6},{8,9},{9,8},{10,11... | collective-permute-start | bytes 1572872 | tf_op jit(solution)/shard_map/ppermute | solution.py:336
  51.1 10.8 %collective-permute-start.8 = (f32[4,128,128]{2,1,0:T(8,128)S(1)}, f32[4,128,128]{2,1,0:T(8,128)S(1)}, u32[]{:S(2)}, u32[]{:S(2)}) collective-permute-start(f32[4,128,128]{2,1,0:T(8,128)S(1)} %state_step.8.refs_4_.refs_0_), channel_id=1, source_target_pairs={{4,8},{8,12},{5,9},{9,13},{6,10},{10,14},{7,11},{11,15},{20,24},{2... | collective-permute-start | bytes 786440 | tf_op jit(solution)/shard_map/ppermute | solution.py:341
  52.6 9.4 %collective-permute-start.4 = (f32[1,128,512]{2,1,0:T(8,128)S(1)}, f32[1,128,512]{2,1,0:T(8,128)S(1)}, u32[]{:S(2)}, u32[]{:S(2)}) collective-permute-start(f32[1,128,512]{2,1,0:T(8,128)S(1)} %get-tuple-element.50.refs_5_), channel_id=1, source_target_pairs={{0,2},{1,3},{2,0},{3,1},{4,6},{5,7},{6,4},{7,5},{8,10},{9,11},{10,... | collective-permute-start | bytes 786440 | tf_op jit(solution)/shard_map/ppermute | solution.py:336
  62.8 2.9 %collective-permute-start.9 = (f32[2,128,512]{2,1,0:T(8,128)S(1)}, f32[2,128,512]{2,1,0:T(8,128)S(1)}, u32[]{:S(2)}, u32[]{:S(2)}) collective-permute-start(f32[2,128,512]{2,1,0:T(8,128)S(1)} %get-tuple-element.60), channel_id=1, source_target_pairs={{0,1},{1,0},{2,3},{3,2},{4,5},{5,4},{6,7},{7,6},{8,9},{9,8},{10,11... | collective-permute-start | bytes 1572872 | tf_op jit(solution)/shard_map/ppermute | solution.py:336
  62.9 8.7 %collective-permute-start.7 = (f32[1,128,512]{2,1,0:T(8,128)S(1)}, f32[1,128,512]{2,1,0:T(8,128)S(1)}, u32[]{:S(2)}, u32[]{:S(2)}) collective-permute-start(f32[1,128,512]{2,1,0:T(8,128)S(1)} %get-tuple-element.56.refs_3_), channel_id=1, source_target_pairs={{0,2},{1,3},{2,0},{3,1},{4,6},{5,7},{6,4},{7,5},{8,10},{9,11},{10,... | collective-permute-start | bytes 786440 | tf_op jit(solution)/shard_map/ppermute | solution.py:336
  64.5 10.3 %collective-permute-start.11 = (f32[4,128,128]{2,1,0:T(8,128)S(1)}, f32[4,128,128]{2,1,0:T(8,128)S(1)}, u32[]{:S(2)}, u32[]{:S(2)}) collective-permute-start(f32[4,128,128]{2,1,0:T(8,128)S(1)} %state_step.9.refs_4_.refs_0_), channel_id=1, source_target_pairs={{8,12},{9,13},{10,14},{11,15},{24,28},{25,29},{26,30},{27,31}} | collective-permute-start | bytes 786440 | tf_op jit(solution)/shard_map/ppermute | solution.py:341
  75.4 2.0 %collective-permute-start.12 = (f32[2,128,512]{2,1,0:T(8,128)S(1)}, f32[2,128,512]{2,1,0:T(8,128)S(1)}, u32[]{:S(2)}, u32[]{:S(2)}) collective-permute-start(f32[2,128,512]{2,1,0:T(8,128)S(1)} %get-tuple-element.66), channel_id=1, source_target_pairs={{0,1},{1,0},{2,3},{3,2},{4,5},{5,4},{6,7},{7,6},{8,9},{9,8},{10,11... | collective-permute-start | bytes 1572872 | tf_op jit(solution)/shard_map/ppermute | solution.py:336
  75.5 9.2 %collective-permute-start.10 = (f32[1,128,512]{2,1,0:T(8,128)S(1)}, f32[1,128,512]{2,1,0:T(8,128)S(1)}, u32[]{:S(2)}, u32[]{:S(2)}) collective-permute-start(f32[1,128,512]{2,1,0:T(8,128)S(1)} %get-tuple-element.62.refs_4_.refs_0_), channel_id=1, source_target_pairs={{0,2},{1,3},{2,0},{3,1},{4,6},{5,7},{6,4},{7,5},{8,10},{9,11},{10,... | collective-permute-start | bytes 786440 | tf_op jit(solution)/shard_map/ppermute | solution.py:336
  77.5 12.4 %collective-permute-start.13 = (f32[1,128,512]{2,1,0:T(8,128)S(1)}, f32[1,128,512]{2,1,0:T(8,128)S(1)}, u32[]{:S(2)}, u32[]{:S(2)}) collective-permute-start(f32[1,128,512]{2,1,0:T(8,128)S(1)} %get-tuple-element.68), channel_id=1, source_target_pairs={{0,2},{1,3},{2,0},{3,1},{4,6},{5,7},{6,4},{7,5},{8,10},{9,11},{10,... | collective-permute-start | bytes 786440 | tf_op jit(solution)/shard_map/ppermute | solution.py:336

commit v3 on v2

--- a/solution.py
+++ b/solution.py
@@ -281,7 +281,8 @@
 
 def project_kernel(choices, groups, here_ref, place_ref, reach_ref, own_ref, *refs):
     states, w_ref = refs[:choices], refs[choices]
-    send_ref, keep_ref, head_ref, state_ref = refs[-4:]
+    keep_ref, head_ref, state_ref = refs[-3:]
+    send_refs = refs[-3 - groups // 2:-3]
     heads, _, size = reach_ref.shape
     here, place = here_ref[0], place_ref[0]
     part = w_ref.shape[1] // groups
@@ -307,7 +308,7 @@
         start = pl.multiple_of((place ^ r) * part, part)
         share = mm(head_ref[...], w_ref[:, pl.ds(start, part)])
         if r % 2:
-            send_ref[r // 2] = share
+            send_refs[r // 2][...] = share
         else:
             keep_ref[r // 2] = share
 
@@ -315,12 +316,14 @@
 def project(groups, here, place, reach, own, states, w_out, earlier=()):
     heads, tok, size = reach.shape
     part = w_out.shape[1] // groups
+    mid = groups // 2
     smem = pl.BlockSpec(memory_space=pltpu.SMEM)
-    return pl.pallas_call(
+    outs = pl.pallas_call(
         functools.partial(project_kernel, len(states), groups),
         in_specs=[smem, smem] + vmem(3 + len(states)) + untouched(earlier),
-        out_specs=vmem(2),
-        out_shape=[jax.ShapeDtypeStruct((groups // 2, tok, part), f32)] * 2,
+        out_specs=vmem(mid + 1),
+        out_shape=[jax.ShapeDtypeStruct((tok, part), f32)] * mid
+        + [jax.ShapeDtypeStruct((mid, tok, part), f32)],
         scratch_shapes=[
             pltpu.VMEM((tok, heads * size), bf16),
             pltpu.VMEM((heads, size, size), f32),
@@ -329,6 +332,7 @@
         cost_estimate=small_cost,
         name="project",
     )(here, place, reach, own, *states, w_out, *earlier)
+    return outs[:mid], outs[mid]
 
 
 def swapped(x, axis, bit):
@@ -341,24 +345,24 @@
     return lax.ppermute(x, "seq", pairs)
 
 
-def add_kernel(mine_ref, other_ref, *refs):
+def add_kernel(mine_ref, *refs):
     leave_ref, stay_ref = refs[-2:]
     for r in range(mine_ref.shape[0]):
         out_ref = leave_ref if r % 2 else stay_ref
-        out_ref[r // 2] = mine_ref[r] + other_ref[r]
-
-
-def add_parts(mine, other, earlier=()):
+        out_ref[r // 2] = mine_ref[r] + refs[r][...]
+
+
+def add_parts(mine, others, earlier=()):
     part = jax.ShapeDtypeStruct((mine.shape[0] // 2,) + mine.shape[1:], f32)
     return pl.pallas_call(
         add_kernel,
-        in_specs=vmem(2) + untouched(earlier),
+        in_specs=vmem(1 + len(others)) + untouched(earlier),
         out_specs=vmem(2),
         out_shape=[part] * 2,
         compiler_params=pltpu.CompilerParams(vmem_limit_bytes=4 << 20),
         cost_estimate=small_cost,
         name="add_parts",
-    )(mine, other, *earlier)
+    )(mine, *others, *earlier)
 
 
 def reduced(send, keep):
@@ -367,7 +371,7 @@
         other = swapped(send, "head", bit)
         if keep.shape[0] == 1:
             return keep[0], other[0]
-        send, keep = add_parts(keep, other)
+        send, keep = add_parts(keep, list(other))
         bit *= 2
 
 
@@ -404,42 +408,59 @@
         outs = []
         for s in range(chunks):
             one = jnp.ones((1,), jnp.int32)
-            send, keep = project(groups, one, place, terms[s][2], terms[s][3], [states[s]], w_out)
-            leave, stay = add_parts(keep, swapped(send, "head", 1))
+            sends, keep = project(groups, one, place, terms[s][2], terms[s][3], [states[s]], w_out)
+            leave, stay = add_parts(keep, [swapped(x, "head", 1) for x in sends])
             outs.append(reduced(leave, stay))
         return jnp.stack([mine + other for mine, other in outs])
 
     last_round = chunks + devices - 3
-    terms, arrived, outs = [], [], []
+    terms, arrived, partial, outs = [], [], [], []
     token = ()
-    for r in range(last_round + devices):
+
+    def add_up(c, token):
+        sends, keep = partial[c]
+        settled = (outs[c - 2][1],) if c == chunks - 1 and c >= 2 else ()
+        leave, stay = add_parts(keep, [swapped(x, "head", 1) for x in sends], token + settled)
+        outs.append(reduced(leave, stay))
+        return (leave,)
+
+    def projected(c, token):
+        if 2 <= c < chunks - 1:
+            token = token + (outs[c - 2][1],)
+        partial.append(
+            project(
+                groups, here, place, terms[c][2], terms[c][3],
+                [arrived[c + i] for i in range(devices - 1)], w_out, token,
+            )
+        )
+        return (partial[c][1],)
+
+    for r in range(last_round + 1):
         if r < chunks:
             terms.append(local(r, token))
             token = (terms[r][1],)
+        if r == 0:
+            sent = terms[0][1]
+        else:
+            valid = [r - i for i in range(devices - 1) if 0 <= r - i < chunks]
+            sent = step(
+                here - (r - valid[0]),
+                [terms[c][0] for c in valid],
+                [terms[c][1] for c in valid],
+                arrived[r - 1],
+                token,
+            )
+            token = (sent,)
+        arrived.append(carry_on(devices, sent, r, chunks))
         done = r - devices + 1
-        if r <= last_round:
-            if r == 0:
-                sent = terms[0][1]
-            else:
-                valid = [r - i for i in range(devices - 1) if 0 <= r - i < chunks]
-                sent = step(
-                    here - (r - valid[0]),
-                    [terms[c][0] for c in valid],
-                    [terms[c][1] for c in valid],
-                    arrived[r - 1],
-                    token,
-                )
-                token = (sent,)
-            arrived.append(carry_on(devices, sent, r, chunks))
-        if 0 <= done < chunks:
-            settled = (outs[done - 2][1],) if done >= 2 else ()
-            send, keep = project(
-                groups, here, place, terms[done][2], terms[done][3],
-                [arrived[done + i] for i in range(devices - 1)], w_out, token + settled,
-            )
-            leave, stay = add_parts(keep, swapped(send, "head", 1), token)
-            token = (leave,)
-            outs.append(reduced(leave, stay))
+        if done >= 1:
+            token = add_up(done - 1, token)
+        if done >= 0:
+            token = projected(done, token)
+    done = last_round - devices + 2
+    token = projected(done, token)
+    token = add_up(done - 1, token)
+    token = add_up(done, token)
     return jnp.stack([mine + other for mine, other in outs])
 
 

time: 91.2 us -> 81.7 us (0.90)
  the two profiles are of different devices: /device:TPU:24 before, /device:TPU:22 now
where the time goes in v3:
time: 81.7 us; the launch traced here: 80.5 us
  Pallas kernels  28.7 us (35%)
  waiting for transfers between devices  24.1 us (29%)
  starting transfers between devices  14.9 us (18%)
  local copies, waits for them, and re-layouts  11 us (13%)
  other arithmetic  1.19 us (1%)
    pallas_call x4, Pallas kernels, local_terms(): pl.pallas_call(functools.partial(local_kernel, head_count, seq), grid_spe...  23.7 us
    ppermute x12, waiting for transfers between devices, swapped(): return lax.ppermute(x, axis, [(i, i ^ bit) for i in range(size)])  12.4 us
    ppermute x6, waiting for transfers between devices, carry_on(): return lax.ppermute(x, 'seq', pairs)  11.8 us
    ppermute x6, starting transfers between devices, carry_on(): return lax.ppermute(x, 'seq', pairs)  10.1 us
    unnamed x76, local copies, waits for them, and re-layouts  7.97 us
    ppermute x12, starting transfers between devices, swapped(): return lax.ppermute(x, axis, [(i, i ^ bit) for i in range(size)])  4.77 us
    pallas_call x4, Pallas kernels, project(): pl.pallas_call(functools.partial(project_kernel, len(states), groups), in...  2.95 us
    pallas_call x5, Pallas kernels, step(): pl.pallas_call(functools.partial(step_kernel, len(maps)), in_specs=[pl.Bl...  1.81 us
  transfers between devices with their start and end apart: 18, of which 8 were waited for; matrix products, arithmetic and copies ran while one was open for 0% of the time, Pallas kernels for 27%

profile of v3, /device:TPU:22, one launch (start us, length us, event | category | flops | bytes accessed | tf_op | source)
XLA Modules:
  0.0 80.5 jit_solution(1057206576605056841)
XLA Ops:
  0.0 1.5 %reshape.14.k_ref = bf16[4,256,512]{2,1,0:T(8,128)(2,1)S(1)} reshape(bf16[4,128,2,512]{3,2,1,0:T(2,128)(2,1)} %param.8) | data formatting | bytes 2097152 | tf_op jit(solution)/shard_map/reshape | solution.py:385
  1.6 1.5 %reshape.15.v_ref = bf16[4,256,512]{2,1,0:T(8,128)(2,1)S(1)} reshape(bf16[4,128,2,512]{3,2,1,0:T(2,128)(2,1)} %param.9) | data formatting | bytes 2097152 | tf_op jit(solution)/shard_map/reshape | solution.py:386
  3.1 5.9 %local_terms.4 = (f32[4,128,128]{2,1,0:T(8,128)S(1)}, f32[4,128,128]{2,1,0:T(8,128)S(1)}, f32[4,128,128]{2,1,0:T(8,128)S(1)}, f32[4,128,128]{2,1,0:T(8,128)S(1)}) custom-call(s32[1]{0:T(128)S(6)} %mul.3.offset_ref, s32[4,3]{1,0:T(4,128)S(1)} %copy-done.37, bf16[4,128,512]{2,1,0:T(8,128)(2,1)S(1)} %copy-done.3, bf16[4,256,512]{2,1,0:T(8,128)(2,1)S(1)} %reshape.14.k_ref, ...), custom_call_target="tpu_custom_call" | custom-call | tf_op jit(solution)/shard_map/local_terms/pallas_call | solution.py:219
  9.0 0.7 copy-done.32
  9.7 0.7 copy-done.34
  10.4 0.7 collective-permute-start
  11.1 5.9 %local_terms.5 = (f32[4,128,128]{2,1,0:T(8,128)S(1)}, f32[4,128,128]{2,1,0:T(8,128)S(1)}, f32[4,128,128]{2,1,0:T(8,128)S(1)}, f32[4,128,128]{2,1,0:T(8,128)S(1)}) custom-call(s32[1]{0:T(128)S(6)} %mul.3.offset_ref, s32[4,3]{1,0:T(4,128)S(1)} %copy-done.37, bf16[4,128,512]{2,1,0:T(8,128)(2,1)S(1)} %copy-done.3, bf16[4,256,512]{2,1,0:T(8,128)(2,1)S(1)} %reshape.14.k_ref, ...), custom_call_target="tpu_custom_call" | custom-call | tf_op jit(solution)/shard_map/local_terms/pallas_call | solution.py:219
  17.1 0.6 copy-done.28
  17.7 0.1 copy-done.30
  17.9 1.6 %collective-permute-start.1 = (f32[4,128,128]{2,1,0:T(8,128)S(1)}, f32[4,128,128]{2,1,0:T(8,128)S(1)}, u32[]{:S(2)}, u32[]{:S(2)}) collective-permute-start(f32[4,128,128]{2,1,0:T(8,128)S(1)} %state_step.5.refs_0_), channel_id=1, source_target_pairs={{0,4},{4,8},{1,5},{5,9},{2,6},{6,10},{3,7},{7,11},{16,20},{20,24},... | collective-permute-start | bytes 786440 | tf_op jit(solution)/shard_map/ppermute | solution.py:345
  19.5 5.9 %local_terms.6 = (f32[4,128,128]{2,1,0:T(8,128)S(1)}, f32[4,128,128]{2,1,0:T(8,128)S(1)}, f32[4,128,128]{2,1,0:T(8,128)S(1)}, f32[4,128,128]{2,1,0:T(8,128)S(1)}) custom-call(s32[1]{0:T(128)S(6)} %mul.3.offset_ref, s32[4,3]{1,0:T(4,128)S(1)} %copy-done.37, bf16[4,128,512]{2,1,0:T(8,128)(2,1)S(1)} %copy-done.3, bf16[4,256,512]{2,1,0:T(8,128)(2,1)S(1)} %reshape.14.k_ref, ...), custom_call_target="tpu_custom_call" | custom-call | tf_op jit(solution)/shard_map/local_terms/pallas_call | solution.py:219
  25.4 0.7 copy-done.26
  26.2 2.8 %collective-permute-done.1.refs_6_.refs_1_.refs_0_ = f32[4,128,128]{2,1,0:T(8,128)S(1)} collective-permute-done((f32[4,128,128]{2,1,0:T(8,128)S(1)}, f32[4,128,128]{2,1,0:T(8,128)S(1)}, u32[]{:S(2)}, u32[]{:S(2)}) %collective-permute-start.1) | collective-permute-done | bytes 262176 | tf_op jit(solution)/shard_map/ppermute | solution.py:345
  29.0 0.3 state_step.6.refs_0_
  29.2 0.4 copy-done.14
  29.7 2.0 %collective-permute-start.2 = (f32[4,128,128]{2,1,0:T(8,128)S(1)}, f32[4,128,128]{2,1,0:T(8,128)S(1)}, u32[]{:S(2)}, u32[]{:S(2)}) collective-permute-start(f32[4,128,128]{2,1,0:T(8,128)S(1)} %state_step.6.refs_0_), channel_id=1, source_target_pairs={{0,4},{4,8},{8,12},{1,5},{5,9},{9,13},{2,6},{6,10},{10,14},{3,7},{... | collective-permute-start | bytes 786440 | tf_op jit(solution)/shard_map/ppermute | solution.py:345
  31.7 5.9 %local_terms.7 = (f32[4,128,128]{2,1,0:T(8,128)S(1)}, f32[4,128,128]{2,1,0:T(8,128)S(1)}, f32[4,128,128]{2,1,0:T(8,128)S(1)}, f32[4,128,128]{2,1,0:T(8,128)S(1)}) custom-call(s32[1]{0:T(128)S(6)} %mul.3.offset_ref, s32[4,3]{1,0:T(4,128)S(1)} %copy-done.37, bf16[4,128,512]{2,1,0:T(8,128)(2,1)S(1)} %copy-done.4, bf16[4,256,512]{2,1,0:T(8,128)(2,1)S(1)} %reshape.14.k_ref, ...), custom_call_target="tpu_custom_call" | custom-call | tf_op jit(solution)/shard_map/local_terms/pallas_call | solution.py:219
  37.7 0.9 %collective-permute-done.2.refs_6_.refs_2_.refs_1_.refs_0_ = f32[4,128,128]{2,1,0:T(8,128)S(1)} collective-permute-done((f32[4,128,128]{2,1,0:T(8,128)S(1)}, f32[4,128,128]{2,1,0:T(8,128)S(1)}, u32[]{:S(2)}, u32[]{:S(2)}) %collective-permute-start.2) | collective-permute-done | bytes 262176 | tf_op jit(solution)/shard_map/ppermute | solution.py:345
  38.6 1.0 %state_step.7.refs_4_ = f32[4,128,128]{2,1,0:T(8,128)} custom-call(s32[1]{0:T(128)} %bitcast.here_ref, f32[4,128,128]{2,1,0:T(8,128)S(1)} %get-tuple-element.49.refs_0_, f32[4,128,128]{2,1,0:T(8,128)S(1)} %get-tuple-element.47.refs_0_.refs_1_, f32[4,128,128]{2,1,0:T(8,128)S(1)} %get-tuple-element.44.refs_0_.refs_1_.refs_2_, ...), custom_call_target="tpu_custom_call" | custom-call | flops 1048576 | bytes 1024 | tf_op jit(solution)/shard_map/state_step/pallas_call | solution.py:269
  39.6 0.7 copy-done.5
  40.3 1.9 %collective-permute-start.5 = (f32[4,128,128]{2,1,0:T(8,128)}, f32[4,128,128]{2,1,0:T(8,128)S(1)}, u32[]{:S(2)}, u32[]{:S(2)}) collective-permute-start(f32[4,128,128]{2,1,0:T(8,128)} %state_step.7.refs_4_), channel_id=1, source_target_pairs={{0,4},{4,8},{8,12},{1,5},{5,9},{9,13},{2,6},{6,10},{10,14},{3,7},{... | collective-permute-start | bytes 786440 | tf_op jit(solution)/shard_map/ppermute | solution.py:345
  42.3 1.0 %copy-done.8 = f32[4,128,128]{2,1,0:T(8,128)S(1)} copy-done((f32[4,128,128]{2,1,0:T(8,128)S(1)}, f32[4,128,128]{2,1,0:T(8,128)}, u32[]{:S(2)}) %copy-start.8) | copy-done | bytes 262168
  43.3 0.9 %copy-done.18 = f32[4,128,128]{2,1,0:T(8,128)S(1)} copy-done((f32[4,128,128]{2,1,0:T(8,128)S(1)}, f32[4,128,128]{2,1,0:T(8,128)}, u32[]{:S(2)}) %copy-start.18) | copy-done | bytes 262168
  44.2 0.9 %copy-done.33 = f32[4,128,128]{2,1,0:T(8,128)S(1)} copy-done((f32[4,128,128]{2,1,0:T(8,128)S(1)}, f32[4,128,128]{2,1,0:T(8,128)}, u32[]{:S(2)}) %copy-start.33) | copy-done | bytes 262168
  45.2 0.9 %copy-done.35 = f32[4,128,128]{2,1,0:T(8,128)S(1)} copy-done((f32[4,128,128]{2,1,0:T(8,128)S(1)}, f32[4,128,128]{2,1,0:T(8,128)}, u32[]{:S(2)}) %copy-start.35) | copy-done | bytes 262168
  46.1 0.7 project.4
  47.0 0.5 collective-permute-start.4
  47.5 1.3 %collective-permute-done.5.refs_4_.refs_2_.refs_1_.refs_0_ = f32[4,128,128]{2,1,0:T(8,128)S(1)} collective-permute-done((f32[4,128,128]{2,1,0:T(8,128)}, f32[4,128,128]{2,1,0:T(8,128)S(1)}, u32[]{:S(2)}, u32[]{:S(2)}) %collective-permute-start.5) | collective-permute-done | bytes 262176 | tf_op jit(solution)/shard_map/ppermute | solution.py:345
  48.8 0.3 state_step.8.refs_2_
  49.1 1.9 %collective-permute-start.9 = (f32[4,128,128]{2,1,0:T(8,128)S(1)}, f32[4,128,128]{2,1,0:T(8,128)S(1)}, u32[]{:S(2)}, u32[]{:S(2)}) collective-permute-start(f32[4,128,128]{2,1,0:T(8,128)S(1)} %state_step.8.refs_2_), channel_id=1, source_target_pairs={{4,8},{8,12},{5,9},{9,13},{6,10},{10,14},{7,11},{11,15},{20,24},{2... | collective-permute-start | bytes 786440 | tf_op jit(solution)/shard_map/ppermute | solution.py:345
  51.1 0.7 project.5
  52.0 0.5 collective-permute-start.8
  52.5 0.5 collective-permute-start.6
  53.0 5.0 %collective-permute-done.9.refs_2_.refs_1_ = f32[4,128,128]{2,1,0:T(8,128)S(1)} collective-permute-done((f32[4,128,128]{2,1,0:T(8,128)S(1)}, f32[4,128,128]{2,1,0:T(8,128)S(1)}, u32[]{:S(2)}, u32[]{:S(2)}) %collective-permute-start.9) | collective-permute-done | bytes 262176 | tf_op jit(solution)/shard_map/ppermute | solution.py:345
  58.0 0.3 state_step.9.refs_2_
  58.2 2.0 %collective-permute-start.13 = (f32[4,128,128]{2,1,0:T(8,128)S(1)}, f32[4,128,128]{2,1,0:T(8,128)S(1)}, u32[]{:S(2)}, u32[]{:S(2)}) collective-permute-start(f32[4,128,128]{2,1,0:T(8,128)S(1)} %state_step.9.refs_2_), channel_id=1, source_target_pairs={{8,12},{9,13},{10,14},{11,15},{24,28},{25,29},{26,30},{27,31}} | collective-permute-start | bytes 786440 | tf_op jit(solution)/shard_map/ppermute | solution.py:345
  60.3 0.6 collective-permute-start.10
  60.9 0.8 project.6
  61.7 0.5 collective-permute-start.12
  62.2 1.8 %collective-permute-done.13.refs_2_ = f32[4,128,128]{2,1,0:T(8,128)S(1)} collective-permute-done((f32[4,128,128]{2,1,0:T(8,128)S(1)}, f32[4,128,128]{2,1,0:T(8,128)S(1)}, u32[]{:S(2)}, u32[]{:S(2)}) %collective-permute-start.13) | collective-permute-done | bytes 262176 | tf_op jit(solution)/shard_map/ppermute | solution.py:345
  64.1 0.7 project.7
  64.9 0.5 collective-permute-start.16
  65.4 0.6 collective-permute-start.14
  66.0 0.7 collective-permute-done.10
  66.8 0.8 %collective-permute-start.17 = (f32[1,128,512]{2,1,0:T(8,128)S(1)}, f32[1,128,512]{2,1,0:T(8,128)S(1)}, u32[]{:S(2)}, u32[]{:S(2)}) collective-permute-start(f32[1,128,512]{2,1,0:T(8,128)S(1)} %get-tuple-element.76), channel_id=1, source_target_pairs={{0,2},{1,3},{2,0},{3,1},{4,6},{5,7},{6,4},{7,5},{8,10},{9,11},{10,... | collective-permute-start | bytes 786440 | tf_op jit(solution)/shard_map/ppermute | solution.py:340
  67.8 6.9 %collective-permute-done.14 = f32[1,128,512]{2,1,0:T(8,128)S(1)} collective-permute-done((f32[1,128,512]{2,1,0:T(8,128)S(1)}, f32[1,128,512]{2,1,0:T(8,128)S(1)}, u32[]{:S(2)}, u32[]{:S(2)}) %collective-permute-start.14) | collective-permute-done | bytes 262176 | tf_op jit(solution)/shard_map/ppermute | solution.py:340
  74.7 4.7 %collective-permute-done.17 = f32[1,128,512]{2,1,0:T(8,128)S(1)} collective-permute-done((f32[1,128,512]{2,1,0:T(8,128)S(1)}, f32[1,128,512]{2,1,0:T(8,128)S(1)}, u32[]{:S(2)}, u32[]{:S(2)}) %collective-permute-start.17) | collective-permute-done | bytes 262176 | tf_op jit(solution)/shard_map/ppermute | solution.py:340
  79.4 1.0 %pad_maximum_fusion = f32[4,128,512]{2,1,0:T(8,128)} fusion(f32[1,128,512]{2,1,0:T(8,128)S(1)} %add.21, f32[1,128,512]{2,1,0:T(8,128)S(1)} %add.20, f32[1,128,512]{2,1,0:T(8,128)S(1)} %add.19, f32[1,128,512]{2,1,0:T(8,128)S(1)} %add.18), kind=kLoop, calls=%fused_computation | loop fusion | flops 786432 | bytes 2097152 | tf_op jit(solution)/shard_map/stack | solution.py:464
  (88 shorter events, 1.0 us)
Async XLA Ops:
  0.0 3.0 %copy-start.3 = (bf16[4,128,512]{2,1,0:T(8,128)(2,1)S(1)}, bf16[4,128,512]{2,1,0:T(8,128)(2,1)}, u32[]{:S(2)}) copy-start(bf16[4,128,512]{2,1,0:T(8,128)(2,1)} %q_ref.7) | copy-start | bytes 1572868
  0.0 3.1 %copy-start.19 = (f32[4,2,4,128]{3,2,1,0:T(4,128)S(1)}, f32[4,2,4,128]{3,2,1,0:T(4,128)}, u32[]{:S(2)}) copy-start(f32[4,2,4,128]{3,2,1,0:T(4,128)} %beta_ref.7) | copy-start | bytes 49156
  0.0 3.1 %copy-start.36 = (f32[4,4,128]{2,1,0:T(4,128)S(1)}, f32[4,4,128]{2,1,0:T(4,128)}, u32[]{:S(2)}) copy-start(f32[4,4,128]{2,1,0:T(4,128)} %gate_ref.7) | copy-start | bytes 24580
  0.0 3.1 %copy-start.37 = (s32[4,3]{1,0:T(4,128)S(1)}, s32[4,3]{1,0:T(4,128)}, u32[]{:S(2)}) copy-start(s32[4,3]{1,0:T(4,128)} %resets_ref.7) | copy-start | bytes 148
  3.0 16.5 %copy-start.1 = (bf16[4,256,512]{2,1,0:T(8,128)(2,1)}, bf16[4,256,512]{2,1,0:T(8,128)(2,1)S(1)}, u32[]{:S(2)}) copy-start(bf16[4,256,512]{2,1,0:T(8,128)(2,1)S(1)} %reshape.15.v_ref) | copy-start | bytes 3145732
  10.4 6.6 %collective-permute-start = (f32[4,128,128]{2,1,0:T(8,128)S(1)}, f32[4,128,128]{2,1,0:T(8,128)S(1)}, u32[]{:S(2)}, u32[]{:S(2)}) collective-permute-start(f32[4,128,128]{2,1,0:T(8,128)S(1)} %get-tuple-element.43.refs_0_.refs_3_.refs_5_), channel_id=1, source_target_pairs={{0,4},{1,5},{2,6},{3,7},{16,20},{17,21},{18,22},{19,23}} | collective-permute-start | bytes 786440 | tf_op jit(solution)/shard_map/ppermute | solution.py:345
  17.9 13.8 %copy-start.4 = (bf16[4,128,512]{2,1,0:T(8,128)(2,1)S(1)}, bf16[4,128,512]{2,1,0:T(8,128)(2,1)}, u32[]{:S(2)}) copy-start(bf16[4,128,512]{2,1,0:T(8,128)(2,1)} %q_ref.7) | copy-start | bytes 1572868
  17.9 11.1 %collective-permute-start.1 = (f32[4,128,128]{2,1,0:T(8,128)S(1)}, f32[4,128,128]{2,1,0:T(8,128)S(1)}, u32[]{:S(2)}, u32[]{:S(2)}) collective-permute-start(f32[4,128,128]{2,1,0:T(8,128)S(1)} %state_step.5.refs_0_), channel_id=1, source_target_pairs={{0,4},{4,8},{1,5},{5,9},{2,6},{6,10},{3,7},{7,11},{16,20},{20,24},... | collective-permute-start | bytes 786440 | tf_op jit(solution)/shard_map/ppermute | solution.py:345
  26.1 3.1 %copy-start.24 = (f32[4,128,128]{2,1,0:T(8,128)}, f32[4,128,128]{2,1,0:T(8,128)S(1)}, u32[]{:S(2)}) copy-start(f32[4,128,128]{2,1,0:T(8,128)S(1)} %get-tuple-element.63.reach_ref) | copy-start | bytes 786436
  26.1 12.5 %copy-start.10 = (f32[4,128,128]{2,1,0:T(8,128)}, f32[4,128,128]{2,1,0:T(8,128)S(1)}, u32[]{:S(2)}) copy-start(f32[4,128,128]{2,1,0:T(8,128)S(1)} %get-tuple-element.47.refs_0_.refs_1_) | copy-start | bytes 786436
  26.2 5.6 %copy-start.2 = (bf16[4,256,512]{2,1,0:T(8,128)(2,1)S(1)}, bf16[4,256,512]{2,1,0:T(8,128)(2,1)}, u32[]{:S(2)}) copy-start(bf16[4,256,512]{2,1,0:T(8,128)(2,1)} %copy-done.1) | copy-start | bytes 3145732
  29.7 12.6 %copy-start = (bf16[512,2048]{1,0:T(8,128)(2,1)S(1)}, bf16[512,2048]{1,0:T(8,128)(2,1)}, u32[]{:S(2)}) copy-start(bf16[512,2048]{1,0:T(8,128)(2,1)} %refs_3_.7) | copy-start | bytes 6291460
  29.7 8.9 %collective-permute-start.2 = (f32[4,128,128]{2,1,0:T(8,128)S(1)}, f32[4,128,128]{2,1,0:T(8,128)S(1)}, u32[]{:S(2)}, u32[]{:S(2)}) collective-permute-start(f32[4,128,128]{2,1,0:T(8,128)S(1)} %state_step.6.refs_0_), channel_id=1, source_target_pairs={{0,4},{4,8},{8,12},{1,5},{5,9},{9,13},{2,6},{6,10},{10,14},{3,7},{... | collective-permute-start | bytes 786440 | tf_op jit(solution)/shard_map/ppermute | solution.py:345
  37.7 1.9 %copy-start.12 = (f32[4,128,128]{2,1,0:T(8,128)}, f32[4,128,128]{2,1,0:T(8,128)S(1)}, u32[]{:S(2)}) copy-start(f32[4,128,128]{2,1,0:T(8,128)S(1)} %get-tuple-element.49.refs_0_) | copy-start | bytes 786436
  37.7 1.9 %copy-start.20 = (f32[4,128,128]{2,1,0:T(8,128)}, f32[4,128,128]{2,1,0:T(8,128)S(1)}, u32[]{:S(2)}) copy-start(f32[4,128,128]{2,1,0:T(8,128)S(1)} %get-tuple-element.68.reach_ref) | copy-start | bytes 786436
  37.7 1.9 %copy-start.22 = (f32[4,128,128]{2,1,0:T(8,128)}, f32[4,128,128]{2,1,0:T(8,128)S(1)}, u32[]{:S(2)}) copy-start(f32[4,128,128]{2,1,0:T(8,128)S(1)} %get-tuple-element.69.own_ref) | copy-start | bytes 786436
  37.7 4.5 %copy-start.15 = (f32[4,128,128]{2,1,0:T(8,128)S(1)}, f32[4,128,128]{2,1,0:T(8,128)}, u32[]{:S(2)}) copy-start(f32[4,128,128]{2,1,0:T(8,128)} %copy-done.14) | copy-start | bytes 786436
  38.6 1.0 %copy-start.7 = (f32[4,128,128]{2,1,0:T(8,128)}, f32[4,128,128]{2,1,0:T(8,128)S(1)}, u32[]{:S(2)}) copy-start(f32[4,128,128]{2,1,0:T(8,128)S(1)} %collective-permute-done.2.refs_6_.refs_2_.refs_1_.refs_0_) | copy-start | bytes 786436
  40.3 8.5 %collective-permute-start.5 = (f32[4,128,128]{2,1,0:T(8,128)}, f32[4,128,128]{2,1,0:T(8,128)S(1)}, u32[]{:S(2)}, u32[]{:S(2)}) collective-permute-start(f32[4,128,128]{2,1,0:T(8,128)} %state_step.7.refs_4_), channel_id=1, source_target_pairs={{0,4},{4,8},{8,12},{1,5},{5,9},{9,13},{2,6},{6,10},{10,14},{3,7},{... | collective-permute-start | bytes 786440 | tf_op jit(solution)/shard_map/ppermute | solution.py:345
  42.2 6.6 %copy-start.6 = (f32[4,128,128]{2,1,0:T(8,128)S(1)}, f32[4,128,128]{2,1,0:T(8,128)}, u32[]{:S(2)}) copy-start(f32[4,128,128]{2,1,0:T(8,128)} %copy-done.5) | copy-start | bytes 786436
  42.3 1.0 %copy-start.8 = (f32[4,128,128]{2,1,0:T(8,128)S(1)}, f32[4,128,128]{2,1,0:T(8,128)}, u32[]{:S(2)}) copy-start(f32[4,128,128]{2,1,0:T(8,128)} %copy-done.7) | copy-start | bytes 786436
  43.3 0.9 %copy-start.18 = (f32[4,128,128]{2,1,0:T(8,128)S(1)}, f32[4,128,128]{2,1,0:T(8,128)}, u32[]{:S(2)}) copy-start(f32[4,128,128]{2,1,0:T(8,128)} %copy-done.17) | copy-start | bytes 786436
  44.2 0.9 %copy-start.33 = (f32[4,128,128]{2,1,0:T(8,128)S(1)}, f32[4,128,128]{2,1,0:T(8,128)}, u32[]{:S(2)}) copy-start(f32[4,128,128]{2,1,0:T(8,128)} %copy-done.32) | copy-start | bytes 786436
  45.2 0.9 %copy-start.35 = (f32[4,128,128]{2,1,0:T(8,128)S(1)}, f32[4,128,128]{2,1,0:T(8,128)}, u32[]{:S(2)}) copy-start(f32[4,128,128]{2,1,0:T(8,128)} %copy-done.34) | copy-start | bytes 786436
  46.1 2.7 %copy-start.11 = (f32[4,128,128]{2,1,0:T(8,128)S(1)}, f32[4,128,128]{2,1,0:T(8,128)}, u32[]{:S(2)}) copy-start(f32[4,128,128]{2,1,0:T(8,128)} %copy-done.10) | copy-start | bytes 786436
  46.1 2.7 %copy-start.13 = (f32[4,128,128]{2,1,0:T(8,128)S(1)}, f32[4,128,128]{2,1,0:T(8,128)}, u32[]{:S(2)}) copy-start(f32[4,128,128]{2,1,0:T(8,128)} %copy-done.12) | copy-start | bytes 786436
  46.8 4.2 %copy-start.9 = (f32[4,128,128]{2,1,0:T(8,128)S(1)}, f32[4,128,128]{2,1,0:T(8,128)}, u32[]{:S(2)}) copy-start(f32[4,128,128]{2,1,0:T(8,128)} %copy-done.7) | copy-start | bytes 786436
  46.9 4.2 %copy-start.16 = (f32[4,128,128]{2,1,0:T(8,128)S(1)}, f32[4,128,128]{2,1,0:T(8,128)}, u32[]{:S(2)}) copy-start(f32[4,128,128]{2,1,0:T(8,128)} %copy-done.14) | copy-start | bytes 786436
  46.9 4.2 %copy-start.29 = (f32[4,128,128]{2,1,0:T(8,128)S(1)}, f32[4,128,128]{2,1,0:T(8,128)}, u32[]{:S(2)}) copy-start(f32[4,128,128]{2,1,0:T(8,128)} %copy-done.28) | copy-start | bytes 786436
  46.9 4.2 %copy-start.31 = (f32[4,128,128]{2,1,0:T(8,128)S(1)}, f32[4,128,128]{2,1,0:T(8,128)}, u32[]{:S(2)}) copy-start(f32[4,128,128]{2,1,0:T(8,128)} %copy-done.30) | copy-start | bytes 786436
  46.9 4.1 %collective-permute-start.3 = (f32[128,512]{1,0:T(8,128)S(1)}, f32[128,512]{1,0:T(8,128)S(1)}, u32[]{:S(2)}, u32[]{:S(2)}) collective-permute-start(f32[128,512]{1,0:T(8,128)S(1)} %get-tuple-element.52), channel_id=1, source_target_pairs={{0,1},{1,0},{2,3},{3,2},{4,5},{5,4},{6,7},{7,6},{8,9},{9,8},{10,11... | collective-permute-start | bytes 786440 | tf_op jit(solution)/shard_map/ppermute | solution.py:340
  47.0 4.1 %collective-permute-start.4 = (f32[128,512]{1,0:T(8,128)S(1)}, f32[128,512]{1,0:T(8,128)S(1)}, u32[]{:S(2)}, u32[]{:S(2)}) collective-permute-start(f32[128,512]{1,0:T(8,128)S(1)} %get-tuple-element.53), channel_id=1, source_target_pairs={{0,1},{1,0},{2,3},{3,2},{4,5},{5,4},{6,7},{7,6},{8,9},{9,8},{10,11... | collective-permute-start | bytes 786440 | tf_op jit(solution)/shard_map/ppermute | solution.py:340
  49.1 8.9 %collective-permute-start.9 = (f32[4,128,128]{2,1,0:T(8,128)S(1)}, f32[4,128,128]{2,1,0:T(8,128)S(1)}, u32[]{:S(2)}, u32[]{:S(2)}) collective-permute-start(f32[4,128,128]{2,1,0:T(8,128)S(1)} %state_step.8.refs_2_), channel_id=1, source_target_pairs={{4,8},{8,12},{5,9},{9,13},{6,10},{10,14},{7,11},{11,15},{20,24},{2... | collective-permute-start | bytes 786440 | tf_op jit(solution)/shard_map/ppermute | solution.py:345
  51.9 9.0 %copy-start.25 = (f32[4,128,128]{2,1,0:T(8,128)S(1)}, f32[4,128,128]{2,1,0:T(8,128)}, u32[]{:S(2)}) copy-start(f32[4,128,128]{2,1,0:T(8,128)} %copy-done.24) | copy-start | bytes 786436
  51.9 9.0 %copy-start.27 = (f32[4,128,128]{2,1,0:T(8,128)S(1)}, f32[4,128,128]{2,1,0:T(8,128)}, u32[]{:S(2)}) copy-start(f32[4,128,128]{2,1,0:T(8,128)} %copy-done.26) | copy-start | bytes 786436
  51.9 8.3 %collective-permute-start.7 = (f32[128,512]{1,0:T(8,128)S(1)}, f32[128,512]{1,0:T(8,128)S(1)}, u32[]{:S(2)}, u32[]{:S(2)}) collective-permute-start(f32[128,512]{1,0:T(8,128)S(1)} %get-tuple-element.59), channel_id=1, source_target_pairs={{0,1},{1,0},{2,3},{3,2},{4,5},{5,4},{6,7},{7,6},{8,9},{9,8},{10,11... | collective-permute-start | bytes 786440 | tf_op jit(solution)/shard_map/ppermute | solution.py:340
  52.0 8.2 %collective-permute-start.8 = (f32[128,512]{1,0:T(8,128)S(1)}, f32[128,512]{1,0:T(8,128)S(1)}, u32[]{:S(2)}, u32[]{:S(2)}) collective-permute-start(f32[128,512]{1,0:T(8,128)S(1)} %get-tuple-element.60), channel_id=1, source_target_pairs={{0,1},{1,0},{2,3},{3,2},{4,5},{5,4},{6,7},{7,6},{8,9},{9,8},{10,11... | collective-permute-start | bytes 786440 | tf_op jit(solution)/shard_map/ppermute | solution.py:340
  52.5 8.4 %collective-permute-start.6 = (f32[1,128,512]{2,1,0:T(8,128)S(1)}, f32[1,128,512]{2,1,0:T(8,128)S(1)}, u32[]{:S(2)}, u32[]{:S(2)}) collective-permute-start(f32[1,128,512]{2,1,0:T(8,128)S(1)} %get-tuple-element.55.refs_4_), channel_id=1, source_target_pairs={{0,2},{1,3},{2,0},{3,1},{4,6},{5,7},{6,4},{7,5},{8,10},{9,11},{10,... | collective-permute-start | bytes 786440 | tf_op jit(solution)/shard_map/ppermute | solution.py:340
  58.2 5.8 %collective-permute-start.13 = (f32[4,128,128]{2,1,0:T(8,128)S(1)}, f32[4,128,128]{2,1,0:T(8,128)S(1)}, u32[]{:S(2)}, u32[]{:S(2)}) collective-permute-start(f32[4,128,128]{2,1,0:T(8,128)S(1)} %state_step.9.refs_2_), channel_id=1, source_target_pairs={{8,12},{9,13},{10,14},{11,15},{24,28},{25,29},{26,30},{27,31}} | collective-permute-start | bytes 786440 | tf_op jit(solution)/shard_map/ppermute | solution.py:345
  60.3 3.8 %copy-start.21 = (f32[4,128,128]{2,1,0:T(8,128)S(1)}, f32[4,128,128]{2,1,0:T(8,128)}, u32[]{:S(2)}) copy-start(f32[4,128,128]{2,1,0:T(8,128)} %copy-done.20) | copy-start | bytes 786436
  60.3 3.7 %copy-start.23 = (f32[4,128,128]{2,1,0:T(8,128)S(1)}, f32[4,128,128]{2,1,0:T(8,128)}, u32[]{:S(2)}) copy-start(f32[4,128,128]{2,1,0:T(8,128)} %copy-done.22) | copy-start | bytes 786436
  60.3 6.4 %collective-permute-start.10 = (f32[1,128,512]{2,1,0:T(8,128)S(1)}, f32[1,128,512]{2,1,0:T(8,128)S(1)}, u32[]{:S(2)}, u32[]{:S(2)}) collective-permute-start(f32[1,128,512]{2,1,0:T(8,128)S(1)} %get-tuple-element.62.refs_4_), channel_id=1, source_target_pairs={{0,2},{1,3},{2,0},{3,1},{4,6},{5,7},{6,4},{7,5},{8,10},{9,11},{10,... | collective-permute-start | bytes 786440 | tf_op jit(solution)/shard_map/ppermute | solution.py:340
  61.7 3.7 %collective-permute-start.11 = (f32[128,512]{1,0:T(8,128)S(1)}, f32[128,512]{1,0:T(8,128)S(1)}, u32[]{:S(2)}, u32[]{:S(2)}) collective-permute-start(f32[128,512]{1,0:T(8,128)S(1)} %get-tuple-element.66), channel_id=1, source_target_pairs={{0,1},{1,0},{2,3},{3,2},{4,5},{5,4},{6,7},{7,6},{8,9},{9,8},{10,11... | collective-permute-start | bytes 786440 | tf_op jit(solution)/shard_map/ppermute | solution.py:340
  61.7 3.6 %collective-permute-start.12 = (f32[128,512]{1,0:T(8,128)S(1)}, f32[128,512]{1,0:T(8,128)S(1)}, u32[]{:S(2)}, u32[]{:S(2)}) collective-permute-start(f32[128,512]{1,0:T(8,128)S(1)} %get-tuple-element.67), channel_id=1, source_target_pairs={{0,1},{1,0},{2,3},{3,2},{4,5},{5,4},{6,7},{7,6},{8,9},{9,8},{10,11... | collective-permute-start | bytes 786440 | tf_op jit(solution)/shard_map/ppermute | solution.py:340
  64.8 2.0 %collective-permute-start.15 = (f32[128,512]{1,0:T(8,128)S(1)}, f32[128,512]{1,0:T(8,128)S(1)}, u32[]{:S(2)}, u32[]{:S(2)}) collective-permute-start(f32[128,512]{1,0:T(8,128)S(1)} %get-tuple-element.73), channel_id=1, source_target_pairs={{0,1},{1,0},{2,3},{3,2},{4,5},{5,4},{6,7},{7,6},{8,9},{9,8},{10,11... | collective-permute-start | bytes 786440 | tf_op jit(solution)/shard_map/ppermute | solution.py:340
  64.9 1.9 %collective-permute-start.16 = (f32[128,512]{1,0:T(8,128)S(1)}, f32[128,512]{1,0:T(8,128)S(1)}, u32[]{:S(2)}, u32[]{:S(2)}) collective-permute-start(f32[128,512]{1,0:T(8,128)S(1)} %get-tuple-element.74), channel_id=1, source_target_pairs={{0,1},{1,0},{2,3},{3,2},{4,5},{5,4},{6,7},{7,6},{8,9},{9,8},{10,11... | collective-permute-start | bytes 786440 | tf_op jit(solution)/shard_map/ppermute | solution.py:340
  65.4 9.2 %collective-permute-start.14 = (f32[1,128,512]{2,1,0:T(8,128)S(1)}, f32[1,128,512]{2,1,0:T(8,128)S(1)}, u32[]{:S(2)}, u32[]{:S(2)}) collective-permute-start(f32[1,128,512]{2,1,0:T(8,128)S(1)} %get-tuple-element.72.refs_2_), channel_id=1, source_target_pairs={{0,2},{1,3},{2,0},{3,1},{4,6},{5,7},{6,4},{7,5},{8,10},{9,11},{10,... | collective-permute-start | bytes 786440 | tf_op jit(solution)/shard_map/ppermute | solution.py:340
  66.8 12.6 %collective-permute-start.17 = (f32[1,128,512]{2,1,0:T(8,128)S(1)}, f32[1,128,512]{2,1,0:T(8,128)S(1)}, u32[]{:S(2)}, u32[]{:S(2)}) collective-permute-start(f32[1,128,512]{2,1,0:T(8,128)S(1)} %get-tuple-element.76), channel_id=1, source_target_pairs={{0,2},{1,3},{2,0},{3,1},{4,6},{5,7},{6,4},{7,5},{8,10},{9,11},{10,... | collective-permute-start | bytes 786440 | tf_op jit(solution)/shard_map/ppermute | solution.py:340
  (8 other events, 5.9 us)

commit v4 on v3

--- a/solution.py
+++ b/solution.py
@@ -92,9 +92,11 @@
     h_i, h_j = iota((half, half), 0), iota((half, half), 1)
     eye_half = h_i == h_j
     apart = jnp.where(h_i > h_j, h_i ^ h_j, 0)
-    widths = [1 << n for n in range((half - 1).bit_length())]
+    spans = [(1, 2)]
+    while spans[-1][1] < half:
+        spans.append((spans[-1][1], min(4 * spans[-1][1], half)))
     masks = [
-        jnp.logical_and(apart >= w, apart < 2 * w).astype(f32).astype(bf16) for w in widths
+        jnp.logical_and(apart >= a, apart < b).astype(f32).astype(bf16) for a, b in spans
     ]
     eye16 = eye_half.astype(f32).astype(bf16)
     eye_size = (iota((size, size), 0) == iota((size, size), 1)).astype(f32)
@@ -106,8 +108,8 @@
     )
 
     q = [q_ref[0, :, h * size:(h + 1) * size] for h in heads]
-    k = [k_ref[0, :, h * size:(h + 1) * size] for h in heads]
-    v = [v_ref[0, :, h * size:(h + 1) * size] for h in heads]
+    k = [k_ref[0, :, :, h * size:(h + 1) * size].astype(f32).reshape(2 * tok, size).astype(bf16) for h in heads]
+    v = [v_ref[0, :, :, h * size:(h + 1) * size].astype(f32).reshape(2 * tok, size).astype(bf16) for h in heads]
 
     def unit(x):
         return lax.rsqrt(jnp.sum(x * x, axis=1, keepdims=True) + epsilon)
@@ -154,8 +156,13 @@
     part = {(h, b): top[h][0] if b == 0 else bottom[h][0][:, half:] for h, b in blocks}
     inv = {key: eye16 - part[key] * masks[0] for key in blocks}
     for mask in masks[1:]:
-        inner = {key: mm(part[key] * mask, inv[key]).astype(bf16) for key in blocks}
-        inv = {key: inv[key] - mm(inv[key], inner[key]).astype(bf16) for key in blocks}
+        cross = {key: mm(inv[key], part[key] * mask).astype(bf16) for key in blocks}
+        square = {key: mm(cross[key], cross[key]).astype(bf16) for key in blocks}
+        near = {key: inv[key] - mm(cross[key], inv[key]).astype(bf16) for key in blocks}
+        inv = {
+            key: (near[key].astype(f32) + mm(square[key], near[key])).astype(bf16)
+            for key in blocks
+        }
     lower = []
     for h in heads:
         inner = mm(bottom[h][0][:, :half], inv[h, 0]).astype(bf16)
@@ -223,8 +230,8 @@
             grid=(1,),
             in_specs=[
                 block((tok, packed)),
-                block((2 * tok, packed)),
-                block((2 * tok, packed)),
+                block((tok, 2, packed)),
+                block((tok, 2, packed)),
                 block((head_count, tok)),
                 block((2, head_count, tok)),
             ]
@@ -234,8 +241,8 @@
         out_shape=[
             jax.ShapeDtypeStruct((head_count, size, size), f32),
             jax.ShapeDtypeStruct((head_count, size, size), f32),
-            jax.ShapeDtypeStruct((head_count, tok, size), f32),
-            jax.ShapeDtypeStruct((head_count, tok, size), f32),
+            pltpu.HBM((head_count, tok, size), f32),
+            pltpu.HBM((head_count, tok, size), f32),
         ],
         compiler_params=pltpu.CompilerParams(vmem_limit_bytes=16 << 20),
         name="local_terms",
@@ -382,12 +389,10 @@
     here = lax.axis_index("seq").astype(jnp.int32).reshape(1)
     offset = here * tok
     place = lax.axis_index("head").astype(jnp.int32).reshape(1)
-    key_rows = keys.reshape(chunks, 2 * tok, packed)
-    value_rows = values.reshape(chunks, 2 * tok, packed)
 
     def local(s, earlier=()):
         return local_terms(
-            s, offset, resets, queries, key_rows, value_rows, log_gate, beta, earlier
+            s, offset, resets, queries, keys, values, log_gate, beta, earlier
         )
 
     if devices > 8:

time: 81.7 us -> 82.2 us (level)
  Pallas kernels: 28.7 us -> 30.3 us
    reshape x2 -> x0, local copies, waits for them, and re-layouts: 2.99 us -> none  [the longest x1 1.52 us: shards(): key_rows = keys.reshape(chunks, 2 * tok, packed)]
    unnamed x76 -> x42, local copies, waits for them, and re-layouts: 7.97 us -> 10.6 us
    pallas_call x4, Pallas kernels: 23.7 us -> 25.3 us  [local_terms(): pl.pallas_call(functools.partial(local_kernel, head_count, seq), grid_spe...]
  transfers between devices with their start and end apart: 18 -> 18, of which waited for: 8 -> 8; matrix products, arithmetic and copies ran while one was open for 0% -> 0% of each run, Pallas kernels for 27% -> 28%
where the time goes in v4:
time: 82.2 us; the launch traced here: 80.7 us
  Pallas kernels  30.3 us (37%)
  waiting for transfers between devices  23.5 us (29%)
  starting transfers between devices  14.8 us (18%)
  local copies, waits for them, and re-layouts  10.6 us (13%)
  other arithmetic  1.18 us (1%)
    pallas_call x4, Pallas kernels, local_terms(): pl.pallas_call(functools.partial(local_kernel, head_count, seq), grid_spe...  25.3 us
    ppermute x12, waiting for transfers between devices, swapped(): return lax.ppermute(x, axis, [(i, i ^ bit) for i in range(size)])  12.4 us
    ppermute x6, waiting for transfers between devices, carry_on(): return lax.ppermute(x, 'seq', pairs)  11.2 us
    unnamed x42, local copies, waits for them, and re-layouts  10.6 us
    ppermute x6, starting transfers between devices, carry_on(): return lax.ppermute(x, 'seq', pairs)  9.95 us
    ppermute x12, starting transfers between devices, swapped(): return lax.ppermute(x, axis, [(i, i ^ bit) for i in range(size)])  4.82 us
    pallas_call x4, Pallas kernels, project(): pl.pallas_call(functools.partial(project_kernel, len(states), groups), in...  2.95 us
    pallas_call x5, Pallas kernels, step(): pl.pallas_call(functools.partial(step_kernel, len(maps)), in_specs=[pl.Bl...  1.8 us
  transfers between devices with their start and end apart: 18, of which 8 were waited for; matrix products, arithmetic and copies ran while one was open for 0% of the time, Pallas kernels for 28%

profile of v4, /device:TPU:22, one launch (start us, length us, event | category | flops | bytes accessed | tf_op | source)
XLA Modules:
  0.0 80.7 jit_solution(5404727167498541416)
XLA Ops:
  0.0 1.2 %copy-done.1 = bf16[4,128,2,512]{3,2,1,0:T(2,128)(2,1)S(1)} copy-done((bf16[4,128,2,512]{3,2,1,0:T(2,128)(2,1)S(1)}, bf16[4,128,2,512]{3,2,1,0:T(2,128)(2,1)}, u32[]{:S(2)}) %copy-start.1) | copy-done | bytes 1048600
  1.2 1.2 %copy-done.2 = bf16[4,128,2,512]{3,2,1,0:T(2,128)(2,1)S(1)} copy-done((bf16[4,128,2,512]{3,2,1,0:T(2,128)(2,1)S(1)}, bf16[4,128,2,512]{3,2,1,0:T(2,128)(2,1)}, u32[]{:S(2)}) %copy-start.2) | copy-done | bytes 1048600
  2.5 1.0 %copy-done.3 = bf16[4,128,512]{2,1,0:T(8,128)(2,1)S(1)} copy-done((bf16[4,128,512]{2,1,0:T(8,128)(2,1)S(1)}, bf16[4,128,512]{2,1,0:T(8,128)(2,1)}, u32[]{:S(2)}) %copy-start.3) | copy-done | bytes 524312
  3.5 0.7 copy-done.10
  4.2 0.7 copy-done.19
  4.9 0.7 copy-done.20
  5.6 6.3 %local_terms.4 = (f32[4,128,128]{2,1,0:T(8,128)S(1)}, f32[4,128,128]{2,1,0:T(8,128)S(1)}, f32[4,128,128]{2,1,0:T(8,128)}, f32[4,128,128]{2,1,0:T(8,128)}) custom-call(s32[1]{0:T(128)S(6)} %mul.3.offset_ref, s32[4,3]{1,0:T(4,128)S(1)} %copy-done.20, bf16[4,128,512]{2,1,0:T(8,128)(2,1)S(1)} %copy-done.3, bf16[4,128,2,512]{3,2,1,0:T(2,128)(2,1)S(1)} %copy-done.1, ...), custom_call_target="tpu_custom_call" | custom-call | tf_op jit(solution)/shard_map/local_terms/pallas_call | solution.py:226
  11.9 0.7 collective-permute-start
  12.6 6.3 %local_terms.5 = (f32[4,128,128]{2,1,0:T(8,128)S(1)}, f32[4,128,128]{2,1,0:T(8,128)S(1)}, f32[4,128,128]{2,1,0:T(8,128)}, f32[4,128,128]{2,1,0:T(8,128)}) custom-call(s32[1]{0:T(128)S(6)} %mul.3.offset_ref, s32[4,3]{1,0:T(4,128)S(1)} %copy-done.20, bf16[4,128,512]{2,1,0:T(8,128)(2,1)S(1)} %copy-done.3, bf16[4,128,2,512]{3,2,1,0:T(2,128)(2,1)S(1)} %copy-done.1, ...), custom_call_target="tpu_custom_call" | custom-call | tf_op jit(solution)/shard_map/local_terms/pallas_call | solution.py:226
  18.9 0.7 copy-done.8
  19.6 1.5 %collective-permute-start.1 = (f32[4,128,128]{2,1,0:T(8,128)S(1)}, f32[4,128,128]{2,1,0:T(8,128)S(1)}, u32[]{:S(2)}, u32[]{:S(2)}) collective-permute-start(f32[4,128,128]{2,1,0:T(8,128)S(1)} %state_step.5.refs_0_), channel_id=1, source_target_pairs={{0,4},{4,8},{1,5},{5,9},{2,6},{6,10},{3,7},{7,11},{16,20},{20,24},... | collective-permute-start | bytes 786440 | tf_op jit(solution)/shard_map/ppermute | solution.py:352
  21.1 6.3 %local_terms.6 = (f32[4,128,128]{2,1,0:T(8,128)S(1)}, f32[4,128,128]{2,1,0:T(8,128)S(1)}, f32[4,128,128]{2,1,0:T(8,128)}, f32[4,128,128]{2,1,0:T(8,128)}) custom-call(s32[1]{0:T(128)S(6)} %mul.3.offset_ref, s32[4,3]{1,0:T(4,128)S(1)} %copy-done.20, bf16[4,128,512]{2,1,0:T(8,128)(2,1)S(1)} %copy-done.3, bf16[4,128,2,512]{3,2,1,0:T(2,128)(2,1)S(1)} %copy-done.1, ...), custom_call_target="tpu_custom_call" | custom-call | tf_op jit(solution)/shard_map/local_terms/pallas_call | solution.py:226
  27.4 2.9 %collective-permute-done.1.refs_6_.refs_1_.refs_0_ = f32[4,128,128]{2,1,0:T(8,128)S(1)} collective-permute-done((f32[4,128,128]{2,1,0:T(8,128)S(1)}, f32[4,128,128]{2,1,0:T(8,128)S(1)}, u32[]{:S(2)}, u32[]{:S(2)}) %collective-permute-start.1) | collective-permute-done | bytes 262176 | tf_op jit(solution)/shard_map/ppermute | solution.py:352
  30.3 0.3 state_step.6.refs_0_
  30.6 0.4 copy-done.6
  31.0 2.0 %collective-permute-start.2 = (f32[4,128,128]{2,1,0:T(8,128)S(1)}, f32[4,128,128]{2,1,0:T(8,128)S(1)}, u32[]{:S(2)}, u32[]{:S(2)}) collective-permute-start(f32[4,128,128]{2,1,0:T(8,128)S(1)} %state_step.6.refs_0_), channel_id=1, source_target_pairs={{0,4},{4,8},{8,12},{1,5},{5,9},{9,13},{2,6},{6,10},{10,14},{3,7},{... | collective-permute-start | bytes 786440 | tf_op jit(solution)/shard_map/ppermute | solution.py:352
  33.1 6.3 %local_terms.7 = (f32[4,128,128]{2,1,0:T(8,128)S(1)}, f32[4,128,128]{2,1,0:T(8,128)S(1)}, f32[4,128,128]{2,1,0:T(8,128)}, f32[4,128,128]{2,1,0:T(8,128)}) custom-call(s32[1]{0:T(128)S(6)} %mul.3.offset_ref, s32[4,3]{1,0:T(4,128)S(1)} %copy-done.20, bf16[4,128,512]{2,1,0:T(8,128)(2,1)S(1)} %copy-done.3, bf16[4,128,2,512]{3,2,1,0:T(2,128)(2,1)S(1)} %copy-done.1, ...), custom_call_target="tpu_custom_call" | custom-call | tf_op jit(solution)/shard_map/local_terms/pallas_call | solution.py:226
  39.4 0.2 collective-permute-done.2.refs_6_.refs_2_.refs_1_.refs_0_
  39.6 1.0 %state_step.7.refs_4_ = f32[4,128,128]{2,1,0:T(8,128)} custom-call(s32[1]{0:T(128)} %bitcast.here_ref, f32[4,128,128]{2,1,0:T(8,128)S(1)} %get-tuple-element.49.refs_0_, f32[4,128,128]{2,1,0:T(8,128)S(1)} %get-tuple-element.47.refs_0_.refs_1_, f32[4,128,128]{2,1,0:T(8,128)S(1)} %get-tuple-element.44.refs_0_.refs_1_.refs_2_, ...), custom_call_target="tpu_custom_call" | custom-call | flops 1048576 | bytes 1024 | tf_op jit(solution)/shard_map/state_step/pallas_call | solution.py:276
  40.6 1.9 %collective-permute-start.5 = (f32[4,128,128]{2,1,0:T(8,128)}, f32[4,128,128]{2,1,0:T(8,128)S(1)}, u32[]{:S(2)}, u32[]{:S(2)}) collective-permute-start(f32[4,128,128]{2,1,0:T(8,128)} %state_step.7.refs_4_), channel_id=1, source_target_pairs={{0,4},{4,8},{8,12},{1,5},{5,9},{9,13},{2,6},{6,10},{10,14},{3,7},{... | collective-permute-start | bytes 786440 | tf_op jit(solution)/shard_map/ppermute | solution.py:352
  42.5 1.0 %copy-done.7 = f32[4,128,128]{2,1,0:T(8,128)S(1)} copy-done((f32[4,128,128]{2,1,0:T(8,128)S(1)}, f32[4,128,128]{2,1,0:T(8,128)}, u32[]{:S(2)}) %copy-start.7) | copy-done | bytes 262168
  43.5 0.9 %copy-done.9 = f32[4,128,128]{2,1,0:T(8,128)S(1)} copy-done((f32[4,128,128]{2,1,0:T(8,128)S(1)}, f32[4,128,128]{2,1,0:T(8,128)}, u32[]{:S(2)}) %copy-start.9) | copy-done | bytes 262168
  44.5 0.9 %copy-done.17 = f32[4,128,128]{2,1,0:T(8,128)S(1)} copy-done((f32[4,128,128]{2,1,0:T(8,128)S(1)}, f32[4,128,128]{2,1,0:T(8,128)}, u32[]{:S(2)}) %copy-start.17) | copy-done | bytes 262168
  45.4 0.9 %copy-done.18 = f32[4,128,128]{2,1,0:T(8,128)S(1)} copy-done((f32[4,128,128]{2,1,0:T(8,128)S(1)}, f32[4,128,128]{2,1,0:T(8,128)}, u32[]{:S(2)}) %copy-start.18) | copy-done | bytes 262168
  46.4 0.7 project.4
  47.1 0.1 collective-permute-start.3
  47.2 0.5 collective-permute-start.4
  47.7 1.4 %collective-permute-done.5.refs_4_.refs_2_.refs_1_.refs_0_ = f32[4,128,128]{2,1,0:T(8,128)S(1)} collective-permute-done((f32[4,128,128]{2,1,0:T(8,128)}, f32[4,128,128]{2,1,0:T(8,128)S(1)}, u32[]{:S(2)}, u32[]{:S(2)}) %collective-permute-start.5) | collective-permute-done | bytes 262176 | tf_op jit(solution)/shard_map/ppermute | solution.py:352
  49.1 0.3 state_step.8.refs_2_
  49.3 1.9 %collective-permute-start.9 = (f32[4,128,128]{2,1,0:T(8,128)S(1)}, f32[4,128,128]{2,1,0:T(8,128)S(1)}, u32[]{:S(2)}, u32[]{:S(2)}) collective-permute-start(f32[4,128,128]{2,1,0:T(8,128)S(1)} %state_step.8.refs_2_), channel_id=1, source_target_pairs={{4,8},{8,12},{5,9},{9,13},{6,10},{10,14},{7,11},{11,15},{20,24},{2... | collective-permute-start | bytes 786440 | tf_op jit(solution)/shard_map/ppermute | solution.py:352
  51.4 0.7 project.5
  52.2 0.5 collective-permute-start.8
  52.7 0.5 collective-permute-start.6
  53.2 4.9 %collective-permute-done.9.refs_2_.refs_1_ = f32[4,128,128]{2,1,0:T(8,128)S(1)} collective-permute-done((f32[4,128,128]{2,1,0:T(8,128)S(1)}, f32[4,128,128]{2,1,0:T(8,128)S(1)}, u32[]{:S(2)}, u32[]{:S(2)}) %collective-permute-start.9) | collective-permute-done | bytes 262176 | tf_op jit(solution)/shard_map/ppermute | solution.py:352
  58.2 0.3 state_step.9.refs_2_
  58.4 2.0 %collective-permute-start.13 = (f32[4,128,128]{2,1,0:T(8,128)S(1)}, f32[4,128,128]{2,1,0:T(8,128)S(1)}, u32[]{:S(2)}, u32[]{:S(2)}) collective-permute-start(f32[4,128,128]{2,1,0:T(8,128)S(1)} %state_step.9.refs_2_), channel_id=1, source_target_pairs={{8,12},{9,13},{10,14},{11,15},{24,28},{25,29},{26,30},{27,31}} | collective-permute-start | bytes 786440 | tf_op jit(solution)/shard_map/ppermute | solution.py:352
  60.5 0.6 collective-permute-start.10
  61.1 0.8 project.6
  62.0 0.5 collective-permute-start.12
  62.5 1.8 %collective-permute-done.13.refs_2_ = f32[4,128,128]{2,1,0:T(8,128)S(1)} collective-permute-done((f32[4,128,128]{2,1,0:T(8,128)S(1)}, f32[4,128,128]{2,1,0:T(8,128)S(1)}, u32[]{:S(2)}, u32[]{:S(2)}) %collective-permute-start.13) | collective-permute-done | bytes 262176 | tf_op jit(solution)/shard_map/ppermute | solution.py:352
  64.3 0.7 project.7
  65.1 0.5 collective-permute-start.16
  65.6 0.6 collective-permute-start.14
  66.2 0.7 collective-permute-done.10
  67.0 0.8 %collective-permute-start.17 = (f32[1,128,512]{2,1,0:T(8,128)S(1)}, f32[1,128,512]{2,1,0:T(8,128)S(1)}, u32[]{:S(2)}, u32[]{:S(2)}) collective-permute-start(f32[1,128,512]{2,1,0:T(8,128)S(1)} %get-tuple-element.76), channel_id=1, source_target_pairs={{0,2},{1,3},{2,0},{3,1},{4,6},{5,7},{6,4},{7,5},{8,10},{9,11},{10,... | collective-permute-start | bytes 786440 | tf_op jit(solution)/shard_map/ppermute | solution.py:347
  68.0 6.9 %collective-permute-done.14 = f32[1,128,512]{2,1,0:T(8,128)S(1)} collective-permute-done((f32[1,128,512]{2,1,0:T(8,128)S(1)}, f32[1,128,512]{2,1,0:T(8,128)S(1)}, u32[]{:S(2)}, u32[]{:S(2)}) %collective-permute-start.14) | collective-permute-done | bytes 262176 | tf_op jit(solution)/shard_map/ppermute | solution.py:347
  74.9 4.7 %collective-permute-done.17 = f32[1,128,512]{2,1,0:T(8,128)S(1)} collective-permute-done((f32[1,128,512]{2,1,0:T(8,128)S(1)}, f32[1,128,512]{2,1,0:T(8,128)S(1)}, u32[]{:S(2)}, u32[]{:S(2)}) %collective-permute-start.17) | collective-permute-done | bytes 262176 | tf_op jit(solution)/shard_map/ppermute | solution.py:347
  79.7 1.0 %pad_maximum_fusion = f32[4,128,512]{2,1,0:T(8,128)} fusion(f32[1,128,512]{2,1,0:T(8,128)S(1)} %add.21, f32[1,128,512]{2,1,0:T(8,128)S(1)} %add.20, f32[1,128,512]{2,1,0:T(8,128)S(1)} %add.19, f32[1,128,512]{2,1,0:T(8,128)S(1)} %add.18), kind=kLoop, calls=%fused_computation | loop fusion | flops 786432 | bytes 2097152 | tf_op jit(solution)/shard_map/stack | solution.py:469
  (52 shorter events, 0.7 us)
Async XLA Ops:
  0.0 1.2 %copy-start.1 = (bf16[4,128,2,512]{3,2,1,0:T(2,128)(2,1)S(1)}, bf16[4,128,2,512]{3,2,1,0:T(2,128)(2,1)}, u32[]{:S(2)}) copy-start(bf16[4,128,2,512]{3,2,1,0:T(2,128)(2,1)} %k_ref.7) | copy-start | bytes 3145732
  1.2 1.2 %copy-start.2 = (bf16[4,128,2,512]{3,2,1,0:T(2,128)(2,1)S(1)}, bf16[4,128,2,512]{3,2,1,0:T(2,128)(2,1)}, u32[]{:S(2)}) copy-start(bf16[4,128,2,512]{3,2,1,0:T(2,128)(2,1)} %v_ref.7) | copy-start | bytes 3145732
  2.5 1.0 %copy-start.3 = (bf16[4,128,512]{2,1,0:T(8,128)(2,1)S(1)}, bf16[4,128,512]{2,1,0:T(8,128)(2,1)}, u32[]{:S(2)}) copy-start(bf16[4,128,512]{2,1,0:T(8,128)(2,1)} %q_ref.7) | copy-start | bytes 1572868
  3.5 0.7 copy-start.10
  4.2 0.7 copy-start.19
  4.9 0.7 copy-start.20
  11.9 7.0 %collective-permute-start = (f32[4,128,128]{2,1,0:T(8,128)S(1)}, f32[4,128,128]{2,1,0:T(8,128)S(1)}, u32[]{:S(2)}, u32[]{:S(2)}) collective-permute-start(f32[4,128,128]{2,1,0:T(8,128)S(1)} %get-tuple-element.43.refs_0_.refs_3_.refs_5_), channel_id=1, source_target_pairs={{0,4},{1,5},{2,6},{3,7},{16,20},{17,21},{18,22},{19,23}} | collective-permute-start | bytes 786440 | tf_op jit(solution)/shard_map/ppermute | solution.py:352
  18.9 0.7 copy-start.8
  19.6 10.7 %collective-permute-start.1 = (f32[4,128,128]{2,1,0:T(8,128)S(1)}, f32[4,128,128]{2,1,0:T(8,128)S(1)}, u32[]{:S(2)}, u32[]{:S(2)}) collective-permute-start(f32[4,128,128]{2,1,0:T(8,128)S(1)} %state_step.5.refs_0_), channel_id=1, source_target_pairs={{0,4},{4,8},{1,5},{5,9},{2,6},{6,10},{3,7},{7,11},{16,20},{20,24},... | collective-permute-start | bytes 786440 | tf_op jit(solution)/shard_map/ppermute | solution.py:352
  30.3 0.7 copy-start.6
  31.0 11.5 %copy-start = (bf16[512,2048]{1,0:T(8,128)(2,1)S(1)}, bf16[512,2048]{1,0:T(8,128)(2,1)}, u32[]{:S(2)}) copy-start(bf16[512,2048]{1,0:T(8,128)(2,1)} %refs_3_.7) | copy-start | bytes 6291460
  31.0 8.6 %collective-permute-start.2 = (f32[4,128,128]{2,1,0:T(8,128)S(1)}, f32[4,128,128]{2,1,0:T(8,128)S(1)}, u32[]{:S(2)}, u32[]{:S(2)}) collective-permute-start(f32[4,128,128]{2,1,0:T(8,128)S(1)} %state_step.6.refs_0_), channel_id=1, source_target_pairs={{0,4},{4,8},{8,12},{1,5},{5,9},{9,13},{2,6},{6,10},{10,14},{3,7},{... | collective-permute-start | bytes 786440 | tf_op jit(solution)/shard_map/ppermute | solution.py:352
  39.4 1.2 %copy-start.4 = (f32[4,128,128]{2,1,0:T(8,128)}, f32[4,128,128]{2,1,0:T(8,128)S(1)}, u32[]{:S(2)}) copy-start(f32[4,128,128]{2,1,0:T(8,128)S(1)} %get-tuple-element.49.refs_0_) | copy-start | bytes 786436
  40.6 8.5 %collective-permute-start.5 = (f32[4,128,128]{2,1,0:T(8,128)}, f32[4,128,128]{2,1,0:T(8,128)S(1)}, u32[]{:S(2)}, u32[]{:S(2)}) collective-permute-start(f32[4,128,128]{2,1,0:T(8,128)} %state_step.7.refs_4_), channel_id=1, source_target_pairs={{0,4},{4,8},{8,12},{1,5},{5,9},{9,13},{2,6},{6,10},{10,14},{3,7},{... | collective-permute-start | bytes 786440 | tf_op jit(solution)/shard_map/ppermute | solution.py:352
  42.5 6.6 %copy-start.5 = (f32[4,128,128]{2,1,0:T(8,128)S(1)}, f32[4,128,128]{2,1,0:T(8,128)}, u32[]{:S(2)}) copy-start(f32[4,128,128]{2,1,0:T(8,128)} %copy-done.4) | copy-start | bytes 786436
  42.5 1.0 %copy-start.7 = (f32[4,128,128]{2,1,0:T(8,128)S(1)}, f32[4,128,128]{2,1,0:T(8,128)}, u32[]{:S(2)}) copy-start(f32[4,128,128]{2,1,0:T(8,128)} %copy-done.6) | copy-start | bytes 786436
  43.5 0.9 %copy-start.9 = (f32[4,128,128]{2,1,0:T(8,128)S(1)}, f32[4,128,128]{2,1,0:T(8,128)}, u32[]{:S(2)}) copy-start(f32[4,128,128]{2,1,0:T(8,128)} %copy-done.8) | copy-start | bytes 786436
  44.5 0.9 %copy-start.17 = (f32[4,128,128]{2,1,0:T(8,128)S(1)}, f32[4,128,128]{2,1,0:T(8,128)}, u32[]{:S(2)}) copy-start(f32[4,128,128]{2,1,0:T(8,128)} %get-tuple-element.41.reach_ref) | copy-start | bytes 786436
  45.4 0.9 %copy-start.18 = (f32[4,128,128]{2,1,0:T(8,128)S(1)}, f32[4,128,128]{2,1,0:T(8,128)}, u32[]{:S(2)}) copy-start(f32[4,128,128]{2,1,0:T(8,128)} %get-tuple-element.42.own_ref) | copy-start | bytes 786436
  47.1 4.2 %copy-start.15 = (f32[4,128,128]{2,1,0:T(8,128)S(1)}, f32[4,128,128]{2,1,0:T(8,128)}, u32[]{:S(2)}) copy-start(f32[4,128,128]{2,1,0:T(8,128)} %get-tuple-element.56.reach_ref) | copy-start | bytes 786436
  47.1 4.2 %copy-start.16 = (f32[4,128,128]{2,1,0:T(8,128)S(1)}, f32[4,128,128]{2,1,0:T(8,128)}, u32[]{:S(2)}) copy-start(f32[4,128,128]{2,1,0:T(8,128)} %get-tuple-element.57.own_ref) | copy-start | bytes 786436
  47.1 4.1 %collective-permute-start.3 = (f32[128,512]{1,0:T(8,128)S(1)}, f32[128,512]{1,0:T(8,128)S(1)}, u32[]{:S(2)}, u32[]{:S(2)}) collective-permute-start(f32[128,512]{1,0:T(8,128)S(1)} %get-tuple-element.52), channel_id=1, source_target_pairs={{0,1},{1,0},{2,3},{3,2},{4,5},{5,4},{6,7},{7,6},{8,9},{9,8},{10,11... | collective-permute-start | bytes 786440 | tf_op jit(solution)/shard_map/ppermute | solution.py:347
  47.2 4.1 %collective-permute-start.4 = (f32[128,512]{1,0:T(8,128)S(1)}, f32[128,512]{1,0:T(8,128)S(1)}, u32[]{:S(2)}, u32[]{:S(2)}) collective-permute-start(f32[128,512]{1,0:T(8,128)S(1)} %get-tuple-element.53), channel_id=1, source_target_pairs={{0,1},{1,0},{2,3},{3,2},{4,5},{5,4},{6,7},{7,6},{8,9},{9,8},{10,11... | collective-permute-start | bytes 786440 | tf_op jit(solution)/shard_map/ppermute | solution.py:347
  49.3 8.8 %collective-permute-start.9 = (f32[4,128,128]{2,1,0:T(8,128)S(1)}, f32[4,128,128]{2,1,0:T(8,128)S(1)}, u32[]{:S(2)}, u32[]{:S(2)}) collective-permute-start(f32[4,128,128]{2,1,0:T(8,128)S(1)} %state_step.8.refs_2_), channel_id=1, source_target_pairs={{4,8},{8,12},{5,9},{9,13},{6,10},{10,14},{7,11},{11,15},{20,24},{2... | collective-permute-start | bytes 786440 | tf_op jit(solution)/shard_map/ppermute | solution.py:352
  52.1 9.0 %copy-start.13 = (f32[4,128,128]{2,1,0:T(8,128)S(1)}, f32[4,128,128]{2,1,0:T(8,128)}, u32[]{:S(2)}) copy-start(f32[4,128,128]{2,1,0:T(8,128)} %get-tuple-element.63.reach_ref) | copy-start | bytes 786436
  52.1 9.0 %copy-start.14 = (f32[4,128,128]{2,1,0:T(8,128)S(1)}, f32[4,128,128]{2,1,0:T(8,128)}, u32[]{:S(2)}) copy-start(f32[4,128,128]{2,1,0:T(8,128)} %get-tuple-element.64.own_ref) | copy-start | bytes 786436
  52.1 8.3 %collective-permute-start.7 = (f32[128,512]{1,0:T(8,128)S(1)}, f32[128,512]{1,0:T(8,128)S(1)}, u32[]{:S(2)}, u32[]{:S(2)}) collective-permute-start(f32[128,512]{1,0:T(8,128)S(1)} %get-tuple-element.59), channel_id=1, source_target_pairs={{0,1},{1,0},{2,3},{3,2},{4,5},{5,4},{6,7},{7,6},{8,9},{9,8},{10,11... | collective-permute-start | bytes 786440 | tf_op jit(solution)/shard_map/ppermute | solution.py:347
  52.2 8.2 %collective-permute-start.8 = (f32[128,512]{1,0:T(8,128)S(1)}, f32[128,512]{1,0:T(8,128)S(1)}, u32[]{:S(2)}, u32[]{:S(2)}) collective-permute-start(f32[128,512]{1,0:T(8,128)S(1)} %get-tuple-element.60), channel_id=1, source_target_pairs={{0,1},{1,0},{2,3},{3,2},{4,5},{5,4},{6,7},{7,6},{8,9},{9,8},{10,11... | collective-permute-start | bytes 786440 | tf_op jit(solution)/shard_map/ppermute | solution.py:347
  52.7 8.4 %collective-permute-start.6 = (f32[1,128,512]{2,1,0:T(8,128)S(1)}, f32[1,128,512]{2,1,0:T(8,128)S(1)}, u32[]{:S(2)}, u32[]{:S(2)}) collective-permute-start(f32[1,128,512]{2,1,0:T(8,128)S(1)} %get-tuple-element.55.refs_4_), channel_id=1, source_target_pairs={{0,2},{1,3},{2,0},{3,1},{4,6},{5,7},{6,4},{7,5},{8,10},{9,11},{10,... | collective-permute-start | bytes 786440 | tf_op jit(solution)/shard_map/ppermute | solution.py:347
  58.4 5.8 %collective-permute-start.13 = (f32[4,128,128]{2,1,0:T(8,128)S(1)}, f32[4,128,128]{2,1,0:T(8,128)S(1)}, u32[]{:S(2)}, u32[]{:S(2)}) collective-permute-start(f32[4,128,128]{2,1,0:T(8,128)S(1)} %state_step.9.refs_2_), channel_id=1, source_target_pairs={{8,12},{9,13},{10,14},{11,15},{24,28},{25,29},{26,30},{27,31}} | collective-permute-start | bytes 786440 | tf_op jit(solution)/shard_map/ppermute | solution.py:352
  60.5 3.8 %copy-start.11 = (f32[4,128,128]{2,1,0:T(8,128)S(1)}, f32[4,128,128]{2,1,0:T(8,128)}, u32[]{:S(2)}) copy-start(f32[4,128,128]{2,1,0:T(8,128)} %get-tuple-element.68.reach_ref) | copy-start | bytes 786436
  60.5 3.8 %copy-start.12 = (f32[4,128,128]{2,1,0:T(8,128)S(1)}, f32[4,128,128]{2,1,0:T(8,128)}, u32[]{:S(2)}) copy-start(f32[4,128,128]{2,1,0:T(8,128)} %get-tuple-element.69.own_ref) | copy-start | bytes 786436
  60.5 6.4 %collective-permute-start.10 = (f32[1,128,512]{2,1,0:T(8,128)S(1)}, f32[1,128,512]{2,1,0:T(8,128)S(1)}, u32[]{:S(2)}, u32[]{:S(2)}) collective-permute-start(f32[1,128,512]{2,1,0:T(8,128)S(1)} %get-tuple-element.62.refs_4_), channel_id=1, source_target_pairs={{0,2},{1,3},{2,0},{3,1},{4,6},{5,7},{6,4},{7,5},{8,10},{9,11},{10,... | collective-permute-start | bytes 786440 | tf_op jit(solution)/shard_map/ppermute | solution.py:347
  61.9 3.7 %collective-permute-start.11 = (f32[128,512]{1,0:T(8,128)S(1)}, f32[128,512]{1,0:T(8,128)S(1)}, u32[]{:S(2)}, u32[]{:S(2)}) collective-permute-start(f32[128,512]{1,0:T(8,128)S(1)} %get-tuple-element.66), channel_id=1, source_target_pairs={{0,1},{1,0},{2,3},{3,2},{4,5},{5,4},{6,7},{7,6},{8,9},{9,8},{10,11... | collective-permute-start | bytes 786440 | tf_op jit(solution)/shard_map/ppermute | solution.py:347
  62.0 3.6 %collective-permute-start.12 = (f32[128,512]{1,0:T(8,128)S(1)}, f32[128,512]{1,0:T(8,128)S(1)}, u32[]{:S(2)}, u32[]{:S(2)}) collective-permute-start(f32[128,512]{1,0:T(8,128)S(1)} %get-tuple-element.67), channel_id=1, source_target_pairs={{0,1},{1,0},{2,3},{3,2},{4,5},{5,4},{6,7},{7,6},{8,9},{9,8},{10,11... | collective-permute-start | bytes 786440 | tf_op jit(solution)/shard_map/ppermute | solution.py:347
  65.0 2.0 %collective-permute-start.15 = (f32[128,512]{1,0:T(8,128)S(1)}, f32[128,512]{1,0:T(8,128)S(1)}, u32[]{:S(2)}, u32[]{:S(2)}) collective-permute-start(f32[128,512]{1,0:T(8,128)S(1)} %get-tuple-element.73), channel_id=1, source_target_pairs={{0,1},{1,0},{2,3},{3,2},{4,5},{5,4},{6,7},{7,6},{8,9},{9,8},{10,11... | collective-permute-start | bytes 786440 | tf_op jit(solution)/shard_map/ppermute | solution.py:347
  65.1 1.9 %collective-permute-start.16 = (f32[128,512]{1,0:T(8,128)S(1)}, f32[128,512]{1,0:T(8,128)S(1)}, u32[]{:S(2)}, u32[]{:S(2)}) collective-permute-start(f32[128,512]{1,0:T(8,128)S(1)} %get-tuple-element.74), channel_id=1, source_target_pairs={{0,1},{1,0},{2,3},{3,2},{4,5},{5,4},{6,7},{7,6},{8,9},{9,8},{10,11... | collective-permute-start | bytes 786440 | tf_op jit(solution)/shard_map/ppermute | solution.py:347
  65.6 9.2 %collective-permute-start.14 = (f32[1,128,512]{2,1,0:T(8,128)S(1)}, f32[1,128,512]{2,1,0:T(8,128)S(1)}, u32[]{:S(2)}, u32[]{:S(2)}) collective-permute-start(f32[1,128,512]{2,1,0:T(8,128)S(1)} %get-tuple-element.72.refs_2_), channel_id=1, source_target_pairs={{0,2},{1,3},{2,0},{3,1},{4,6},{5,7},{6,4},{7,5},{8,10},{9,11},{10,... | collective-permute-start | bytes 786440 | tf_op jit(solution)/shard_map/ppermute | solution.py:347
  67.0 12.6 %collective-permute-start.17 = (f32[1,128,512]{2,1,0:T(8,128)S(1)}, f32[1,128,512]{2,1,0:T(8,128)S(1)}, u32[]{:S(2)}, u32[]{:S(2)}) collective-permute-start(f32[1,128,512]{2,1,0:T(8,128)S(1)} %get-tuple-element.76), channel_id=1, source_target_pairs={{0,2},{1,3},{2,0},{3,1},{4,6},{5,7},{6,4},{7,5},{8,10},{9,11},{10,... | collective-permute-start | bytes 786440 | tf_op jit(solution)/shard_map/ppermute | solution.py:347

commit v5 on v4

--- a/solution.py
+++ b/solution.py
@@ -47,11 +47,31 @@
     return lax.broadcasted_iota(jnp.int32, shape, axis)
 
 
-def local_kernel(head_count, seq, offset_ref, resets_ref, q_ref, k_ref, v_ref, gate_ref, beta_ref,
-                 *refs):
-    transit_ref, filled_ref, reach_ref, own_ref = refs[-4:]
-    tok = q_ref.shape[1]
-    size = q_ref.shape[2] // head_count
+def local_kernel(head_count, seq, fetch, ahead, later, offset_ref, resets_ref, *refs):
+    refs = list(refs)
+    inputs = [refs.pop(0) for _ in range(5)]
+    sources = inputs if fetch else [refs.pop(0) for _ in range(5)] if ahead else []
+    refs = refs[later:]
+    transit_ref, filled_ref, reach_hbm, own_hbm = [refs.pop(0) for _ in range(4)]
+    nexts = [refs.pop(0) for _ in range(5)] if ahead else []
+    reach_ref, own_ref, sems = refs.pop(0), refs.pop(0), refs.pop(0)
+    arrivals, ahead_copies = [], []
+    if fetch:
+        arrivals = [
+            pltpu.make_async_copy(source.at[seq], refs[n], sems.at[n])
+            for n, source in enumerate(sources)
+        ]
+        inputs = refs
+    if ahead:
+        ahead_copies = [
+            pltpu.make_async_copy(source.at[seq + 1], nexts[n], sems.at[5 + n])
+            for n, source in enumerate(sources)
+        ]
+    for copy in arrivals + ahead_copies:
+        copy.start()
+    q_ref, k_ref, v_ref, gate_ref, beta_ref = inputs
+    tok = q_ref.shape[0]
+    size = q_ref.shape[1] // head_count
     keys = 2 * tok
     half = keys // 2
     heads = range(head_count)
@@ -78,11 +98,13 @@
         return m[:n] + m[n:2 * n] + m[2 * n:3 * n]
 
     tok_i, key_i = iota((tok, keys), 0), iota((tok, keys), 1)
-    gate3 = stacked(gate_ref[0])
+    for copy in arrivals:
+        copy.wait()
+    gate3 = stacked(gate_ref[...])
     gs_row = folded(mm(gate3, (tok_i <= (key_i >> 1)).astype(f32).astype(bf16)))
     beta_row = folded(
-        mm(stacked(beta_ref[0, 0]), (key_i == 2 * tok_i).astype(f32).astype(bf16))
-        + mm(stacked(beta_ref[0, 1]), (key_i == 2 * tok_i + 1).astype(f32).astype(bf16))
+        mm(stacked(beta_ref[0]), (key_i == 2 * tok_i).astype(f32).astype(bf16))
+        + mm(stacked(beta_ref[1]), (key_i == 2 * tok_i + 1).astype(f32).astype(bf16))
     )
     gs_tok_row = folded(
         mm(gate3, (iota((tok, tok), 0) <= iota((tok, tok), 1)).astype(f32).astype(bf16))
@@ -107,9 +129,9 @@
         (iota((tok, keys), 1) >> 1) <= iota((tok, keys), 0), doc_tok == doc_row
     )
 
-    q = [q_ref[0, :, h * size:(h + 1) * size] for h in heads]
-    k = [k_ref[0, :, :, h * size:(h + 1) * size].astype(f32).reshape(2 * tok, size).astype(bf16) for h in heads]
-    v = [v_ref[0, :, :, h * size:(h + 1) * size].astype(f32).reshape(2 * tok, size).astype(bf16) for h in heads]
+    q = [q_ref[:, h * size:(h + 1) * size] for h in heads]
+    k = [k_ref[:, :, h * size:(h + 1) * size].astype(f32).reshape(2 * tok, size).astype(bf16) for h in heads]
+    v = [v_ref[:, :, h * size:(h + 1) * size].astype(f32).reshape(2 * tok, size).astype(bf16) for h in heads]
 
     def unit(x):
         return lax.rsqrt(jnp.sum(x * x, axis=1, keepdims=True) + epsilon)
@@ -194,59 +216,57 @@
         )
 
     for h in heads:
-        gr, gc, gt = gs_row[h:h + 1], gs_col[:, h:h + 1], gs_tok[:, h:h + 1]
-        last = gr[:, keys - 1:]
+        gr, gt = gs_row[h:h + 1], gs_tok[:, h:h + 1]
         carried_tok = jnp.where(doc_tok == start_doc, jnp.exp(gt), 0.0)
-        closing = jnp.where(doc_col == last_doc, jnp.exp(last - gc), 0.0)
+        q32 = q[h].astype(f32)
+        q_norm = unit(q32)
+        probes = jnp.where(
+            tok_linked, mm_nt(q[h], k[h]) * jnp.exp(gt - gr) * k_row[h] * q_norm, 0.0
+        )
+        outs = dot3(probes, both[h])
+        reach_ref[h] = (carried_tok * q_norm) * q32 - outs[:, :size]
+        own_ref[h] = outs[:, size:]
+    departures = [
+        pltpu.make_async_copy(reach_ref, reach_hbm, sems.at[10]),
+        pltpu.make_async_copy(own_ref, own_hbm, sems.at[11]),
+    ]
+    for copy in departures:
+        copy.start()
+    for h in heads:
+        last = gs_row[h:h + 1, keys - 1:]
+        closing = jnp.where(doc_col == last_doc, jnp.exp(last - gs_col[:, h:h + 1]), 0.0)
         end_high, end_low = split(both[h] * (closing * k_col[h]))
         ends = mm_tn(k[h], end_high) + mm_tn(k[h], end_low)
         keep = jnp.where(last_doc == start_doc, jnp.exp(last), 0.0)
         transit_ref[h] = keep * eye_size - ends[:, :size]
         filled_ref[h] = ends[:, size:]
-        q32 = q[h].astype(f32)
-        q_norm = unit(q32)
-        probes = jnp.where(
-            tok_linked, mm_nt(q[h], k[h]) * jnp.exp(gt - gr) * k_row[h] * q_norm, 0.0
-        )
-        outs = dot3(probes, both[h])
-        reach_ref[h] = (carried_tok * q_norm) * q32 - outs[:, :size]
-        own_ref[h] = outs[:, size:]
-
-
-def local_terms(seq, offset, resets, queries, keys, values, log_gate, beta, earlier=()):
-    _, tok, packed = queries.shape
-    head_count = log_gate.shape[1]
+    for copy in departures + ahead_copies:
+        copy.wait()
+
+
+def local_terms(seq, offset, resets, arrays, loaded, earlier=()):
+    count, tok, packed = arrays[0].shape
+    head_count = arrays[3].shape[1]
     size = packed // head_count
-
-    def block(shape):
-        return pl.BlockSpec((1,) + shape, lambda i, o, r: (seq,) + (0,) * len(shape))
-
-    whole = pl.BlockSpec((head_count, size, size), lambda i, o, r: (0, 0, 0))
-    tall = pl.BlockSpec((head_count, tok, size), lambda i, o, r: (0, 0, 0))
-    return pl.pallas_call(
-        functools.partial(local_kernel, head_count, seq),
-        grid_spec=pltpu.PrefetchScalarGridSpec(
-            num_scalar_prefetch=2,
-            grid=(1,),
-            in_specs=[
-                block((tok, packed)),
-                block((tok, 2, packed)),
-                block((tok, 2, packed)),
-                block((head_count, tok)),
-                block((2, head_count, tok)),
-            ]
-            + untouched(earlier),
-            out_specs=[whole, whole, tall, tall],
-        ),
-        out_shape=[
-            jax.ShapeDtypeStruct((head_count, size, size), f32),
-            jax.ShapeDtypeStruct((head_count, size, size), f32),
-            pltpu.HBM((head_count, tok, size), f32),
-            pltpu.HBM((head_count, tok, size), f32),
-        ],
+    fetch, ahead = loaded is None, seq + 1 < count
+    smem, hbm = pl.BlockSpec(memory_space=pltpu.SMEM), pl.BlockSpec(memory_space=pltpu.HBM)
+    operands = list(arrays) if fetch else list(loaded) + (list(arrays) if ahead else [])
+    specs = [hbm] * 5 if fetch else vmem(5) + ([hbm] * 5 if ahead else [])
+    squares = [pltpu.VMEM((head_count, size, size), f32)] * 2
+    talls = [pltpu.HBM((head_count, tok, size), f32)] * 2
+    blocks = [pltpu.VMEM(x.shape[1:], x.dtype) for x in arrays]
+    outs = pl.pallas_call(
+        functools.partial(local_kernel, head_count, seq, fetch, ahead, len(earlier)),
+        in_specs=[smem, smem] + specs + untouched(earlier),
+        out_specs=vmem(2) + [hbm] * 2 + (vmem(5) if ahead else []),
+        out_shape=squares + talls + (blocks if ahead else []),
+        scratch_shapes=[pltpu.VMEM((head_count, tok, size), f32)] * 2
+        + [pltpu.SemaphoreType.DMA((12,))]
+        + (blocks if fetch else []),
         compiler_params=pltpu.CompilerParams(vmem_limit_bytes=16 << 20),
         name="local_terms",
-    )(offset, resets, queries, keys, values, log_gate, beta, *earlier)
+    )(offset, resets, *operands, *earlier)
+    return outs[:4], outs[4:]
 
 
 def vmem(count):
@@ -279,7 +299,7 @@
         + vmem(2 * len(maps) + 1)
         + untouched(earlier),
         out_specs=pl.BlockSpec(memory_space=pltpu.VMEM),
-        out_shape=jax.ShapeDtypeStruct(state.shape, f32),
+        out_shape=pltpu.VMEM(state.shape, f32),
         compiler_params=pltpu.CompilerParams(vmem_limit_bytes=8 << 20),
         cost_estimate=small_cost,
         name="state_step",
@@ -329,8 +349,8 @@
         functools.partial(project_kernel, len(states), groups),
         in_specs=[smem, smem] + vmem(3 + len(states)) + untouched(earlier),
         out_specs=vmem(mid + 1),
-        out_shape=[jax.ShapeDtypeStruct((tok, part), f32)] * mid
-        + [jax.ShapeDtypeStruct((mid, tok, part), f32)],
+        out_shape=[pltpu.VMEM((tok, part), f32)] * mid
+        + [pltpu.VMEM((mid, tok, part), f32)],
         scratch_shapes=[
             pltpu.VMEM((tok, heads * size), bf16),
             pltpu.VMEM((heads, size, size), f32),
@@ -360,7 +380,7 @@
 
 
 def add_parts(mine, others, earlier=()):
-    part = jax.ShapeDtypeStruct((mine.shape[0] // 2,) + mine.shape[1:], f32)
+    part = pltpu.VMEM((mine.shape[0] // 2,) + mine.shape[1:], f32)
     return pl.pallas_call(
         add_kernel,
         in_specs=vmem(1 + len(others)) + untouched(earlier),
@@ -390,13 +410,18 @@
     offset = here * tok
     place = lax.axis_index("head").astype(jnp.int32).reshape(1)
 
-    def local(s, earlier=()):
-        return local_terms(
-            s, offset, resets, queries, keys, values, log_gate, beta, earlier
-        )
+    arrays = [
+        pltpu.with_memory_space_constraint(x, pltpu.HBM)
+        for x in (queries, keys, values, log_gate, beta)
+    ]
+    resets = pltpu.with_memory_space_constraint(resets, pltpu.HBM)
+    loaded = None
 
     if devices > 8:
-        terms = [local(s) for s in range(chunks)]
+        terms = []
+        for s in range(chunks):
+            term, loaded = local_terms(s, offset, resets, arrays, loaded)
+            terms.append(term)
         pairs = [(i, i + 1) for i in range(devices - 1)]
         no_choice = jnp.zeros((1,), jnp.int32)
 
@@ -442,8 +467,9 @@
 
     for r in range(last_round + 1):
         if r < chunks:
-            terms.append(local(r, token))
-            token = (terms[r][1],)
+            term, loaded = local_terms(r, offset, resets, arrays, loaded, token)
+            terms.append(term)
+            token = (term[1],)
         if r == 0:
             sent = terms[0][1]
         else:

time: 82.2 us -> 77.2 us (0.939)
  local copies, waits for them, and re-layouts: 10.6 us -> 3.88 us
  Pallas kernels: 30.3 us -> 32.1 us
    unnamed x42 -> x30, local copies, waits for them, and re-layouts: 10.6 us -> 3.88 us
    pallas_call x4, Pallas kernels: 25.3 us -> 27.1 us  [local_terms(): pl.pallas_call(functools.partial(local_kernel, head_count, seq, fetch, ah...]
  transfers between devices with their start and end apart: 18 -> 18, of which waited for: 8 -> 8; matrix products, arithmetic and copies ran while one was open for 0% -> 0% of each run, Pallas kernels for 28% -> 31%
where the time goes in v5:
time: 77.2 us; the launch traced here: 75.8 us
  Pallas kernels  32.1 us (42%)
  waiting for transfers between devices  23.3 us (30%)
  starting transfers between devices  14.9 us (19%)
  local copies, waits for them, and re-layouts  3.88 us (5%)
  other arithmetic  1.18 us (2%)
    pallas_call x4, Pallas kernels, local_terms(): pl.pallas_call(functools.partial(local_kernel, head_count, seq, fetch, ah...  27.1 us
    ppermute x12, waiting for transfers between devices, swapped(): return lax.ppermute(x, axis, [(i, i ^ bit) for i in range(size)])  12.3 us
    ppermute x6, waiting for transfers between devices, carry_on(): return lax.ppermute(x, 'seq', pairs)  11 us
    ppermute x6, starting transfers between devices, carry_on(): return lax.ppermute(x, 'seq', pairs)  9.99 us
    ppermute x12, starting transfers between devices, swapped(): return lax.ppermute(x, axis, [(i, i ^ bit) for i in range(size)])  4.88 us
    unnamed x30, local copies, waits for them, and re-layouts  3.88 us
    pallas_call x4, Pallas kernels, project(): pl.pallas_call(functools.partial(project_kernel, len(states), groups), in...  2.95 us
    pallas_call x5, Pallas kernels, step(): pl.pallas_call(functools.partial(step_kernel, len(maps)), in_specs=[pl.Bl...  1.81 us
  transfers between devices with their start and end apart: 18, of which 8 were waited for; matrix products, arithmetic and copies ran while one was open for 0% of the time, Pallas kernels for 31%

profile of v5, /device:TPU:22, one launch (start us, length us, event | category | flops | bytes accessed | tf_op | source)
XLA Modules:
  0.0 75.8 jit_solution(3434192123188316655)
XLA Ops:
  0.0 7.4 %local_terms.4 = (f32[4,128,128]{2,1,0:T(8,128)S(1)}, f32[4,128,128]{2,1,0:T(8,128)S(1)}, f32[4,128,128]{2,1,0:T(8,128)}, f32[4,128,128]{2,1,0:T(8,128)}, bf16[1...) custom-call(s32[1]{0:T(128)S(6)} %mul.3.offset_ref, ...), custom_call_target="tpu_custom_call" | custom-call | tf_op jit(solution)/shard_map/local_terms/pallas_call | solution.py:258
  7.4 0.7 collective-permute-start
  8.1 6.7 %local_terms.5 = (f32[4,128,128]{2,1,0:T(8,128)S(1)}, f32[4,128,128]{2,1,0:T(8,128)S(1)}, f32[4,128,128]{2,1,0:T(8,128)}, f32[4,128,128]{2,1,0:T(8,128)}, bf16[1...) custom-call(s32[1]{0:T(128)S(6)} %mul.3.offset_ref, ...), custom_call_target="tpu_custom_call" | custom-call | tf_op jit(solution)/shard_map/local_terms/pallas_call | solution.py:258
  14.9 1.5 %collective-permute-start.1 = (f32[4,128,128]{2,1,0:T(8,128)S(1)}, f32[4,128,128]{2,1,0:T(8,128)S(1)}, u32[]{:S(2)}, u32[]{:S(2)}) collective-permute-start(f32[4,128,128]{2,1,0:T(8,128)S(1)} %state_step.5.refs_10_), channel_id=1, source_target_pairs={{0,4},{4,8},{1,5},{5,9},{2,6},{6,10},{3,7},{7,11},{16,20},{20,24},... | collective-permute-start | bytes 786440 | tf_op jit(solution)/shard_map/ppermute | solution.py:372
  16.3 6.7 %local_terms.6 = (f32[4,128,128]{2,1,0:T(8,128)S(1)}, f32[4,128,128]{2,1,0:T(8,128)S(1)}, f32[4,128,128]{2,1,0:T(8,128)}, f32[4,128,128]{2,1,0:T(8,128)}, bf16[1...) custom-call(s32[1]{0:T(128)S(6)} %mul.3.offset_ref, ...), custom_call_target="tpu_custom_call" | custom-call | tf_op jit(solution)/shard_map/local_terms/pallas_call | solution.py:258
  23.1 2.3 %collective-permute-done.1.refs_6_.refs_1_.refs_0_ = f32[4,128,128]{2,1,0:T(8,128)S(1)} collective-permute-done((f32[4,128,128]{2,1,0:T(8,128)S(1)}, f32[4,128,128]{2,1,0:T(8,128)S(1)}, u32[]{:S(2)}, u32[]{:S(2)}) %collective-permute-start.1) | collective-permute-done | bytes 262176 | tf_op jit(solution)/shard_map/ppermute | solution.py:372
  25.4 0.3 state_step.6.refs_5_
  25.7 2.1 %collective-permute-start.2 = (f32[4,128,128]{2,1,0:T(8,128)S(1)}, f32[4,128,128]{2,1,0:T(8,128)S(1)}, u32[]{:S(2)}, u32[]{:S(2)}) collective-permute-start(f32[4,128,128]{2,1,0:T(8,128)S(1)} %state_step.6.refs_5_), channel_id=1, source_target_pairs={{0,4},{4,8},{8,12},{1,5},{5,9},{9,13},{2,6},{6,10},{10,14},{3,7},{... | collective-permute-start | bytes 786440 | tf_op jit(solution)/shard_map/ppermute | solution.py:372
  27.7 6.3 %local_terms.7 = (f32[4,128,128]{2,1,0:T(8,128)S(1)}, f32[4,128,128]{2,1,0:T(8,128)S(1)}, f32[4,128,128]{2,1,0:T(8,128)}, f32[4,128,128]{2,1,0:T(8,128)}) custom-call(s32[1]{0:T(128)S(6)} %mul.3.offset_ref, s32[4,3]{1,0:T(4,128)} %resets_ref.7, bf16[128,512]{1,0:T(8,128)(2,1)S(1)} %get-tuple-element.74.refs_0_, ...), custom_call_target="tpu_custom_call" | custom-call | tf_op jit(solution)/shard_map/local_terms/pallas_call | solution.py:258
  34.1 0.6 collective-permute-done.2.refs_6_.refs_2_.refs_1_.refs_0_
  34.7 1.0 %state_step.7.refs_4_ = f32[4,128,128]{2,1,0:T(8,128)} custom-call(s32[1]{0:T(128)} %bitcast.here_ref, f32[4,128,128]{2,1,0:T(8,128)S(1)} %get-tuple-element.79.refs_0_, f32[4,128,128]{2,1,0:T(8,128)S(1)} %get-tuple-element.72.refs_0_.refs_1_, f32[4,128,128]{2,1,0:T(8,128)S(1)} %get-tuple-element.64.refs_0_.refs_1_.refs_2_, ...), custom_call_target="tpu_custom_call" | custom-call | flops 1048576 | bytes 1024 | tf_op jit(solution)/shard_map/state_step/pallas_call | solution.py:296
  35.7 1.9 %collective-permute-start.5 = (f32[4,128,128]{2,1,0:T(8,128)}, f32[4,128,128]{2,1,0:T(8,128)S(1)}, u32[]{:S(2)}, u32[]{:S(2)}) collective-permute-start(f32[4,128,128]{2,1,0:T(8,128)} %state_step.7.refs_4_), channel_id=1, source_target_pairs={{0,4},{4,8},{8,12},{1,5},{5,9},{9,13},{2,6},{6,10},{10,14},{3,7},{... | collective-permute-start | bytes 786440 | tf_op jit(solution)/shard_map/ppermute | solution.py:372
  37.6 1.0 %copy-done.4 = f32[4,128,128]{2,1,0:T(8,128)S(1)} copy-done((f32[4,128,128]{2,1,0:T(8,128)S(1)}, f32[4,128,128]{2,1,0:T(8,128)}, u32[]{:S(2)}) %copy-start.4) | copy-done | bytes 262168
  38.6 0.9 %copy-done.6 = f32[4,128,128]{2,1,0:T(8,128)S(1)} copy-done((f32[4,128,128]{2,1,0:T(8,128)S(1)}, f32[4,128,128]{2,1,0:T(8,128)}, u32[]{:S(2)}) %copy-start.6) | copy-done | bytes 262168
  39.5 0.9 %copy-done.13 = f32[4,128,128]{2,1,0:T(8,128)S(1)} copy-done((f32[4,128,128]{2,1,0:T(8,128)S(1)}, f32[4,128,128]{2,1,0:T(8,128)}, u32[]{:S(2)}) %copy-start.13) | copy-done | bytes 262168
  40.5 0.9 %copy-done.14 = f32[4,128,128]{2,1,0:T(8,128)S(1)} copy-done((f32[4,128,128]{2,1,0:T(8,128)S(1)}, f32[4,128,128]{2,1,0:T(8,128)}, u32[]{:S(2)}) %copy-start.14) | copy-done | bytes 262168
  41.4 0.7 project.4
  42.2 0.1 collective-permute-start.3
  42.3 0.5 collective-permute-start.4
  42.8 1.4 %collective-permute-done.5.refs_4_.refs_2_.refs_1_.refs_0_ = f32[4,128,128]{2,1,0:T(8,128)S(1)} collective-permute-done((f32[4,128,128]{2,1,0:T(8,128)}, f32[4,128,128]{2,1,0:T(8,128)S(1)}, u32[]{:S(2)}, u32[]{:S(2)}) %collective-permute-start.5) | collective-permute-done | bytes 262176 | tf_op jit(solution)/shard_map/ppermute | solution.py:372
  44.2 0.3 state_step.8.refs_2_
  44.4 1.9 %collective-permute-start.9 = (f32[4,128,128]{2,1,0:T(8,128)S(1)}, f32[4,128,128]{2,1,0:T(8,128)S(1)}, u32[]{:S(2)}, u32[]{:S(2)}) collective-permute-start(f32[4,128,128]{2,1,0:T(8,128)S(1)} %state_step.8.refs_2_), channel_id=1, source_target_pairs={{4,8},{8,12},{5,9},{9,13},{6,10},{10,14},{7,11},{11,15},{20,24},{2... | collective-permute-start | bytes 786440 | tf_op jit(solution)/shard_map/ppermute | solution.py:372
  46.4 0.1 add_parts.4
  46.5 0.7 project.5
  47.2 0.1 collective-permute-start.7
  47.3 0.5 collective-permute-start.8
  47.8 0.5 collective-permute-start.6
  48.4 4.9 %collective-permute-done.9.refs_2_.refs_1_ = f32[4,128,128]{2,1,0:T(8,128)S(1)} collective-permute-done((f32[4,128,128]{2,1,0:T(8,128)S(1)}, f32[4,128,128]{2,1,0:T(8,128)S(1)}, u32[]{:S(2)}, u32[]{:S(2)}) %collective-permute-start.9) | collective-permute-done | bytes 262176 | tf_op jit(solution)/shard_map/ppermute | solution.py:372
  53.2 0.3 state_step.9.refs_2_
  53.5 2.0 %collective-permute-start.13 = (f32[4,128,128]{2,1,0:T(8,128)S(1)}, f32[4,128,128]{2,1,0:T(8,128)S(1)}, u32[]{:S(2)}, u32[]{:S(2)}) collective-permute-start(f32[4,128,128]{2,1,0:T(8,128)S(1)} %state_step.9.refs_2_), channel_id=1, source_target_pairs={{8,12},{9,13},{10,14},{11,15},{24,28},{25,29},{26,30},{27,31}} | collective-permute-start | bytes 786440 | tf_op jit(solution)/shard_map/ppermute | solution.py:372
  55.5 0.1 add_parts.5
  55.6 0.6 collective-permute-start.10
  56.2 0.8 project.6
  57.0 0.1 collective-permute-start.11
  57.0 0.5 collective-permute-start.12
  57.5 1.8 %collective-permute-done.13.refs_2_ = f32[4,128,128]{2,1,0:T(8,128)S(1)} collective-permute-done((f32[4,128,128]{2,1,0:T(8,128)S(1)}, f32[4,128,128]{2,1,0:T(8,128)S(1)}, u32[]{:S(2)}, u32[]{:S(2)}) %collective-permute-start.13) | collective-permute-done | bytes 262176 | tf_op jit(solution)/shard_map/ppermute | solution.py:372
  59.3 0.7 project.7
  60.1 0.1 collective-permute-start.15
  60.2 0.5 collective-permute-start.16
  60.7 0.1 add_parts.6
  60.7 0.6 collective-permute-start.14
  61.3 0.7 collective-permute-done.10
  62.0 0.0 collective-permute-done.16.refs_1_
  62.1 0.1 add_parts.7
  62.1 0.8 %collective-permute-start.17 = (f32[1,128,512]{2,1,0:T(8,128)S(1)}, f32[1,128,512]{2,1,0:T(8,128)S(1)}, u32[]{:S(2)}, u32[]{:S(2)}) collective-permute-start(f32[1,128,512]{2,1,0:T(8,128)S(1)} %get-tuple-element.106), channel_id=1, source_target_pairs={{0,2},{1,3},{2,0},{3,1},{4,6},{5,7},{6,4},{7,5},{8,10},{9,11},{10,... | collective-permute-start | bytes 786440 | tf_op jit(solution)/shard_map/ppermute | solution.py:367
  63.0 6.9 %collective-permute-done.14 = f32[1,128,512]{2,1,0:T(8,128)S(1)} collective-permute-done((f32[1,128,512]{2,1,0:T(8,128)S(1)}, f32[1,128,512]{2,1,0:T(8,128)S(1)}, u32[]{:S(2)}, u32[]{:S(2)}) %collective-permute-start.14) | collective-permute-done | bytes 262176 | tf_op jit(solution)/shard_map/ppermute | solution.py:367
  70.0 4.7 %collective-permute-done.17 = f32[1,128,512]{2,1,0:T(8,128)S(1)} collective-permute-done((f32[1,128,512]{2,1,0:T(8,128)S(1)}, f32[1,128,512]{2,1,0:T(8,128)S(1)}, u32[]{:S(2)}, u32[]{:S(2)}) %collective-permute-start.17) | collective-permute-done | bytes 262176 | tf_op jit(solution)/shard_map/ppermute | solution.py:367
  74.7 1.0 %pad_maximum_fusion = f32[4,128,512]{2,1,0:T(8,128)} fusion(f32[1,128,512]{2,1,0:T(8,128)S(1)} %add.21, f32[1,128,512]{2,1,0:T(8,128)S(1)} %add.20, f32[1,128,512]{2,1,0:T(8,128)S(1)} %add.19, f32[1,128,512]{2,1,0:T(8,128)S(1)} %add.18), kind=kLoop, calls=%fused_computation | loop fusion | flops 786432 | bytes 2097152 | tf_op jit(solution)/shard_map/stack | solution.py:495
  (40 shorter events, 0.3 us)
Async XLA Ops:
  7.4 7.4 %collective-permute-start = (f32[4,128,128]{2,1,0:T(8,128)S(1)}, f32[4,128,128]{2,1,0:T(8,128)S(1)}, u32[]{:S(2)}, u32[]{:S(2)}) collective-permute-start(f32[4,128,128]{2,1,0:T(8,128)S(1)} %get-tuple-element.58.refs_10_.refs_3_.refs_5_), channel_id=1, source_target_pairs={{0,4},{1,5},{2,6},{3,7},{16,20},{17,21},{18,22},{19,23}} | collective-permute-start | bytes 786440 | tf_op jit(solution)/shard_map/ppermute | solution.py:372
  14.8 1.5 %copy-start.5 = (f32[4,128,128]{2,1,0:T(8,128)}, f32[4,128,128]{2,1,0:T(8,128)S(1)}, u32[]{:S(2)}) copy-start(f32[4,128,128]{2,1,0:T(8,128)S(1)} %collective-permute-done.refs_4_.refs_0_) | copy-start | bytes 786436
  14.9 10.5 %collective-permute-start.1 = (f32[4,128,128]{2,1,0:T(8,128)S(1)}, f32[4,128,128]{2,1,0:T(8,128)S(1)}, u32[]{:S(2)}, u32[]{:S(2)}) collective-permute-start(f32[4,128,128]{2,1,0:T(8,128)S(1)} %state_step.5.refs_10_), channel_id=1, source_target_pairs={{0,4},{4,8},{1,5},{5,9},{2,6},{6,10},{3,7},{7,11},{16,20},{20,24},... | collective-permute-start | bytes 786440 | tf_op jit(solution)/shard_map/ppermute | solution.py:372
  25.4 2.4 %copy-start.3 = (f32[4,128,128]{2,1,0:T(8,128)}, f32[4,128,128]{2,1,0:T(8,128)S(1)}, u32[]{:S(2)}) copy-start(f32[4,128,128]{2,1,0:T(8,128)S(1)} %collective-permute-done.1.refs_6_.refs_1_.refs_0_) | copy-start | bytes 786436
  25.7 11.9 %copy-start = (bf16[512,2048]{1,0:T(8,128)(2,1)S(1)}, bf16[512,2048]{1,0:T(8,128)(2,1)}, u32[]{:S(2)}) copy-start(bf16[512,2048]{1,0:T(8,128)(2,1)} %refs_3_.9) | copy-start | bytes 6291460
  25.7 9.0 %collective-permute-start.2 = (f32[4,128,128]{2,1,0:T(8,128)S(1)}, f32[4,128,128]{2,1,0:T(8,128)S(1)}, u32[]{:S(2)}, u32[]{:S(2)}) collective-permute-start(f32[4,128,128]{2,1,0:T(8,128)S(1)} %state_step.6.refs_5_), channel_id=1, source_target_pairs={{0,4},{4,8},{8,12},{1,5},{5,9},{9,13},{2,6},{6,10},{10,14},{3,7},{... | collective-permute-start | bytes 786440 | tf_op jit(solution)/shard_map/ppermute | solution.py:372
  34.1 1.6 %copy-start.1 = (f32[4,128,128]{2,1,0:T(8,128)}, f32[4,128,128]{2,1,0:T(8,128)S(1)}, u32[]{:S(2)}) copy-start(f32[4,128,128]{2,1,0:T(8,128)S(1)} %get-tuple-element.79.refs_0_) | copy-start | bytes 786436
  35.7 8.5 %collective-permute-start.5 = (f32[4,128,128]{2,1,0:T(8,128)}, f32[4,128,128]{2,1,0:T(8,128)S(1)}, u32[]{:S(2)}, u32[]{:S(2)}) collective-permute-start(f32[4,128,128]{2,1,0:T(8,128)} %state_step.7.refs_4_), channel_id=1, source_target_pairs={{0,4},{4,8},{8,12},{1,5},{5,9},{9,13},{2,6},{6,10},{10,14},{3,7},{... | collective-permute-start | bytes 786440 | tf_op jit(solution)/shard_map/ppermute | solution.py:372
  37.6 6.6 %copy-start.2 = (f32[4,128,128]{2,1,0:T(8,128)S(1)}, f32[4,128,128]{2,1,0:T(8,128)}, u32[]{:S(2)}) copy-start(f32[4,128,128]{2,1,0:T(8,128)} %copy-done.1) | copy-start | bytes 786436
  37.6 1.0 %copy-start.4 = (f32[4,128,128]{2,1,0:T(8,128)S(1)}, f32[4,128,128]{2,1,0:T(8,128)}, u32[]{:S(2)}) copy-start(f32[4,128,128]{2,1,0:T(8,128)} %copy-done.3) | copy-start | bytes 786436
  38.6 0.9 %copy-start.6 = (f32[4,128,128]{2,1,0:T(8,128)S(1)}, f32[4,128,128]{2,1,0:T(8,128)}, u32[]{:S(2)}) copy-start(f32[4,128,128]{2,1,0:T(8,128)} %copy-done.5) | copy-start | bytes 786436
  39.5 0.9 %copy-start.13 = (f32[4,128,128]{2,1,0:T(8,128)S(1)}, f32[4,128,128]{2,1,0:T(8,128)}, u32[]{:S(2)}) copy-start(f32[4,128,128]{2,1,0:T(8,128)} %get-tuple-element.56.reach_ref) | copy-start | bytes 786436
  40.5 0.9 %copy-start.14 = (f32[4,128,128]{2,1,0:T(8,128)S(1)}, f32[4,128,128]{2,1,0:T(8,128)}, u32[]{:S(2)}) copy-start(f32[4,128,128]{2,1,0:T(8,128)} %get-tuple-element.57.own_ref) | copy-start | bytes 786436
  42.2 4.3 %copy-start.11 = (f32[4,128,128]{2,1,0:T(8,128)S(1)}, f32[4,128,128]{2,1,0:T(8,128)}, u32[]{:S(2)}) copy-start(f32[4,128,128]{2,1,0:T(8,128)} %get-tuple-element.86.reach_ref) | copy-start | bytes 786436
  42.2 4.3 %copy-start.12 = (f32[4,128,128]{2,1,0:T(8,128)S(1)}, f32[4,128,128]{2,1,0:T(8,128)}, u32[]{:S(2)}) copy-start(f32[4,128,128]{2,1,0:T(8,128)} %get-tuple-element.87.own_ref) | copy-start | bytes 786436
  42.2 4.2 %collective-permute-start.3 = (f32[128,512]{1,0:T(8,128)S(1)}, f32[128,512]{1,0:T(8,128)S(1)}, u32[]{:S(2)}, u32[]{:S(2)}) collective-permute-start(f32[128,512]{1,0:T(8,128)S(1)} %get-tuple-element.82), channel_id=1, source_target_pairs={{0,1},{1,0},{2,3},{3,2},{4,5},{5,4},{6,7},{7,6},{8,9},{9,8},{10,11... | collective-permute-start | bytes 786440 | tf_op jit(solution)/shard_map/ppermute | solution.py:367
  42.3 4.1 %collective-permute-start.4 = (f32[128,512]{1,0:T(8,128)S(1)}, f32[128,512]{1,0:T(8,128)S(1)}, u32[]{:S(2)}, u32[]{:S(2)}) collective-permute-start(f32[128,512]{1,0:T(8,128)S(1)} %get-tuple-element.83), channel_id=1, source_target_pairs={{0,1},{1,0},{2,3},{3,2},{4,5},{5,4},{6,7},{7,6},{8,9},{9,8},{10,11... | collective-permute-start | bytes 786440 | tf_op jit(solution)/shard_map/ppermute | solution.py:367
  44.4 8.8 %collective-permute-start.9 = (f32[4,128,128]{2,1,0:T(8,128)S(1)}, f32[4,128,128]{2,1,0:T(8,128)S(1)}, u32[]{:S(2)}, u32[]{:S(2)}) collective-permute-start(f32[4,128,128]{2,1,0:T(8,128)S(1)} %state_step.8.refs_2_), channel_id=1, source_target_pairs={{4,8},{8,12},{5,9},{9,13},{6,10},{10,14},{7,11},{11,15},{20,24},{2... | collective-permute-start | bytes 786440 | tf_op jit(solution)/shard_map/ppermute | solution.py:372
  47.2 9.0 %copy-start.9 = (f32[4,128,128]{2,1,0:T(8,128)S(1)}, f32[4,128,128]{2,1,0:T(8,128)}, u32[]{:S(2)}) copy-start(f32[4,128,128]{2,1,0:T(8,128)} %get-tuple-element.93.reach_ref) | copy-start | bytes 786436
  47.2 9.0 %copy-start.10 = (f32[4,128,128]{2,1,0:T(8,128)S(1)}, f32[4,128,128]{2,1,0:T(8,128)}, u32[]{:S(2)}) copy-start(f32[4,128,128]{2,1,0:T(8,128)} %get-tuple-element.94.own_ref) | copy-start | bytes 786436
  47.2 8.2 %collective-permute-start.7 = (f32[128,512]{1,0:T(8,128)S(1)}, f32[128,512]{1,0:T(8,128)S(1)}, u32[]{:S(2)}, u32[]{:S(2)}) collective-permute-start(f32[128,512]{1,0:T(8,128)S(1)} %get-tuple-element.89), channel_id=1, source_target_pairs={{0,1},{1,0},{2,3},{3,2},{4,5},{5,4},{6,7},{7,6},{8,9},{9,8},{10,11... | collective-permute-start | bytes 786440 | tf_op jit(solution)/shard_map/ppermute | solution.py:367
  47.3 8.2 %collective-permute-start.8 = (f32[128,512]{1,0:T(8,128)S(1)}, f32[128,512]{1,0:T(8,128)S(1)}, u32[]{:S(2)}, u32[]{:S(2)}) collective-permute-start(f32[128,512]{1,0:T(8,128)S(1)} %get-tuple-element.90), channel_id=1, source_target_pairs={{0,1},{1,0},{2,3},{3,2},{4,5},{5,4},{6,7},{7,6},{8,9},{9,8},{10,11... | collective-permute-start | bytes 786440 | tf_op jit(solution)/shard_map/ppermute | solution.py:367
  47.8 8.4 %collective-permute-start.6 = (f32[1,128,512]{2,1,0:T(8,128)S(1)}, f32[1,128,512]{2,1,0:T(8,128)S(1)}, u32[]{:S(2)}, u32[]{:S(2)}) collective-permute-start(f32[1,128,512]{2,1,0:T(8,128)S(1)} %get-tuple-element.85.refs_4_), channel_id=1, source_target_pairs={{0,2},{1,3},{2,0},{3,1},{4,6},{5,7},{6,4},{7,5},{8,10},{9,11},{10,... | collective-permute-start | bytes 786440 | tf_op jit(solution)/shard_map/ppermute | solution.py:367
  53.5 5.8 %collective-permute-start.13 = (f32[4,128,128]{2,1,0:T(8,128)S(1)}, f32[4,128,128]{2,1,0:T(8,128)S(1)}, u32[]{:S(2)}, u32[]{:S(2)}) collective-permute-start(f32[4,128,128]{2,1,0:T(8,128)S(1)} %state_step.9.refs_2_), channel_id=1, source_target_pairs={{8,12},{9,13},{10,14},{11,15},{24,28},{25,29},{26,30},{27,31}} | collective-permute-start | bytes 786440 | tf_op jit(solution)/shard_map/ppermute | solution.py:372
  55.6 3.8 %copy-start.7 = (f32[4,128,128]{2,1,0:T(8,128)S(1)}, f32[4,128,128]{2,1,0:T(8,128)}, u32[]{:S(2)}) copy-start(f32[4,128,128]{2,1,0:T(8,128)} %get-tuple-element.98.reach_ref) | copy-start | bytes 786436
  55.6 3.8 %copy-start.8 = (f32[4,128,128]{2,1,0:T(8,128)S(1)}, f32[4,128,128]{2,1,0:T(8,128)}, u32[]{:S(2)}) copy-start(f32[4,128,128]{2,1,0:T(8,128)} %get-tuple-element.99.own_ref) | copy-start | bytes 786436
  55.6 6.4 %collective-permute-start.10 = (f32[1,128,512]{2,1,0:T(8,128)S(1)}, f32[1,128,512]{2,1,0:T(8,128)S(1)}, u32[]{:S(2)}, u32[]{:S(2)}) collective-permute-start(f32[1,128,512]{2,1,0:T(8,128)S(1)} %get-tuple-element.92.refs_4_), channel_id=1, source_target_pairs={{0,2},{1,3},{2,0},{3,1},{4,6},{5,7},{6,4},{7,5},{8,10},{9,11},{10,... | collective-permute-start | bytes 786440 | tf_op jit(solution)/shard_map/ppermute | solution.py:367
  57.0 3.7 %collective-permute-start.11 = (f32[128,512]{1,0:T(8,128)S(1)}, f32[128,512]{1,0:T(8,128)S(1)}, u32[]{:S(2)}, u32[]{:S(2)}) collective-permute-start(f32[128,512]{1,0:T(8,128)S(1)} %get-tuple-element.96), channel_id=1, source_target_pairs={{0,1},{1,0},{2,3},{3,2},{4,5},{5,4},{6,7},{7,6},{8,9},{9,8},{10,11... | collective-permute-start | bytes 786440 | tf_op jit(solution)/shard_map/ppermute | solution.py:367
  57.0 3.6 %collective-permute-start.12 = (f32[128,512]{1,0:T(8,128)S(1)}, f32[128,512]{1,0:T(8,128)S(1)}, u32[]{:S(2)}, u32[]{:S(2)}) collective-permute-start(f32[128,512]{1,0:T(8,128)S(1)} %get-tuple-element.97), channel_id=1, source_target_pairs={{0,1},{1,0},{2,3},{3,2},{4,5},{5,4},{6,7},{7,6},{8,9},{9,8},{10,11... | collective-permute-start | bytes 786440 | tf_op jit(solution)/shard_map/ppermute | solution.py:367
  60.1 1.9 %collective-permute-start.15 = (f32[128,512]{1,0:T(8,128)S(1)}, f32[128,512]{1,0:T(8,128)S(1)}, u32[]{:S(2)}, u32[]{:S(2)}) collective-permute-start(f32[128,512]{1,0:T(8,128)S(1)} %get-tuple-element.103), channel_id=1, source_target_pairs={{0,1},{1,0},{2,3},{3,2},{4,5},{5,4},{6,7},{7,6},{8,9},{9,8},{10,11... | collective-permute-start | bytes 786440 | tf_op jit(solution)/shard_map/ppermute | solution.py:367
  60.2 1.9 %collective-permute-start.16 = (f32[128,512]{1,0:T(8,128)S(1)}, f32[128,512]{1,0:T(8,128)S(1)}, u32[]{:S(2)}, u32[]{:S(2)}) collective-permute-start(f32[128,512]{1,0:T(8,128)S(1)} %get-tuple-element.104), channel_id=1, source_target_pairs={{0,1},{1,0},{2,3},{3,2},{4,5},{5,4},{6,7},{7,6},{8,9},{9,8},{10,11... | collective-permute-start | bytes 786440 | tf_op jit(solution)/shard_map/ppermute | solution.py:367
  60.7 9.2 %collective-permute-start.14 = (f32[1,128,512]{2,1,0:T(8,128)S(1)}, f32[1,128,512]{2,1,0:T(8,128)S(1)}, u32[]{:S(2)}, u32[]{:S(2)}) collective-permute-start(f32[1,128,512]{2,1,0:T(8,128)S(1)} %get-tuple-element.102.refs_2_), channel_id=1, source_target_pairs={{0,2},{1,3},{2,0},{3,1},{4,6},{5,7},{6,4},{7,5},{8,10},{9,11},{10,... | collective-permute-start | bytes 786440 | tf_op jit(solution)/shard_map/ppermute | solution.py:367
  62.1 12.6 %collective-permute-start.17 = (f32[1,128,512]{2,1,0:T(8,128)S(1)}, f32[1,128,512]{2,1,0:T(8,128)S(1)}, u32[]{:S(2)}, u32[]{:S(2)}) collective-permute-start(f32[1,128,512]{2,1,0:T(8,128)S(1)} %get-tuple-element.106), channel_id=1, source_target_pairs={{0,2},{1,3},{2,0},{3,1},{4,6},{5,7},{6,4},{7,5},{8,10},{9,11},{10,... | collective-permute-start | bytes 786440 | tf_op jit(solution)/shard_map/ppermute | solution.py:367

commit v6 on v5

--- a/solution.py
+++ b/solution.py
@@ -8,6 +8,7 @@
 from jax.sharding import PartitionSpec as P
 
 epsilon = 1e-06
+log2_e = 1.4426950408889634
 small_cost = pl.CostEstimate(flops=1 << 20, transcendentals=0, bytes_accessed=1 << 10)
 f32 = jnp.float32
 bf16 = jnp.bfloat16
@@ -101,12 +102,12 @@
     for copy in arrivals:
         copy.wait()
     gate3 = stacked(gate_ref[...])
-    gs_row = folded(mm(gate3, (tok_i <= (key_i >> 1)).astype(f32).astype(bf16)))
+    gs_row = log2_e * folded(mm(gate3, (tok_i <= (key_i >> 1)).astype(f32).astype(bf16)))
     beta_row = folded(
         mm(stacked(beta_ref[0]), (key_i == 2 * tok_i).astype(f32).astype(bf16))
         + mm(stacked(beta_ref[1]), (key_i == 2 * tok_i + 1).astype(f32).astype(bf16))
     )
-    gs_tok_row = folded(
+    gs_tok_row = log2_e * folded(
         mm(gate3, (iota((tok, tok), 0) <= iota((tok, tok), 1)).astype(f32).astype(bf16))
     )
     gs_col, beta_col, gs_tok = gs_row.T, beta_row.T, gs_tok_row.T
@@ -136,40 +137,53 @@
     def unit(x):
         return lax.rsqrt(jnp.sum(x * x, axis=1, keepdims=True) + epsilon)
 
-    top, bottom, k_col, k_row, right = [], [], [], [], []
-    for h in heads:
-        gram_top = mm_nt(k[h][:half], k[h][:half])
-        gram_bottom = mm_nt(k[h][half:], k[h])
-        k32 = k[h].astype(f32)
-        k_col.append(unit(k32))
-        squares = jnp.concatenate(
+    gram_top = [mm_nt(k[h][:half], k[h][:half]) for h in heads]
+    gram_bottom = [mm_nt(k[h][half:], k[h]) for h in heads]
+    squares = [
+        jnp.concatenate(
             [
                 jnp.sum(jnp.where(eye_half, g, 0.0), axis=0, keepdims=True)
-                for g in (gram_top, gram_bottom[:, half:])
+                for g in (gram_top[h], gram_bottom[h][:, half:])
             ],
             axis=1,
         )
-        k_row.append(lax.rsqrt(squares + epsilon))
+        for h in heads
+    ]
+    k_row = lax.rsqrt(jnp.concatenate(squares, axis=0) + epsilon)
+    k_col = k_row.T
+    left = beta_col * k_col
+    carried = left * jnp.where(doc_col == start_doc, jnp.exp2(gs_col), 0.0)
+    closing = k_col * jnp.where(doc_col == last_doc, jnp.exp2(gs_col[keys - 1:] - gs_col), 0.0)
+    one_top = eye_half.astype(f32)
+    one_bottom = jnp.concatenate([jnp.zeros((half, half), f32), one_top], axis=1)
+    top, bottom, right = [], [], []
+    for h in heads:
         gr, gc = gs_row[h:h + 1], gs_col[:, h:h + 1]
-        b_col = beta_col[:, h:h + 1]
-        left = b_col * k_col[h]
-        carried = jnp.where(doc_col == start_doc, jnp.exp(gc), 0.0)
+        kr, lc = k_row[h:h + 1], left[:, h:h + 1]
         right.append(
-            jnp.concatenate([k32 * (left * carried), v[h].astype(f32) * b_col], axis=1)
+            jnp.concatenate(
+                [
+                    k[h].astype(f32) * carried[:, h:h + 1],
+                    v[h].astype(f32) * beta_col[:, h:h + 1],
+                ],
+                axis=1,
+            )
         )
         top.append(
             split(
                 jnp.where(
                     top_mask,
-                    gram_top * jnp.exp(gc[:half] - gr[:, :half]) * k_row[h][:, :half] * left[:half],
-                    0.0,
+                    gram_top[h] * jnp.exp2(gc[:half] - gr[:, :half]) * kr[:, :half] * lc[:half],
+                    one_top,
                 )
             )
         )
         bottom.append(
             split(
                 jnp.where(
-                    bottom_mask, gram_bottom * jnp.exp(gc[half:] - gr) * k_row[h] * left[half:], 0.0
+                    bottom_mask,
+                    gram_bottom[h] * jnp.exp2(gc[half:] - gr) * kr * lc[half:],
+                    one_bottom,
                 )
             )
         )
@@ -197,34 +211,40 @@
         rough = right[h].astype(bf16)
         g_top = mm(inv[h, 0], rough[:half]).astype(bf16)
         g_bottom = mm(lower[h], rough).astype(bf16)
-        guess = jnp.concatenate([g_top, g_bottom], axis=0)
-        rest_top = right[h][:half] - g_top.astype(f32) - (
-            mm(top[h][0], g_top) + mm(top[h][1], g_top)
-        )
-        rest_bottom = right[h][half:] - g_bottom.astype(f32) - (
-            mm(bottom[h][0], guess) + mm(bottom[h][1], guess)
-        )
-        rest = jnp.concatenate([rest_top.astype(bf16), rest_bottom.astype(bf16)], axis=0)
+        rest_top = right[h][:half] - mm(
+            jnp.concatenate(top[h], axis=1), jnp.concatenate([g_top, g_top], axis=0)
+        )
+        rest_bottom = right[h][half:] - mm(
+            jnp.concatenate(bottom[h], axis=1),
+            jnp.concatenate([g_top, g_bottom, g_top, g_bottom], axis=0),
+        )
+        rest_top, rest_bottom = rest_top.astype(bf16), rest_bottom.astype(bf16)
         both.append(
             jnp.concatenate(
                 [
-                    g_top.astype(f32) + mm(inv[h, 0], rest[:half]),
-                    g_bottom.astype(f32) + mm(lower[h], rest),
+                    mm(
+                        jnp.concatenate([inv[h, 0], eye16], axis=1),
+                        jnp.concatenate([rest_top, g_top], axis=0),
+                    ),
+                    mm(
+                        jnp.concatenate([lower[h], eye16], axis=1),
+                        jnp.concatenate([rest_top, rest_bottom, g_bottom], axis=0),
+                    ),
                 ],
                 axis=0,
             )
         )
 
+    carried_tok = jnp.where(doc_tok == start_doc, jnp.exp2(gs_tok), 0.0)
     for h in heads:
         gr, gt = gs_row[h:h + 1], gs_tok[:, h:h + 1]
-        carried_tok = jnp.where(doc_tok == start_doc, jnp.exp(gt), 0.0)
         q32 = q[h].astype(f32)
         q_norm = unit(q32)
         probes = jnp.where(
-            tok_linked, mm_nt(q[h], k[h]) * jnp.exp(gt - gr) * k_row[h] * q_norm, 0.0
+            tok_linked, mm_nt(q[h], k[h]) * jnp.exp2(gt - gr) * k_row[h:h + 1] * q_norm, 0.0
         )
         outs = dot3(probes, both[h])
-        reach_ref[h] = (carried_tok * q_norm) * q32 - outs[:, :size]
+        reach_ref[h] = (carried_tok[:, h:h + 1] * q_norm) * q32 - outs[:, :size]
         own_ref[h] = outs[:, size:]
     departures = [
         pltpu.make_async_copy(reach_ref, reach_hbm, sems.at[10]),
@@ -233,11 +253,9 @@
     for copy in departures:
         copy.start()
     for h in heads:
-        last = gs_row[h:h + 1, keys - 1:]
-        closing = jnp.where(doc_col == last_doc, jnp.exp(last - gs_col[:, h:h + 1]), 0.0)
-        end_high, end_low = split(both[h] * (closing * k_col[h]))
+        end_high, end_low = split(both[h] * closing[:, h:h + 1])
         ends = mm_tn(k[h], end_high) + mm_tn(k[h], end_low)
-        keep = jnp.where(last_doc == start_doc, jnp.exp(last), 0.0)
+        keep = jnp.where(last_doc == start_doc, jnp.exp2(gs_row[h:h + 1, keys - 1:]), 0.0)
         transit_ref[h] = keep * eye_size - ends[:, :size]
         filled_ref[h] = ends[:, size:]
     for copy in departures + ahead_copies:

time: 77.2 us -> 76.4 us (0.990)
  Pallas kernels: 32.1 us -> 30.4 us
  waiting for transfers between devices: 23.3 us -> 24.3 us
    pallas_call x4, Pallas kernels: 27.1 us -> 25.4 us  [local_terms(): pl.pallas_call(functools.partial(local_kernel, head_count, seq, fetch, ah...]
    ppermute x6, waiting for transfers between devices: 11 us -> 12 us  [carry_on(): return lax.ppermute(x, 'seq', pairs)]
  transfers between devices with their start and end apart: 18 -> 18, of which waited for: 8 -> 8; matrix products, arithmetic and copies ran while one was open for 0% -> 0% of each run, Pallas kernels for 31% -> 29%
where the time goes in v6:
time: 76.4 us; the launch traced here: 75.1 us
  Pallas kernels  30.4 us (40%)
  waiting for transfers between devices  24.3 us (32%)
  starting transfers between devices  14.8 us (19%)
  local copies, waits for them, and re-layouts  3.88 us (5%)
  other arithmetic  1.18 us (2%)
    pallas_call x4, Pallas kernels, local_terms(): pl.pallas_call(functools.partial(local_kernel, head_count, seq, fetch, ah...  25.4 us
    ppermute x12, waiting for transfers between devices, swapped(): return lax.ppermute(x, axis, [(i, i ^ bit) for i in range(size)])  12.4 us
    ppermute x6, waiting for transfers between devices, carry_on(): return lax.ppermute(x, 'seq', pairs)  12 us
    ppermute x6, starting transfers between devices, carry_on(): return lax.ppermute(x, 'seq', pairs)  10 us
    ppermute x12, starting transfers between devices, swapped(): return lax.ppermute(x, axis, [(i, i ^ bit) for i in range(size)])  4.83 us
    unnamed x30, local copies, waits for them, and re-layouts  3.88 us
    pallas_call x4, Pallas kernels, project(): pl.pallas_call(functools.partial(project_kernel, len(states), groups), in...  2.95 us
    pallas_call x5, Pallas kernels, step(): pl.pallas_call(functools.partial(step_kernel, len(maps)), in_specs=[pl.Bl...  1.81 us
  transfers between devices with their start and end apart: 18, of which 8 were waited for; matrix products, arithmetic and copies ran while one was open for 0% of the time, Pallas kernels for 29%

profile of v6, /device:TPU:22, one launch (start us, length us, event | category | flops | bytes accessed | tf_op | source)
XLA Modules:
  0.0 75.1 jit_solution(16796164118143551305)
XLA Ops:
  0.0 7.1 %local_terms.4 = (f32[4,128,128]{2,1,0:T(8,128)S(1)}, f32[4,128,128]{2,1,0:T(8,128)S(1)}, f32[4,128,128]{2,1,0:T(8,128)}, f32[4,128,128]{2,1,0:T(8,128)}, bf16[1...) custom-call(s32[1]{0:T(128)S(6)} %mul.3.offset_ref, ...), custom_call_target="tpu_custom_call" | custom-call | tf_op jit(solution)/shard_map/local_terms/pallas_call | solution.py:276
  7.1 0.7 collective-permute-start
  7.8 6.1 %local_terms.5 = (f32[4,128,128]{2,1,0:T(8,128)S(1)}, f32[4,128,128]{2,1,0:T(8,128)S(1)}, f32[4,128,128]{2,1,0:T(8,128)}, f32[4,128,128]{2,1,0:T(8,128)}, bf16[1...) custom-call(s32[1]{0:T(128)S(6)} %mul.3.offset_ref, ...), custom_call_target="tpu_custom_call" | custom-call | tf_op jit(solution)/shard_map/local_terms/pallas_call | solution.py:276
  14.0 1.5 %collective-permute-start.1 = (f32[4,128,128]{2,1,0:T(8,128)S(1)}, f32[4,128,128]{2,1,0:T(8,128)S(1)}, u32[]{:S(2)}, u32[]{:S(2)}) collective-permute-start(f32[4,128,128]{2,1,0:T(8,128)S(1)} %state_step.5.refs_10_), channel_id=1, source_target_pairs={{0,4},{4,8},{1,5},{5,9},{2,6},{6,10},{3,7},{7,11},{16,20},{20,24},... | collective-permute-start | bytes 786440 | tf_op jit(solution)/shard_map/ppermute | solution.py:390
  15.5 6.1 %local_terms.6 = (f32[4,128,128]{2,1,0:T(8,128)S(1)}, f32[4,128,128]{2,1,0:T(8,128)S(1)}, f32[4,128,128]{2,1,0:T(8,128)}, f32[4,128,128]{2,1,0:T(8,128)}, bf16[1...) custom-call(s32[1]{0:T(128)S(6)} %mul.3.offset_ref, ...), custom_call_target="tpu_custom_call" | custom-call | tf_op jit(solution)/shard_map/local_terms/pallas_call | solution.py:276
  21.6 3.5 %collective-permute-done.1.refs_6_.refs_1_.refs_0_ = f32[4,128,128]{2,1,0:T(8,128)S(1)} collective-permute-done((f32[4,128,128]{2,1,0:T(8,128)S(1)}, f32[4,128,128]{2,1,0:T(8,128)S(1)}, u32[]{:S(2)}, u32[]{:S(2)}) %collective-permute-start.1) | collective-permute-done | bytes 262176 | tf_op jit(solution)/shard_map/ppermute | solution.py:390
  25.1 0.3 state_step.6.refs_5_
  25.4 2.1 %collective-permute-start.2 = (f32[4,128,128]{2,1,0:T(8,128)S(1)}, f32[4,128,128]{2,1,0:T(8,128)S(1)}, u32[]{:S(2)}, u32[]{:S(2)}) collective-permute-start(f32[4,128,128]{2,1,0:T(8,128)S(1)} %state_step.6.refs_5_), channel_id=1, source_target_pairs={{0,4},{4,8},{8,12},{1,5},{5,9},{9,13},{2,6},{6,10},{10,14},{3,7},{... | collective-permute-start | bytes 786440 | tf_op jit(solution)/shard_map/ppermute | solution.py:390
  27.5 6.1 %local_terms.7 = (f32[4,128,128]{2,1,0:T(8,128)S(1)}, f32[4,128,128]{2,1,0:T(8,128)S(1)}, f32[4,128,128]{2,1,0:T(8,128)}, f32[4,128,128]{2,1,0:T(8,128)}) custom-call(s32[1]{0:T(128)S(6)} %mul.3.offset_ref, s32[4,3]{1,0:T(4,128)} %resets_ref.7, bf16[128,512]{1,0:T(8,128)(2,1)S(1)} %get-tuple-element.74.refs_0_, ...), custom_call_target="tpu_custom_call" | custom-call | tf_op jit(solution)/shard_map/local_terms/pallas_call | solution.py:276
  33.6 0.4 collective-permute-done.2.refs_6_.refs_2_.refs_1_.refs_0_
  34.0 1.0 %state_step.7.refs_4_ = f32[4,128,128]{2,1,0:T(8,128)} custom-call(s32[1]{0:T(128)} %bitcast.here_ref, f32[4,128,128]{2,1,0:T(8,128)S(1)} %get-tuple-element.79.refs_0_, f32[4,128,128]{2,1,0:T(8,128)S(1)} %get-tuple-element.72.refs_0_.refs_1_, f32[4,128,128]{2,1,0:T(8,128)S(1)} %get-tuple-element.64.refs_0_.refs_1_.refs_2_, ...), custom_call_target="tpu_custom_call" | custom-call | flops 1048576 | bytes 1024 | tf_op jit(solution)/shard_map/state_step/pallas_call | solution.py:314
  34.9 1.9 %collective-permute-start.5 = (f32[4,128,128]{2,1,0:T(8,128)}, f32[4,128,128]{2,1,0:T(8,128)S(1)}, u32[]{:S(2)}, u32[]{:S(2)}) collective-permute-start(f32[4,128,128]{2,1,0:T(8,128)} %state_step.7.refs_4_), channel_id=1, source_target_pairs={{0,4},{4,8},{8,12},{1,5},{5,9},{9,13},{2,6},{6,10},{10,14},{3,7},{... | collective-permute-start | bytes 786440 | tf_op jit(solution)/shard_map/ppermute | solution.py:390
  36.9 1.0 %copy-done.4 = f32[4,128,128]{2,1,0:T(8,128)S(1)} copy-done((f32[4,128,128]{2,1,0:T(8,128)S(1)}, f32[4,128,128]{2,1,0:T(8,128)}, u32[]{:S(2)}) %copy-start.4) | copy-done | bytes 262168
  37.9 0.9 %copy-done.6 = f32[4,128,128]{2,1,0:T(8,128)S(1)} copy-done((f32[4,128,128]{2,1,0:T(8,128)S(1)}, f32[4,128,128]{2,1,0:T(8,128)}, u32[]{:S(2)}) %copy-start.6) | copy-done | bytes 262168
  38.8 0.9 %copy-done.13 = f32[4,128,128]{2,1,0:T(8,128)S(1)} copy-done((f32[4,128,128]{2,1,0:T(8,128)S(1)}, f32[4,128,128]{2,1,0:T(8,128)}, u32[]{:S(2)}) %copy-start.13) | copy-done | bytes 262168
  39.8 0.9 %copy-done.14 = f32[4,128,128]{2,1,0:T(8,128)S(1)} copy-done((f32[4,128,128]{2,1,0:T(8,128)S(1)}, f32[4,128,128]{2,1,0:T(8,128)}, u32[]{:S(2)}) %copy-start.14) | copy-done | bytes 262168
  40.7 0.7 project.4
  41.5 0.1 collective-permute-start.3
  41.6 0.5 collective-permute-start.4
  42.1 1.3 %collective-permute-done.5.refs_4_.refs_2_.refs_1_.refs_0_ = f32[4,128,128]{2,1,0:T(8,128)S(1)} collective-permute-done((f32[4,128,128]{2,1,0:T(8,128)}, f32[4,128,128]{2,1,0:T(8,128)S(1)}, u32[]{:S(2)}, u32[]{:S(2)}) %collective-permute-start.5) | collective-permute-done | bytes 262176 | tf_op jit(solution)/shard_map/ppermute | solution.py:390
  43.4 0.3 state_step.8.refs_2_
  43.7 1.9 %collective-permute-start.9 = (f32[4,128,128]{2,1,0:T(8,128)S(1)}, f32[4,128,128]{2,1,0:T(8,128)S(1)}, u32[]{:S(2)}, u32[]{:S(2)}) collective-permute-start(f32[4,128,128]{2,1,0:T(8,128)S(1)} %state_step.8.refs_2_), channel_id=1, source_target_pairs={{4,8},{8,12},{5,9},{9,13},{6,10},{10,14},{7,11},{11,15},{20,24},{2... | collective-permute-start | bytes 786440 | tf_op jit(solution)/shard_map/ppermute | solution.py:390
  45.6 0.1 add_parts.4
  45.7 0.7 project.5
  46.5 0.1 collective-permute-start.7
  46.6 0.5 collective-permute-start.8
  47.1 0.5 collective-permute-start.6
  47.6 4.9 %collective-permute-done.9.refs_2_.refs_1_ = f32[4,128,128]{2,1,0:T(8,128)S(1)} collective-permute-done((f32[4,128,128]{2,1,0:T(8,128)S(1)}, f32[4,128,128]{2,1,0:T(8,128)S(1)}, u32[]{:S(2)}, u32[]{:S(2)}) %collective-permute-start.9) | collective-permute-done | bytes 262176 | tf_op jit(solution)/shard_map/ppermute | solution.py:390
  52.5 0.3 state_step.9.refs_2_
  52.8 2.0 %collective-permute-start.13 = (f32[4,128,128]{2,1,0:T(8,128)S(1)}, f32[4,128,128]{2,1,0:T(8,128)S(1)}, u32[]{:S(2)}, u32[]{:S(2)}) collective-permute-start(f32[4,128,128]{2,1,0:T(8,128)S(1)} %state_step.9.refs_2_), channel_id=1, source_target_pairs={{8,12},{9,13},{10,14},{11,15},{24,28},{25,29},{26,30},{27,31}} | collective-permute-start | bytes 786440 | tf_op jit(solution)/shard_map/ppermute | solution.py:390
  54.8 0.1 add_parts.5
  54.9 0.6 collective-permute-start.10
  55.5 0.8 project.6
  56.2 0.1 collective-permute-start.11
  56.3 0.5 collective-permute-start.12
  56.8 1.8 %collective-permute-done.13.refs_2_ = f32[4,128,128]{2,1,0:T(8,128)S(1)} collective-permute-done((f32[4,128,128]{2,1,0:T(8,128)S(1)}, f32[4,128,128]{2,1,0:T(8,128)S(1)}, u32[]{:S(2)}, u32[]{:S(2)}) %collective-permute-start.13) | collective-permute-done | bytes 262176 | tf_op jit(solution)/shard_map/ppermute | solution.py:390
  58.6 0.7 project.7
  59.4 0.1 collective-permute-start.15
  59.5 0.5 collective-permute-start.16
  60.0 0.1 add_parts.6
  60.0 0.6 collective-permute-start.14
  60.6 0.7 collective-permute-done.10
  61.3 0.0 collective-permute-done.16.refs_1_
  61.4 0.1 add_parts.7
  61.4 0.8 %collective-permute-start.17 = (f32[1,128,512]{2,1,0:T(8,128)S(1)}, f32[1,128,512]{2,1,0:T(8,128)S(1)}, u32[]{:S(2)}, u32[]{:S(2)}) collective-permute-start(f32[1,128,512]{2,1,0:T(8,128)S(1)} %get-tuple-element.106), channel_id=1, source_target_pairs={{0,2},{1,3},{2,0},{3,1},{4,6},{5,7},{6,4},{7,5},{8,10},{9,11},{10,... | collective-permute-start | bytes 786440 | tf_op jit(solution)/shard_map/ppermute | solution.py:385
  62.3 6.9 %collective-permute-done.14 = f32[1,128,512]{2,1,0:T(8,128)S(1)} collective-permute-done((f32[1,128,512]{2,1,0:T(8,128)S(1)}, f32[1,128,512]{2,1,0:T(8,128)S(1)}, u32[]{:S(2)}, u32[]{:S(2)}) %collective-permute-start.14) | collective-permute-done | bytes 262176 | tf_op jit(solution)/shard_map/ppermute | solution.py:385
  69.3 4.7 %collective-permute-done.17 = f32[1,128,512]{2,1,0:T(8,128)S(1)} collective-permute-done((f32[1,128,512]{2,1,0:T(8,128)S(1)}, f32[1,128,512]{2,1,0:T(8,128)S(1)}, u32[]{:S(2)}, u32[]{:S(2)}) %collective-permute-start.17) | collective-permute-done | bytes 262176 | tf_op jit(solution)/shard_map/ppermute | solution.py:385
  74.0 1.0 %pad_maximum_fusion = f32[4,128,512]{2,1,0:T(8,128)} fusion(f32[1,128,512]{2,1,0:T(8,128)S(1)} %add.21, f32[1,128,512]{2,1,0:T(8,128)S(1)} %add.20, f32[1,128,512]{2,1,0:T(8,128)S(1)} %add.19, f32[1,128,512]{2,1,0:T(8,128)S(1)} %add.18), kind=kLoop, calls=%fused_computation | loop fusion | flops 786432 | bytes 2097152 | tf_op jit(solution)/shard_map/stack | solution.py:513
  (40 shorter events, 0.3 us)
Async XLA Ops:
  7.1 6.8 %collective-permute-start = (f32[4,128,128]{2,1,0:T(8,128)S(1)}, f32[4,128,128]{2,1,0:T(8,128)S(1)}, u32[]{:S(2)}, u32[]{:S(2)}) collective-permute-start(f32[4,128,128]{2,1,0:T(8,128)S(1)} %get-tuple-element.58.refs_10_.refs_3_.refs_5_), channel_id=1, source_target_pairs={{0,4},{1,5},{2,6},{3,7},{16,20},{17,21},{18,22},{19,23}} | collective-permute-start | bytes 786440 | tf_op jit(solution)/shard_map/ppermute | solution.py:390
  13.9 1.5 %copy-start.5 = (f32[4,128,128]{2,1,0:T(8,128)}, f32[4,128,128]{2,1,0:T(8,128)S(1)}, u32[]{:S(2)}) copy-start(f32[4,128,128]{2,1,0:T(8,128)S(1)} %collective-permute-done.refs_4_.refs_0_) | copy-start | bytes 786436
  14.0 11.1 %collective-permute-start.1 = (f32[4,128,128]{2,1,0:T(8,128)S(1)}, f32[4,128,128]{2,1,0:T(8,128)S(1)}, u32[]{:S(2)}, u32[]{:S(2)}) collective-permute-start(f32[4,128,128]{2,1,0:T(8,128)S(1)} %state_step.5.refs_10_), channel_id=1, source_target_pairs={{0,4},{4,8},{1,5},{5,9},{2,6},{6,10},{3,7},{7,11},{16,20},{20,24},... | collective-permute-start | bytes 786440 | tf_op jit(solution)/shard_map/ppermute | solution.py:390
  25.1 2.4 %copy-start.3 = (f32[4,128,128]{2,1,0:T(8,128)}, f32[4,128,128]{2,1,0:T(8,128)S(1)}, u32[]{:S(2)}) copy-start(f32[4,128,128]{2,1,0:T(8,128)S(1)} %collective-permute-done.1.refs_6_.refs_1_.refs_0_) | copy-start | bytes 786436
  25.4 11.5 %copy-start = (bf16[512,2048]{1,0:T(8,128)(2,1)S(1)}, bf16[512,2048]{1,0:T(8,128)(2,1)}, u32[]{:S(2)}) copy-start(bf16[512,2048]{1,0:T(8,128)(2,1)} %refs_3_.9) | copy-start | bytes 6291460
  25.4 8.5 %collective-permute-start.2 = (f32[4,128,128]{2,1,0:T(8,128)S(1)}, f32[4,128,128]{2,1,0:T(8,128)S(1)}, u32[]{:S(2)}, u32[]{:S(2)}) collective-permute-start(f32[4,128,128]{2,1,0:T(8,128)S(1)} %state_step.6.refs_5_), channel_id=1, source_target_pairs={{0,4},{4,8},{8,12},{1,5},{5,9},{9,13},{2,6},{6,10},{10,14},{3,7},{... | collective-permute-start | bytes 786440 | tf_op jit(solution)/shard_map/ppermute | solution.py:390
  33.6 1.4 %copy-start.1 = (f32[4,128,128]{2,1,0:T(8,128)}, f32[4,128,128]{2,1,0:T(8,128)S(1)}, u32[]{:S(2)}) copy-start(f32[4,128,128]{2,1,0:T(8,128)S(1)} %get-tuple-element.79.refs_0_) | copy-start | bytes 786436
  34.9 8.5 %collective-permute-start.5 = (f32[4,128,128]{2,1,0:T(8,128)}, f32[4,128,128]{2,1,0:T(8,128)S(1)}, u32[]{:S(2)}, u32[]{:S(2)}) collective-permute-start(f32[4,128,128]{2,1,0:T(8,128)} %state_step.7.refs_4_), channel_id=1, source_target_pairs={{0,4},{4,8},{8,12},{1,5},{5,9},{9,13},{2,6},{6,10},{10,14},{3,7},{... | collective-permute-start | bytes 786440 | tf_op jit(solution)/shard_map/ppermute | solution.py:390
  36.9 6.5 %copy-start.2 = (f32[4,128,128]{2,1,0:T(8,128)S(1)}, f32[4,128,128]{2,1,0:T(8,128)}, u32[]{:S(2)}) copy-start(f32[4,128,128]{2,1,0:T(8,128)} %copy-done.1) | copy-start | bytes 786436
  36.9 1.0 %copy-start.4 = (f32[4,128,128]{2,1,0:T(8,128)S(1)}, f32[4,128,128]{2,1,0:T(8,128)}, u32[]{:S(2)}) copy-start(f32[4,128,128]{2,1,0:T(8,128)} %copy-done.3) | copy-start | bytes 786436
  37.9 0.9 %copy-start.6 = (f32[4,128,128]{2,1,0:T(8,128)S(1)}, f32[4,128,128]{2,1,0:T(8,128)}, u32[]{:S(2)}) copy-start(f32[4,128,128]{2,1,0:T(8,128)} %copy-done.5) | copy-start | bytes 786436
  38.8 0.9 %copy-start.13 = (f32[4,128,128]{2,1,0:T(8,128)S(1)}, f32[4,128,128]{2,1,0:T(8,128)}, u32[]{:S(2)}) copy-start(f32[4,128,128]{2,1,0:T(8,128)} %get-tuple-element.56.reach_ref) | copy-start | bytes 786436
  39.8 0.9 %copy-start.14 = (f32[4,128,128]{2,1,0:T(8,128)S(1)}, f32[4,128,128]{2,1,0:T(8,128)}, u32[]{:S(2)}) copy-start(f32[4,128,128]{2,1,0:T(8,128)} %get-tuple-element.57.own_ref) | copy-start | bytes 786436
  41.5 4.2 %copy-start.11 = (f32[4,128,128]{2,1,0:T(8,128)S(1)}, f32[4,128,128]{2,1,0:T(8,128)}, u32[]{:S(2)}) copy-start(f32[4,128,128]{2,1,0:T(8,128)} %get-tuple-element.86.reach_ref) | copy-start | bytes 786436
  41.5 4.2 %copy-start.12 = (f32[4,128,128]{2,1,0:T(8,128)S(1)}, f32[4,128,128]{2,1,0:T(8,128)}, u32[]{:S(2)}) copy-start(f32[4,128,128]{2,1,0:T(8,128)} %get-tuple-element.87.own_ref) | copy-start | bytes 786436
  41.5 4.1 %collective-permute-start.3 = (f32[128,512]{1,0:T(8,128)S(1)}, f32[128,512]{1,0:T(8,128)S(1)}, u32[]{:S(2)}, u32[]{:S(2)}) collective-permute-start(f32[128,512]{1,0:T(8,128)S(1)} %get-tuple-element.82), channel_id=1, source_target_pairs={{0,1},{1,0},{2,3},{3,2},{4,5},{5,4},{6,7},{7,6},{8,9},{9,8},{10,11... | collective-permute-start | bytes 786440 | tf_op jit(solution)/shard_map/ppermute | solution.py:385
  41.6 4.0 %collective-permute-start.4 = (f32[128,512]{1,0:T(8,128)S(1)}, f32[128,512]{1,0:T(8,128)S(1)}, u32[]{:S(2)}, u32[]{:S(2)}) collective-permute-start(f32[128,512]{1,0:T(8,128)S(1)} %get-tuple-element.83), channel_id=1, source_target_pairs={{0,1},{1,0},{2,3},{3,2},{4,5},{5,4},{6,7},{7,6},{8,9},{9,8},{10,11... | collective-permute-start | bytes 786440 | tf_op jit(solution)/shard_map/ppermute | solution.py:385
  43.7 8.9 %collective-permute-start.9 = (f32[4,128,128]{2,1,0:T(8,128)S(1)}, f32[4,128,128]{2,1,0:T(8,128)S(1)}, u32[]{:S(2)}, u32[]{:S(2)}) collective-permute-start(f32[4,128,128]{2,1,0:T(8,128)S(1)} %state_step.8.refs_2_), channel_id=1, source_target_pairs={{4,8},{8,12},{5,9},{9,13},{6,10},{10,14},{7,11},{11,15},{20,24},{2... | collective-permute-start | bytes 786440 | tf_op jit(solution)/shard_map/ppermute | solution.py:390
  46.5 9.0 %copy-start.9 = (f32[4,128,128]{2,1,0:T(8,128)S(1)}, f32[4,128,128]{2,1,0:T(8,128)}, u32[]{:S(2)}) copy-start(f32[4,128,128]{2,1,0:T(8,128)} %get-tuple-element.93.reach_ref) | copy-start | bytes 786436
  46.5 9.0 %copy-start.10 = (f32[4,128,128]{2,1,0:T(8,128)S(1)}, f32[4,128,128]{2,1,0:T(8,128)}, u32[]{:S(2)}) copy-start(f32[4,128,128]{2,1,0:T(8,128)} %get-tuple-element.94.own_ref) | copy-start | bytes 786436
  46.5 8.3 %collective-permute-start.7 = (f32[128,512]{1,0:T(8,128)S(1)}, f32[128,512]{1,0:T(8,128)S(1)}, u32[]{:S(2)}, u32[]{:S(2)}) collective-permute-start(f32[128,512]{1,0:T(8,128)S(1)} %get-tuple-element.89), channel_id=1, source_target_pairs={{0,1},{1,0},{2,3},{3,2},{4,5},{5,4},{6,7},{7,6},{8,9},{9,8},{10,11... | collective-permute-start | bytes 786440 | tf_op jit(solution)/shard_map/ppermute | solution.py:385
  46.6 8.2 %collective-permute-start.8 = (f32[128,512]{1,0:T(8,128)S(1)}, f32[128,512]{1,0:T(8,128)S(1)}, u32[]{:S(2)}, u32[]{:S(2)}) collective-permute-start(f32[128,512]{1,0:T(8,128)S(1)} %get-tuple-element.90), channel_id=1, source_target_pairs={{0,1},{1,0},{2,3},{3,2},{4,5},{5,4},{6,7},{7,6},{8,9},{9,8},{10,11... | collective-permute-start | bytes 786440 | tf_op jit(solution)/shard_map/ppermute | solution.py:385
  47.1 8.4 %collective-permute-start.6 = (f32[1,128,512]{2,1,0:T(8,128)S(1)}, f32[1,128,512]{2,1,0:T(8,128)S(1)}, u32[]{:S(2)}, u32[]{:S(2)}) collective-permute-start(f32[1,128,512]{2,1,0:T(8,128)S(1)} %get-tuple-element.85.refs_4_), channel_id=1, source_target_pairs={{0,2},{1,3},{2,0},{3,1},{4,6},{5,7},{6,4},{7,5},{8,10},{9,11},{10,... | collective-permute-start | bytes 786440 | tf_op jit(solution)/shard_map/ppermute | solution.py:385
  52.8 5.8 %collective-permute-start.13 = (f32[4,128,128]{2,1,0:T(8,128)S(1)}, f32[4,128,128]{2,1,0:T(8,128)S(1)}, u32[]{:S(2)}, u32[]{:S(2)}) collective-permute-start(f32[4,128,128]{2,1,0:T(8,128)S(1)} %state_step.9.refs_2_), channel_id=1, source_target_pairs={{8,12},{9,13},{10,14},{11,15},{24,28},{25,29},{26,30},{27,31}} | collective-permute-start | bytes 786440 | tf_op jit(solution)/shard_map/ppermute | solution.py:390
  54.9 3.8 %copy-start.7 = (f32[4,128,128]{2,1,0:T(8,128)S(1)}, f32[4,128,128]{2,1,0:T(8,128)}, u32[]{:S(2)}) copy-start(f32[4,128,128]{2,1,0:T(8,128)} %get-tuple-element.98.reach_ref) | copy-start | bytes 786436
  54.9 3.8 %copy-start.8 = (f32[4,128,128]{2,1,0:T(8,128)S(1)}, f32[4,128,128]{2,1,0:T(8,128)}, u32[]{:S(2)}) copy-start(f32[4,128,128]{2,1,0:T(8,128)} %get-tuple-element.99.own_ref) | copy-start | bytes 786436
  54.9 6.4 %collective-permute-start.10 = (f32[1,128,512]{2,1,0:T(8,128)S(1)}, f32[1,128,512]{2,1,0:T(8,128)S(1)}, u32[]{:S(2)}, u32[]{:S(2)}) collective-permute-start(f32[1,128,512]{2,1,0:T(8,128)S(1)} %get-tuple-element.92.refs_4_), channel_id=1, source_target_pairs={{0,2},{1,3},{2,0},{3,1},{4,6},{5,7},{6,4},{7,5},{8,10},{9,11},{10,... | collective-permute-start | bytes 786440 | tf_op jit(solution)/shard_map/ppermute | solution.py:385
  56.2 3.7 %collective-permute-start.11 = (f32[128,512]{1,0:T(8,128)S(1)}, f32[128,512]{1,0:T(8,128)S(1)}, u32[]{:S(2)}, u32[]{:S(2)}) collective-permute-start(f32[128,512]{1,0:T(8,128)S(1)} %get-tuple-element.96), channel_id=1, source_target_pairs={{0,1},{1,0},{2,3},{3,2},{4,5},{5,4},{6,7},{7,6},{8,9},{9,8},{10,11... | collective-permute-start | bytes 786440 | tf_op jit(solution)/shard_map/ppermute | solution.py:385
  56.3 3.6 %collective-permute-start.12 = (f32[128,512]{1,0:T(8,128)S(1)}, f32[128,512]{1,0:T(8,128)S(1)}, u32[]{:S(2)}, u32[]{:S(2)}) collective-permute-start(f32[128,512]{1,0:T(8,128)S(1)} %get-tuple-element.97), channel_id=1, source_target_pairs={{0,1},{1,0},{2,3},{3,2},{4,5},{5,4},{6,7},{7,6},{8,9},{9,8},{10,11... | collective-permute-start | bytes 786440 | tf_op jit(solution)/shard_map/ppermute | solution.py:385
  59.4 1.9 %collective-permute-start.15 = (f32[128,512]{1,0:T(8,128)S(1)}, f32[128,512]{1,0:T(8,128)S(1)}, u32[]{:S(2)}, u32[]{:S(2)}) collective-permute-start(f32[128,512]{1,0:T(8,128)S(1)} %get-tuple-element.103), channel_id=1, source_target_pairs={{0,1},{1,0},{2,3},{3,2},{4,5},{5,4},{6,7},{7,6},{8,9},{9,8},{10,11... | collective-permute-start | bytes 786440 | tf_op jit(solution)/shard_map/ppermute | solution.py:385
  59.5 1.9 %collective-permute-start.16 = (f32[128,512]{1,0:T(8,128)S(1)}, f32[128,512]{1,0:T(8,128)S(1)}, u32[]{:S(2)}, u32[]{:S(2)}) collective-permute-start(f32[128,512]{1,0:T(8,128)S(1)} %get-tuple-element.104), channel_id=1, source_target_pairs={{0,1},{1,0},{2,3},{3,2},{4,5},{5,4},{6,7},{7,6},{8,9},{9,8},{10,11... | collective-permute-start | bytes 786440 | tf_op jit(solution)/shard_map/ppermute | solution.py:385
  60.0 9.2 %collective-permute-start.14 = (f32[1,128,512]{2,1,0:T(8,128)S(1)}, f32[1,128,512]{2,1,0:T(8,128)S(1)}, u32[]{:S(2)}, u32[]{:S(2)}) collective-permute-start(f32[1,128,512]{2,1,0:T(8,128)S(1)} %get-tuple-element.102.refs_2_), channel_id=1, source_target_pairs={{0,2},{1,3},{2,0},{3,1},{4,6},{5,7},{6,4},{7,5},{8,10},{9,11},{10,... | collective-permute-start | bytes 786440 | tf_op jit(solution)/shard_map/ppermute | solution.py:385
  61.4 12.6 %collective-permute-start.17 = (f32[1,128,512]{2,1,0:T(8,128)S(1)}, f32[1,128,512]{2,1,0:T(8,128)S(1)}, u32[]{:S(2)}, u32[]{:S(2)}) collective-permute-start(f32[1,128,512]{2,1,0:T(8,128)S(1)} %get-tuple-element.106), channel_id=1, source_target_pairs={{0,2},{1,3},{2,0},{3,1},{4,6},{5,7},{6,4},{7,5},{8,10},{9,11},{10,... | collective-permute-start | bytes 786440 | tf_op jit(solution)/shard_map/ppermute | solution.py:385

commit v7 on v6

--- a/solution.py
+++ b/solution.py
@@ -160,15 +160,6 @@
     for h in heads:
         gr, gc = gs_row[h:h + 1], gs_col[:, h:h + 1]
         kr, lc = k_row[h:h + 1], left[:, h:h + 1]
-        right.append(
-            jnp.concatenate(
-                [
-                    k[h].astype(f32) * carried[:, h:h + 1],
-                    v[h].astype(f32) * beta_col[:, h:h + 1],
-                ],
-                axis=1,
-            )
-        )
         top.append(
             split(
                 jnp.where(
@@ -191,7 +182,7 @@
     blocks = [(h, b) for h in heads for b in range(2)]
     part = {(h, b): top[h][0] if b == 0 else bottom[h][0][:, half:] for h, b in blocks}
     inv = {key: eye16 - part[key] * masks[0] for key in blocks}
-    for mask in masks[1:]:
+    for stage, mask in enumerate(masks[1:]):
         cross = {key: mm(inv[key], part[key] * mask).astype(bf16) for key in blocks}
         square = {key: mm(cross[key], cross[key]).astype(bf16) for key in blocks}
         near = {key: inv[key] - mm(cross[key], inv[key]).astype(bf16) for key in blocks}
@@ -199,6 +190,28 @@
             key: (near[key].astype(f32) + mm(square[key], near[key])).astype(bf16)
             for key in blocks
         }
+        if stage == 0:
+            for h in heads:
+                right.append(
+                    jnp.concatenate(
+                        [
+                            k[h].astype(f32) * carried[:, h:h + 1],
+                            v[h].astype(f32) * beta_col[:, h:h + 1],
+                        ],
+                        axis=1,
+                    )
+                )
+        if stage == 1:
+            probes, norms = [], []
+            for h in heads:
+                gr, gt = gs_row[h:h + 1], gs_tok[:, h:h + 1]
+                q_norm = unit(q[h].astype(f32))
+                norms.append(q_norm)
+                probes.append(
+                    jnp.where(
+                        tok_linked, mm_nt(q[h], k[h]) * jnp.exp2(gt - gr) * k_row[h:h + 1] * q_norm, 0.0
+                    )
+                )
     lower = []
     for h in heads:
         inner = mm(bottom[h][0][:, :half], inv[h, 0]).astype(bf16)
@@ -237,13 +250,9 @@
 
     carried_tok = jnp.where(doc_tok == start_doc, jnp.exp2(gs_tok), 0.0)
     for h in heads:
-        gr, gt = gs_row[h:h + 1], gs_tok[:, h:h + 1]
         q32 = q[h].astype(f32)
-        q_norm = unit(q32)
-        probes = jnp.where(
-            tok_linked, mm_nt(q[h], k[h]) * jnp.exp2(gt - gr) * k_row[h:h + 1] * q_norm, 0.0
-        )
-        outs = dot3(probes, both[h])
+        q_norm = norms[h]
+        outs = dot3(probes[h], both[h])
         reach_ref[h] = (carried_tok[:, h:h + 1] * q_norm) * q32 - outs[:, :size]
         own_ref[h] = outs[:, size:]
     departures = [
@@ -296,7 +305,9 @@
 
 
 def step_kernel(choices, here_ref, *refs):
-    maps, fills, state_ref, out_ref = refs[:choices], refs[choices:2 * choices], refs[2 * choices], refs[-1]
+    maps, fills, state_ref = refs[:choices], refs[choices:2 * choices], refs[2 * choices]
+    out_ref, mark_ref = refs[-2:]
+    mark_ref[...] = jnp.zeros_like(mark_ref)
     here = here_ref[0]
     for n in range(choices):
 
@@ -316,8 +327,8 @@
         in_specs=[pl.BlockSpec(memory_space=pltpu.SMEM)]
         + vmem(2 * len(maps) + 1)
         + untouched(earlier),
-        out_specs=pl.BlockSpec(memory_space=pltpu.VMEM),
-        out_shape=pltpu.VMEM(state.shape, f32),
+        out_specs=vmem(2),
+        out_shape=[pltpu.VMEM(state.shape, f32), pltpu.VMEM((8, 128), f32)],
         compiler_params=pltpu.CompilerParams(vmem_limit_bytes=8 << 20),
         cost_estimate=small_cost,
         name="state_step",
@@ -446,7 +457,7 @@
         def turn(_, incoming):
             return tuple(
                 lax.ppermute(
-                    step(no_choice, [terms[s][0]], [terms[s][1]], incoming[s]), "seq", pairs
+                    step(no_choice, [terms[s][0]], [terms[s][1]], incoming[s])[0], "seq", pairs
                 )
                 for s in range(chunks)
             )
@@ -492,20 +503,20 @@
             sent = terms[0][1]
         else:
             valid = [r - i for i in range(devices - 1) if 0 <= r - i < chunks]
-            sent = step(
+            sent, mark = step(
                 here - (r - valid[0]),
                 [terms[c][0] for c in valid],
                 [terms[c][1] for c in valid],
                 arrived[r - 1],
                 token,
             )
-            token = (sent,)
+            token = (mark,)
         arrived.append(carry_on(devices, sent, r, chunks))
         done = r - devices + 1
+        if done >= 0:
+            token = projected(done, token)
         if done >= 1:
             token = add_up(done - 1, token)
-        if done >= 0:
-            token = projected(done, token)
     done = last_round - devices + 2
     token = projected(done, token)
     token = add_up(done - 1, token)

time: 76.4 us -> 75.5 us (0.988)
  waiting for transfers between devices: 24.3 us -> 25.6 us
  local copies, waits for them, and re-layouts: 3.88 us -> 2.94 us
  Pallas kernels: 30.4 us -> 29.6 us
    ppermute x6, waiting for transfers between devices: 12 us -> 13 us  [carry_on(): return lax.ppermute(x, 'seq', pairs)]
    unnamed x30, local copies, waits for them, and re-layouts: 3.88 us -> 2.94 us
    pallas_call x4, Pallas kernels: 25.4 us -> 24.5 us  [local_terms(): pl.pallas_call(functools.partial(local_kernel, head_count, seq, fetch, ah...]
where the time goes in v7:
time: 75.5 us; the launch traced here: 74 us
  Pallas kernels  29.6 us (39%)
  waiting for transfers between devices  25.6 us (34%)
  starting transfers between devices  14.3 us (19%)
  local copies, waits for them, and re-layouts  2.94 us (4%)
  other arithmetic  1.2 us (2%)
    pallas_call x4, Pallas kernels, local_terms(): pl.pallas_call(functools.partial(local_kernel, head_count, seq, fetch, ah...  24.5 us
    ppermute x6, waiting for transfers between devices, carry_on(): return lax.ppermute(x, 'seq', pairs)  13 us
    ppermute x12, waiting for transfers between devices, swapped(): return lax.ppermute(x, axis, [(i, i ^ bit) for i in range(size)])  12.6 us
    ppermute x6, starting transfers between devices, carry_on(): return lax.ppermute(x, 'seq', pairs)  9.74 us
    ppermute x12, starting transfers between devices, swapped(): return lax.ppermute(x, axis, [(i, i ^ bit) for i in range(size)])  4.55 us
    pallas_call x4, Pallas kernels, project(): pl.pallas_call(functools.partial(project_kernel, len(states), groups), in...  2.97 us
    unnamed x30, local copies, waits for them, and re-layouts  2.94 us
    pallas_call x5, Pallas kernels, step(): pl.pallas_call(functools.partial(step_kernel, len(maps)), in_specs=[pl.Bl...  1.81 us
  transfers between devices with their start and end apart: 18, of which 8 were waited for; matrix products, arithmetic and copies ran while one was open for 0% of the time, Pallas kernels for 29%

profile of v7, /device:TPU:22, one launch (start us, length us, event | category | flops | bytes accessed | tf_op | source)
XLA Modules:
  0.0 74.0 jit_solution(13371765737643859151)
XLA Ops:
  0.0 6.9 %local_terms.4 = (f32[4,128,128]{2,1,0:T(8,128)S(1)}, f32[4,128,128]{2,1,0:T(8,128)S(1)}, f32[4,128,128]{2,1,0:T(8,128)}, f32[4,128,128]{2,1,0:T(8,128)}, bf16[1...) custom-call(s32[1]{0:T(128)S(6)} %mul.3.offset_ref, ...), custom_call_target="tpu_custom_call" | custom-call | tf_op jit(solution)/shard_map/local_terms/pallas_call | solution.py:285
  6.9 0.7 collective-permute-start
  7.6 5.9 %local_terms.5 = (f32[4,128,128]{2,1,0:T(8,128)S(1)}, f32[4,128,128]{2,1,0:T(8,128)S(1)}, f32[4,128,128]{2,1,0:T(8,128)}, f32[4,128,128]{2,1,0:T(8,128)}, bf16[1...) custom-call(s32[1]{0:T(128)S(6)} %mul.3.offset_ref, ...), custom_call_target="tpu_custom_call" | custom-call | tf_op jit(solution)/shard_map/local_terms/pallas_call | solution.py:285
  13.6 1.5 %collective-permute-start.1 = (f32[4,128,128]{2,1,0:T(8,128)S(1)}, f32[4,128,128]{2,1,0:T(8,128)S(1)}, u32[]{:S(2)}, u32[]{:S(2)}) collective-permute-start(f32[4,128,128]{2,1,0:T(8,128)S(1)} %get-tuple-element.77), channel_id=1, source_target_pairs={{0,4},{4,8},{1,5},{5,9},{2,6},{6,10},{3,7},{7,11},{16,20},{20,24},... | collective-permute-start | bytes 786440 | tf_op jit(solution)/shard_map/ppermute | solution.py:401
  15.0 5.9 %local_terms.6 = (f32[4,128,128]{2,1,0:T(8,128)S(1)}, f32[4,128,128]{2,1,0:T(8,128)S(1)}, f32[4,128,128]{2,1,0:T(8,128)}, f32[4,128,128]{2,1,0:T(8,128)}, bf16[1...) custom-call(s32[1]{0:T(128)S(6)} %mul.3.offset_ref, ...), custom_call_target="tpu_custom_call" | custom-call | tf_op jit(solution)/shard_map/local_terms/pallas_call | solution.py:285
  21.0 4.0 %collective-permute-done.1.refs_6_.refs_1_.refs_0_ = f32[4,128,128]{2,1,0:T(8,128)S(1)} collective-permute-done((f32[4,128,128]{2,1,0:T(8,128)S(1)}, f32[4,128,128]{2,1,0:T(8,128)S(1)}, u32[]{:S(2)}, u32[]{:S(2)}) %collective-permute-start.1) | collective-permute-done | bytes 262176 | tf_op jit(solution)/shard_map/ppermute | solution.py:401
  24.9 0.3 state_step.6
  25.2 2.1 %collective-permute-start.2 = (f32[4,128,128]{2,1,0:T(8,128)S(1)}, f32[4,128,128]{2,1,0:T(8,128)S(1)}, u32[]{:S(2)}, u32[]{:S(2)}) collective-permute-start(f32[4,128,128]{2,1,0:T(8,128)S(1)} %get-tuple-element.86), channel_id=1, source_target_pairs={{0,4},{4,8},{8,12},{1,5},{5,9},{9,13},{2,6},{6,10},{10,14},{3,7},{... | collective-permute-start | bytes 786440 | tf_op jit(solution)/shard_map/ppermute | solution.py:401
  27.3 5.8 %local_terms.7 = (f32[4,128,128]{2,1,0:T(8,128)S(1)}, f32[4,128,128]{2,1,0:T(8,128)S(1)}, f32[4,128,128]{2,1,0:T(8,128)}, f32[4,128,128]{2,1,0:T(8,128)}) custom-call(s32[1]{0:T(128)S(6)} %mul.3.offset_ref, s32[4,3]{1,0:T(4,128)} %resets_ref.7, bf16[128,512]{1,0:T(8,128)(2,1)S(1)} %get-tuple-element.87.refs_0_, ...), custom_call_target="tpu_custom_call" | custom-call | tf_op jit(solution)/shard_map/local_terms/pallas_call | solution.py:285
  33.1 0.6 collective-permute-done.2.refs_6_.refs_2_.refs_1_.refs_0_
  33.7 1.0 %state_step.7 = (f32[4,128,128]{2,1,0:T(8,128)}, f32[8,128]{1,0:T(8,128)S(1)}) custom-call(s32[1]{0:T(128)} %bitcast.here_ref, f32[4,128,128]{2,1,0:T(8,128)S(1)} %get-tuple-element.93.refs_0_, f32[4,128,128]{2,1,0:T(8,128)S(1)} %get-tuple-element.84.refs_0_.refs_1_, f32[4,128,128]{2,1,0:T(8,128)S(1)} %get-tuple-element.74.refs_0_.refs_1_.refs_2_, ...), custom_call_target="tpu_custom_call" | custom-call | flops 1048576 | bytes 1024 | tf_op jit(solution)/shard_map/state_step/pallas_call | solution.py:325
  34.7 1.9 %collective-permute-start.5 = (f32[4,128,128]{2,1,0:T(8,128)}, f32[4,128,128]{2,1,0:T(8,128)S(1)}, u32[]{:S(2)}, u32[]{:S(2)}) collective-permute-start(f32[4,128,128]{2,1,0:T(8,128)} %get-tuple-element.101), channel_id=1, source_target_pairs={{0,4},{4,8},{8,12},{1,5},{5,9},{9,13},{2,6},{6,10},{10,14},{3,7},{... | collective-permute-start | bytes 786440 | tf_op jit(solution)/shard_map/ppermute | solution.py:401
  36.7 1.0 %copy-done.6 = f32[4,128,128]{2,1,0:T(8,128)S(1)} copy-done((f32[4,128,128]{2,1,0:T(8,128)S(1)}, f32[4,128,128]{2,1,0:T(8,128)}, u32[]{:S(2)}) %copy-start.6) | copy-done | bytes 262168
  37.7 0.9 %copy-done.11 = f32[4,128,128]{2,1,0:T(8,128)S(1)} copy-done((f32[4,128,128]{2,1,0:T(8,128)S(1)}, f32[4,128,128]{2,1,0:T(8,128)}, u32[]{:S(2)}) %copy-start.11) | copy-done | bytes 262168
  38.7 0.9 %copy-done.12 = f32[4,128,128]{2,1,0:T(8,128)S(1)} copy-done((f32[4,128,128]{2,1,0:T(8,128)S(1)}, f32[4,128,128]{2,1,0:T(8,128)}, u32[]{:S(2)}) %copy-start.12) | copy-done | bytes 262168
  39.6 0.7 project.4
  40.3 0.1 collective-permute-start.3
  40.4 0.5 collective-permute-start.4
  40.9 2.3 %collective-permute-done.5.refs_4_.refs_2_.refs_1_.refs_0_ = f32[4,128,128]{2,1,0:T(8,128)S(1)} collective-permute-done((f32[4,128,128]{2,1,0:T(8,128)}, f32[4,128,128]{2,1,0:T(8,128)S(1)}, u32[]{:S(2)}, u32[]{:S(2)}) %collective-permute-start.5) | collective-permute-done | bytes 262176 | tf_op jit(solution)/shard_map/ppermute | solution.py:401
  43.2 0.3 state_step.8
  43.5 1.9 %collective-permute-start.9 = (f32[4,128,128]{2,1,0:T(8,128)S(1)}, f32[4,128,128]{2,1,0:T(8,128)S(1)}, u32[]{:S(2)}, u32[]{:S(2)}) collective-permute-start(f32[4,128,128]{2,1,0:T(8,128)S(1)} %get-tuple-element.110), channel_id=1, source_target_pairs={{4,8},{8,12},{5,9},{9,13},{6,10},{10,14},{7,11},{11,15},{20,24},{2... | collective-permute-start | bytes 786440 | tf_op jit(solution)/shard_map/ppermute | solution.py:401
  45.4 0.8 %project.5 = (f32[128,512]{1,0:T(8,128)S(1)}, f32[128,512]{1,0:T(8,128)S(1)}, f32[2,128,512]{2,1,0:T(8,128)S(1)}) custom-call(s32[1]{0:T(128)} %bitcast.here_ref, s32[1]{0:T(128)} %bitcast.1.place_ref, f32[4,128,128]{2,1,0:T(8,128)S(1)} %copy-done.9, f32[4,128,128]{2,1,0:T(8,128)S(1)} %copy-done.10, ...), custom_call_target="tpu_custom_call" | custom-call | flops 1048576 | bytes 1024 | tf_op jit(solution)/shard_map/project/pallas_call | solution.py:377
  46.2 0.0 collective-permute-done.4.refs_1_
  46.2 0.1 add_parts.4
  46.3 0.6 collective-permute-start.6
  46.9 0.5 collective-permute-start.8
  47.4 4.3 %collective-permute-done.9.refs_2_.refs_1_ = f32[4,128,128]{2,1,0:T(8,128)S(1)} collective-permute-done((f32[4,128,128]{2,1,0:T(8,128)S(1)}, f32[4,128,128]{2,1,0:T(8,128)S(1)}, u32[]{:S(2)}, u32[]{:S(2)}) %collective-permute-start.9) | collective-permute-done | bytes 262176 | tf_op jit(solution)/shard_map/ppermute | solution.py:401
  51.7 0.3 state_step.9
  52.0 1.7 %collective-permute-start.13 = (f32[4,128,128]{2,1,0:T(8,128)S(1)}, f32[4,128,128]{2,1,0:T(8,128)S(1)}, u32[]{:S(2)}, u32[]{:S(2)}) collective-permute-start(f32[4,128,128]{2,1,0:T(8,128)S(1)} %get-tuple-element.119), channel_id=1, source_target_pairs={{8,12},{9,13},{10,14},{11,15},{24,28},{25,29},{26,30},{27,31}} | collective-permute-start | bytes 786440 | tf_op jit(solution)/shard_map/ppermute | solution.py:401
  53.7 0.7 %project.6 = (f32[128,512]{1,0:T(8,128)S(1)}, f32[128,512]{1,0:T(8,128)S(1)}, f32[2,128,512]{2,1,0:T(8,128)S(1)}) custom-call(s32[1]{0:T(128)} %bitcast.here_ref, s32[1]{0:T(128)} %bitcast.1.place_ref, f32[4,128,128]{2,1,0:T(8,128)S(1)} %copy-done.7, f32[4,128,128]{2,1,0:T(8,128)S(1)} %copy-done.8, ...), custom_call_target="tpu_custom_call" | custom-call | flops 1048576 | bytes 1024 | tf_op jit(solution)/shard_map/project/pallas_call | solution.py:377
  54.5 0.0 collective-permute-done.7.refs_0_
  54.5 0.0 collective-permute-done.8.refs_1_
  54.5 0.1 add_parts.5
  54.6 0.6 collective-permute-start.10
  55.2 0.0 collective-permute-start.11
  55.2 0.5 collective-permute-start.12
  55.7 1.8 %collective-permute-done.13.refs_2_ = f32[4,128,128]{2,1,0:T(8,128)S(1)} collective-permute-done((f32[4,128,128]{2,1,0:T(8,128)S(1)}, f32[4,128,128]{2,1,0:T(8,128)S(1)}, u32[]{:S(2)}, u32[]{:S(2)}) %collective-permute-start.13) | collective-permute-done | bytes 262176 | tf_op jit(solution)/shard_map/ppermute | solution.py:401
  57.6 0.7 project.7
  58.3 0.1 collective-permute-start.15
  58.4 0.5 collective-permute-start.16
  58.9 0.1 add_parts.6
  59.0 0.6 collective-permute-start.14
  59.5 1.5 %collective-permute-done.10 = f32[1,128,512]{2,1,0:T(8,128)S(1)} collective-permute-done((f32[1,128,512]{2,1,0:T(8,128)S(1)}, f32[1,128,512]{2,1,0:T(8,128)S(1)}, u32[]{:S(2)}, u32[]{:S(2)}) %collective-permute-start.10) | collective-permute-done | bytes 262176 | tf_op jit(solution)/shard_map/ppermute | solution.py:396
  61.0 0.1 add_parts.7
  61.1 0.6 collective-permute-start.17
  61.8 6.4 %collective-permute-done.14 = f32[1,128,512]{2,1,0:T(8,128)S(1)} collective-permute-done((f32[1,128,512]{2,1,0:T(8,128)S(1)}, f32[1,128,512]{2,1,0:T(8,128)S(1)}, u32[]{:S(2)}, u32[]{:S(2)}) %collective-permute-start.14) | collective-permute-done | bytes 262176 | tf_op jit(solution)/shard_map/ppermute | solution.py:396
  68.2 4.7 %collective-permute-done.17 = f32[1,128,512]{2,1,0:T(8,128)S(1)} collective-permute-done((f32[1,128,512]{2,1,0:T(8,128)S(1)}, f32[1,128,512]{2,1,0:T(8,128)S(1)}, u32[]{:S(2)}, u32[]{:S(2)}) %collective-permute-start.17) | collective-permute-done | bytes 262176 | tf_op jit(solution)/shard_map/ppermute | solution.py:396
  73.0 1.0 %pad_maximum_fusion = f32[4,128,512]{2,1,0:T(8,128)} fusion(f32[1,128,512]{2,1,0:T(8,128)S(1)} %add.21, f32[1,128,512]{2,1,0:T(8,128)S(1)} %add.20, f32[1,128,512]{2,1,0:T(8,128)S(1)} %add.19, f32[1,128,512]{2,1,0:T(8,128)S(1)} %add.18), kind=kLoop, calls=%fused_computation | loop fusion | flops 786432 | bytes 2097152 | tf_op jit(solution)/shard_map/stack | solution.py:524
  (40 shorter events, 0.3 us)
Async XLA Ops:
  6.9 6.6 %collective-permute-start = (f32[4,128,128]{2,1,0:T(8,128)S(1)}, f32[4,128,128]{2,1,0:T(8,128)S(1)}, u32[]{:S(2)}, u32[]{:S(2)}) collective-permute-start(f32[4,128,128]{2,1,0:T(8,128)S(1)} %get-tuple-element.68.refs_10_.refs_3_.refs_5_), channel_id=1, source_target_pairs={{0,4},{1,5},{2,6},{3,7},{16,20},{17,21},{18,22},{19,23}} | collective-permute-start | bytes 786440 | tf_op jit(solution)/shard_map/ppermute | solution.py:401
  13.5 1.5 %copy-start.5 = (f32[4,128,128]{2,1,0:T(8,128)}, f32[4,128,128]{2,1,0:T(8,128)S(1)}, u32[]{:S(2)}) copy-start(f32[4,128,128]{2,1,0:T(8,128)S(1)} %collective-permute-done.refs_4_.refs_0_) | copy-start | bytes 786436
  13.6 11.4 %collective-permute-start.1 = (f32[4,128,128]{2,1,0:T(8,128)S(1)}, f32[4,128,128]{2,1,0:T(8,128)S(1)}, u32[]{:S(2)}, u32[]{:S(2)}) collective-permute-start(f32[4,128,128]{2,1,0:T(8,128)S(1)} %get-tuple-element.77), channel_id=1, source_target_pairs={{0,4},{4,8},{1,5},{5,9},{2,6},{6,10},{3,7},{7,11},{16,20},{20,24},... | collective-permute-start | bytes 786440 | tf_op jit(solution)/shard_map/ppermute | solution.py:401
  20.9 13.8 %copy-start.1 = (f32[4,128,128]{2,1,0:T(8,128)}, f32[4,128,128]{2,1,0:T(8,128)S(1)}, u32[]{:S(2)}) copy-start(f32[4,128,128]{2,1,0:T(8,128)S(1)} %get-tuple-element.84.refs_0_.refs_1_) | copy-start | bytes 786436
  24.9 11.8 %copy-start = (bf16[512,2048]{1,0:T(8,128)(2,1)S(1)}, bf16[512,2048]{1,0:T(8,128)(2,1)}, u32[]{:S(2)}) copy-start(bf16[512,2048]{1,0:T(8,128)(2,1)} %refs_3_.9) | copy-start | bytes 6291460
  25.2 8.5 %collective-permute-start.2 = (f32[4,128,128]{2,1,0:T(8,128)S(1)}, f32[4,128,128]{2,1,0:T(8,128)S(1)}, u32[]{:S(2)}, u32[]{:S(2)}) collective-permute-start(f32[4,128,128]{2,1,0:T(8,128)S(1)} %get-tuple-element.86), channel_id=1, source_target_pairs={{0,4},{4,8},{8,12},{1,5},{5,9},{9,13},{2,6},{6,10},{10,14},{3,7},{... | collective-permute-start | bytes 786440 | tf_op jit(solution)/shard_map/ppermute | solution.py:401
  33.1 1.6 %copy-start.3 = (f32[4,128,128]{2,1,0:T(8,128)}, f32[4,128,128]{2,1,0:T(8,128)S(1)}, u32[]{:S(2)}) copy-start(f32[4,128,128]{2,1,0:T(8,128)S(1)} %get-tuple-element.93.refs_0_) | copy-start | bytes 786436
  34.7 8.5 %collective-permute-start.5 = (f32[4,128,128]{2,1,0:T(8,128)}, f32[4,128,128]{2,1,0:T(8,128)S(1)}, u32[]{:S(2)}, u32[]{:S(2)}) collective-permute-start(f32[4,128,128]{2,1,0:T(8,128)} %get-tuple-element.101), channel_id=1, source_target_pairs={{0,4},{4,8},{8,12},{1,5},{5,9},{9,13},{2,6},{6,10},{10,14},{3,7},{... | collective-permute-start | bytes 786440 | tf_op jit(solution)/shard_map/ppermute | solution.py:401
  36.7 6.5 %copy-start.2 = (f32[4,128,128]{2,1,0:T(8,128)S(1)}, f32[4,128,128]{2,1,0:T(8,128)}, u32[]{:S(2)}) copy-start(f32[4,128,128]{2,1,0:T(8,128)} %copy-done.1) | copy-start | bytes 786436
  36.7 6.5 %copy-start.4 = (f32[4,128,128]{2,1,0:T(8,128)S(1)}, f32[4,128,128]{2,1,0:T(8,128)}, u32[]{:S(2)}) copy-start(f32[4,128,128]{2,1,0:T(8,128)} %copy-done.3) | copy-start | bytes 786436
  36.7 1.0 %copy-start.6 = (f32[4,128,128]{2,1,0:T(8,128)S(1)}, f32[4,128,128]{2,1,0:T(8,128)}, u32[]{:S(2)}) copy-start(f32[4,128,128]{2,1,0:T(8,128)} %copy-done.5) | copy-start | bytes 786436
  37.7 0.9 %copy-start.11 = (f32[4,128,128]{2,1,0:T(8,128)S(1)}, f32[4,128,128]{2,1,0:T(8,128)}, u32[]{:S(2)}) copy-start(f32[4,128,128]{2,1,0:T(8,128)} %get-tuple-element.66.reach_ref) | copy-start | bytes 786436
  38.7 0.9 %copy-start.12 = (f32[4,128,128]{2,1,0:T(8,128)S(1)}, f32[4,128,128]{2,1,0:T(8,128)}, u32[]{:S(2)}) copy-start(f32[4,128,128]{2,1,0:T(8,128)} %get-tuple-element.67.own_ref) | copy-start | bytes 786436
  39.6 5.8 %copy-start.9 = (f32[4,128,128]{2,1,0:T(8,128)S(1)}, f32[4,128,128]{2,1,0:T(8,128)}, u32[]{:S(2)}) copy-start(f32[4,128,128]{2,1,0:T(8,128)} %get-tuple-element.99.reach_ref) | copy-start | bytes 786436
  39.6 5.8 %copy-start.10 = (f32[4,128,128]{2,1,0:T(8,128)S(1)}, f32[4,128,128]{2,1,0:T(8,128)}, u32[]{:S(2)}) copy-start(f32[4,128,128]{2,1,0:T(8,128)} %get-tuple-element.100.own_ref) | copy-start | bytes 786436
  40.3 5.9 %collective-permute-start.3 = (f32[128,512]{1,0:T(8,128)S(1)}, f32[128,512]{1,0:T(8,128)S(1)}, u32[]{:S(2)}, u32[]{:S(2)}) collective-permute-start(f32[128,512]{1,0:T(8,128)S(1)} %get-tuple-element.97), channel_id=1, source_target_pairs={{0,1},{1,0},{2,3},{3,2},{4,5},{5,4},{6,7},{7,6},{8,9},{9,8},{10,11... | collective-permute-start | bytes 786440 | tf_op jit(solution)/shard_map/ppermute | solution.py:396
  40.4 5.8 %collective-permute-start.4 = (f32[128,512]{1,0:T(8,128)S(1)}, f32[128,512]{1,0:T(8,128)S(1)}, u32[]{:S(2)}, u32[]{:S(2)}) collective-permute-start(f32[128,512]{1,0:T(8,128)S(1)} %get-tuple-element.98), channel_id=1, source_target_pairs={{0,1},{1,0},{2,3},{3,2},{4,5},{5,4},{6,7},{7,6},{8,9},{9,8},{10,11... | collective-permute-start | bytes 786440 | tf_op jit(solution)/shard_map/ppermute | solution.py:396
  43.5 8.3 %collective-permute-start.9 = (f32[4,128,128]{2,1,0:T(8,128)S(1)}, f32[4,128,128]{2,1,0:T(8,128)S(1)}, u32[]{:S(2)}, u32[]{:S(2)}) collective-permute-start(f32[4,128,128]{2,1,0:T(8,128)S(1)} %get-tuple-element.110), channel_id=1, source_target_pairs={{4,8},{8,12},{5,9},{9,13},{6,10},{10,14},{7,11},{11,15},{20,24},{2... | collective-permute-start | bytes 786440 | tf_op jit(solution)/shard_map/ppermute | solution.py:401
  46.2 7.5 %copy-start.7 = (f32[4,128,128]{2,1,0:T(8,128)S(1)}, f32[4,128,128]{2,1,0:T(8,128)}, u32[]{:S(2)}) copy-start(f32[4,128,128]{2,1,0:T(8,128)} %get-tuple-element.108.reach_ref) | copy-start | bytes 786436
  46.2 7.5 %copy-start.8 = (f32[4,128,128]{2,1,0:T(8,128)S(1)}, f32[4,128,128]{2,1,0:T(8,128)}, u32[]{:S(2)}) copy-start(f32[4,128,128]{2,1,0:T(8,128)} %get-tuple-element.109.own_ref) | copy-start | bytes 786436
  46.3 7.4 %collective-permute-start.6 = (f32[1,128,512]{2,1,0:T(8,128)S(1)}, f32[1,128,512]{2,1,0:T(8,128)S(1)}, u32[]{:S(2)}, u32[]{:S(2)}) collective-permute-start(f32[1,128,512]{2,1,0:T(8,128)S(1)} %get-tuple-element.105.refs_3_), channel_id=1, source_target_pairs={{0,2},{1,3},{2,0},{3,1},{4,6},{5,7},{6,4},{7,5},{8,10},{9,11},{10,... | collective-permute-start | bytes 786440 | tf_op jit(solution)/shard_map/ppermute | solution.py:396
  46.9 7.6 %collective-permute-start.7 = (f32[128,512]{1,0:T(8,128)S(1)}, f32[128,512]{1,0:T(8,128)S(1)}, u32[]{:S(2)}, u32[]{:S(2)}) collective-permute-start(f32[128,512]{1,0:T(8,128)S(1)} %get-tuple-element.106), channel_id=1, source_target_pairs={{0,1},{1,0},{2,3},{3,2},{4,5},{5,4},{6,7},{7,6},{8,9},{9,8},{10,11... | collective-permute-start | bytes 786440 | tf_op jit(solution)/shard_map/ppermute | solution.py:396
  46.9 7.6 %collective-permute-start.8 = (f32[128,512]{1,0:T(8,128)S(1)}, f32[128,512]{1,0:T(8,128)S(1)}, u32[]{:S(2)}, u32[]{:S(2)}) collective-permute-start(f32[128,512]{1,0:T(8,128)S(1)} %get-tuple-element.107), channel_id=1, source_target_pairs={{0,1},{1,0},{2,3},{3,2},{4,5},{5,4},{6,7},{7,6},{8,9},{9,8},{10,11... | collective-permute-start | bytes 786440 | tf_op jit(solution)/shard_map/ppermute | solution.py:396
  52.0 5.5 %collective-permute-start.13 = (f32[4,128,128]{2,1,0:T(8,128)S(1)}, f32[4,128,128]{2,1,0:T(8,128)S(1)}, u32[]{:S(2)}, u32[]{:S(2)}) collective-permute-start(f32[4,128,128]{2,1,0:T(8,128)S(1)} %get-tuple-element.119), channel_id=1, source_target_pairs={{8,12},{9,13},{10,14},{11,15},{24,28},{25,29},{26,30},{27,31}} | collective-permute-start | bytes 786440 | tf_op jit(solution)/shard_map/ppermute | solution.py:401
  53.7 3.8 %copy-start.13 = (f32[4,128,128]{2,1,0:T(8,128)S(1)}, f32[4,128,128]{2,1,0:T(8,128)}, u32[]{:S(2)}) copy-start(f32[4,128,128]{2,1,0:T(8,128)} %get-tuple-element.117.reach_ref) | copy-start | bytes 786436
  53.7 3.8 %copy-start.14 = (f32[4,128,128]{2,1,0:T(8,128)S(1)}, f32[4,128,128]{2,1,0:T(8,128)}, u32[]{:S(2)}) copy-start(f32[4,128,128]{2,1,0:T(8,128)} %get-tuple-element.118.own_ref) | copy-start | bytes 786436
  54.6 6.4 %collective-permute-start.10 = (f32[1,128,512]{2,1,0:T(8,128)S(1)}, f32[1,128,512]{2,1,0:T(8,128)S(1)}, u32[]{:S(2)}, u32[]{:S(2)}) collective-permute-start(f32[1,128,512]{2,1,0:T(8,128)S(1)} %get-tuple-element.114.refs_4_), channel_id=1, source_target_pairs={{0,2},{1,3},{2,0},{3,1},{4,6},{5,7},{6,4},{7,5},{8,10},{9,11},{10,... | collective-permute-start | bytes 786440 | tf_op jit(solution)/shard_map/ppermute | solution.py:396
  55.2 3.7 %collective-permute-start.11 = (f32[128,512]{1,0:T(8,128)S(1)}, f32[128,512]{1,0:T(8,128)S(1)}, u32[]{:S(2)}, u32[]{:S(2)}) collective-permute-start(f32[128,512]{1,0:T(8,128)S(1)} %get-tuple-element.115), channel_id=1, source_target_pairs={{0,1},{1,0},{2,3},{3,2},{4,5},{5,4},{6,7},{7,6},{8,9},{9,8},{10,11... | collective-permute-start | bytes 786440 | tf_op jit(solution)/shard_map/ppermute | solution.py:396
  55.2 3.7 %collective-permute-start.12 = (f32[128,512]{1,0:T(8,128)S(1)}, f32[128,512]{1,0:T(8,128)S(1)}, u32[]{:S(2)}, u32[]{:S(2)}) collective-permute-start(f32[128,512]{1,0:T(8,128)S(1)} %get-tuple-element.116), channel_id=1, source_target_pairs={{0,1},{1,0},{2,3},{3,2},{4,5},{5,4},{6,7},{7,6},{8,9},{9,8},{10,11... | collective-permute-start | bytes 786440 | tf_op jit(solution)/shard_map/ppermute | solution.py:396
  58.3 2.7 %collective-permute-start.15 = (f32[128,512]{1,0:T(8,128)S(1)}, f32[128,512]{1,0:T(8,128)S(1)}, u32[]{:S(2)}, u32[]{:S(2)}) collective-permute-start(f32[128,512]{1,0:T(8,128)S(1)} %get-tuple-element.123), channel_id=1, source_target_pairs={{0,1},{1,0},{2,3},{3,2},{4,5},{5,4},{6,7},{7,6},{8,9},{9,8},{10,11... | collective-permute-start | bytes 786440 | tf_op jit(solution)/shard_map/ppermute | solution.py:396
  58.4 2.6 %collective-permute-start.16 = (f32[128,512]{1,0:T(8,128)S(1)}, f32[128,512]{1,0:T(8,128)S(1)}, u32[]{:S(2)}, u32[]{:S(2)}) collective-permute-start(f32[128,512]{1,0:T(8,128)S(1)} %get-tuple-element.124), channel_id=1, source_target_pairs={{0,1},{1,0},{2,3},{3,2},{4,5},{5,4},{6,7},{7,6},{8,9},{9,8},{10,11... | collective-permute-start | bytes 786440 | tf_op jit(solution)/shard_map/ppermute | solution.py:396
  59.0 9.2 %collective-permute-start.14 = (f32[1,128,512]{2,1,0:T(8,128)S(1)}, f32[1,128,512]{2,1,0:T(8,128)S(1)}, u32[]{:S(2)}, u32[]{:S(2)}) collective-permute-start(f32[1,128,512]{2,1,0:T(8,128)S(1)} %get-tuple-element.122.refs_2_), channel_id=1, source_target_pairs={{0,2},{1,3},{2,0},{3,1},{4,6},{5,7},{6,4},{7,5},{8,10},{9,11},{10,... | collective-permute-start | bytes 786440 | tf_op jit(solution)/shard_map/ppermute | solution.py:396
  61.1 11.8 %collective-permute-start.17 = (f32[1,128,512]{2,1,0:T(8,128)S(1)}, f32[1,128,512]{2,1,0:T(8,128)S(1)}, u32[]{:S(2)}, u32[]{:S(2)}) collective-permute-start(f32[1,128,512]{2,1,0:T(8,128)S(1)} %get-tuple-element.126), channel_id=1, source_target_pairs={{0,2},{1,3},{2,0},{3,1},{4,6},{5,7},{6,4},{7,5},{8,10},{9,11},{10,... | collective-permute-start | bytes 786440 | tf_op jit(solution)/shard_map/ppermute | solution.py:396

commit v8 on v7

--- a/solution.py
+++ b/solution.py
@@ -391,6 +391,36 @@
     return outs[:mid], outs[mid]
 
 
+def finish_kernel(first, count, *refs):
+    out_ref, sums_ref, sems = refs[-3:]
+    copies = []
+    for n in range(count):
+        sums_ref[n] = refs[2 * n][...] + refs[2 * n + 1][...]
+        copies.append(
+            pltpu.make_async_copy(sums_ref.at[n], out_ref.at[first + n], sems.at[n])
+        )
+        copies[n].start()
+    for copy in copies:
+        copy.wait()
+
+
+def finish(pairs, first, chunks, begun=None):
+    count, shape = len(pairs), pairs[0][0].shape
+    hbm = pl.BlockSpec(memory_space=pltpu.HBM)
+    held = [] if begun is None else [begun]
+    return pl.pallas_call(
+        functools.partial(finish_kernel, first, count),
+        in_specs=vmem(2 * count) + [hbm] * len(held),
+        out_specs=hbm,
+        out_shape=pltpu.HBM((chunks,) + shape, f32),
+        scratch_shapes=[pltpu.VMEM((count,) + shape, f32), pltpu.SemaphoreType.DMA((count,))],
+        input_output_aliases={2 * count: 0} if held else {},
+        compiler_params=pltpu.CompilerParams(vmem_limit_bytes=4 << 20),
+        cost_estimate=small_cost,
+        name="finish",
+    )(*[x for pair in pairs for x in pair], *held)
+
+
 def swapped(x, axis, bit):
     size = lax.axis_size(axis)
     return lax.ppermute(x, axis, [(i, i ^ bit) for i in range(size)])
@@ -521,7 +551,7 @@
     token = projected(done, token)
     token = add_up(done - 1, token)
     token = add_up(done, token)
-    return jnp.stack([mine + other for mine, other in outs])
+    return finish(outs[-1:], chunks - 1, chunks, finish(outs[:-1], 0, chunks))
 
 
 def solution(mesh):

time: 75.5 us -> 76.7 us (1.016)
  Pallas kernels: 29.6 us -> 31.2 us
  other arithmetic: 1.2 us -> 0 us
  waiting for transfers between devices: 25.6 us -> 26.6 us
    pallas_call x0 -> x2, Pallas kernels: none -> 1.67 us  [finish(): pl.pallas_call(functools.partial(finish_kernel, first, count), in_specs=v...]
    another operation x1 -> x0, other arithmetic: 1.04 us -> none  [shards(): return jnp.stack([mine + other for mine, other in outs])]
    ppermute x12, waiting for transfers between devices: 12.6 us -> 13.6 us  [swapped(): return lax.ppermute(x, axis, [(i, i ^ bit) for i in range(size)])]
  transfers between devices with their start and end apart: 18 -> 18, of which waited for: 8 -> 8; matrix products, arithmetic and copies ran while one was open for 0% -> 0% of each run, Pallas kernels for 29% -> 30%
where the time goes in v8:
time: 76.7 us; the launch traced here: 75.6 us
  Pallas kernels  31.2 us (41%)
  waiting for transfers between devices  26.6 us (35%)
  starting transfers between devices  14.3 us (19%)
  local copies, waits for them, and re-layouts  2.94 us (4%)
    pallas_call x4, Pallas kernels, local_terms(): pl.pallas_call(functools.partial(local_kernel, head_count, seq, fetch, ah...  24.5 us
    ppermute x12, waiting for transfers between devices, swapped(): return lax.ppermute(x, axis, [(i, i ^ bit) for i in range(size)])  13.6 us
    ppermute x6, waiting for transfers between devices, carry_on(): return lax.ppermute(x, 'seq', pairs)  13 us
    ppermute x6, starting transfers between devices, carry_on(): return lax.ppermute(x, 'seq', pairs)  9.74 us
    ppermute x12, starting transfers between devices, swapped(): return lax.ppermute(x, axis, [(i, i ^ bit) for i in range(size)])  4.6 us
    pallas_call x4, Pallas kernels, project(): pl.pallas_call(functools.partial(project_kernel, len(states), groups), in...  2.97 us
    unnamed x30, local copies, waits for them, and re-layouts  2.94 us
    pallas_call x5, Pallas kernels, step(): pl.pallas_call(functools.partial(step_kernel, len(maps)), in_specs=[pl.Bl...  1.81 us
  transfers between devices with their start and end apart: 18, of which 8 were waited for; matrix products, arithmetic and copies ran while one was open for 0% of the time, Pallas kernels for 30%

profile of v8, /device:TPU:22, one launch (start us, length us, event | category | flops | bytes accessed | tf_op | source)
XLA Modules:
  0.0 75.6 jit_solution(11729724367370064974)
XLA Ops:
  0.0 6.9 %local_terms.4 = (f32[4,128,128]{2,1,0:T(8,128)S(1)}, f32[4,128,128]{2,1,0:T(8,128)S(1)}, f32[4,128,128]{2,1,0:T(8,128)}, f32[4,128,128]{2,1,0:T(8,128)}, bf16[1...) custom-call(s32[1]{0:T(128)S(6)} %mul.3.offset_ref, ...), custom_call_target="tpu_custom_call" | custom-call | tf_op jit(solution)/shard_map/local_terms/pallas_call | solution.py:285
  6.9 0.7 collective-permute-start
  7.6 5.9 %local_terms.5 = (f32[4,128,128]{2,1,0:T(8,128)S(1)}, f32[4,128,128]{2,1,0:T(8,128)S(1)}, f32[4,128,128]{2,1,0:T(8,128)}, f32[4,128,128]{2,1,0:T(8,128)}, bf16[1...) custom-call(s32[1]{0:T(128)S(6)} %mul.3.offset_ref, ...), custom_call_target="tpu_custom_call" | custom-call | tf_op jit(solution)/shard_map/local_terms/pallas_call | solution.py:285
  13.5 0.0 collective-permute-done.refs_4_.refs_0_
  13.6 1.5 %collective-permute-start.1 = (f32[4,128,128]{2,1,0:T(8,128)S(1)}, f32[4,128,128]{2,1,0:T(8,128)S(1)}, u32[]{:S(2)}, u32[]{:S(2)}) collective-permute-start(f32[4,128,128]{2,1,0:T(8,128)S(1)} %get-tuple-element.88), channel_id=1, source_target_pairs={{0,4},{4,8},{1,5},{5,9},{2,6},{6,10},{3,7},{7,11},{16,20},{20,24},... | collective-permute-start | bytes 786440 | tf_op jit(solution)/shard_map/ppermute | solution.py:431
  15.0 5.9 %local_terms.6 = (f32[4,128,128]{2,1,0:T(8,128)S(1)}, f32[4,128,128]{2,1,0:T(8,128)S(1)}, f32[4,128,128]{2,1,0:T(8,128)}, f32[4,128,128]{2,1,0:T(8,128)}, bf16[1...) custom-call(s32[1]{0:T(128)S(6)} %mul.3.offset_ref, ...), custom_call_target="tpu_custom_call" | custom-call | tf_op jit(solution)/shard_map/local_terms/pallas_call | solution.py:285
  21.0 4.0 %collective-permute-done.1.refs_6_.refs_1_.refs_0_ = f32[4,128,128]{2,1,0:T(8,128)S(1)} collective-permute-done((f32[4,128,128]{2,1,0:T(8,128)S(1)}, f32[4,128,128]{2,1,0:T(8,128)S(1)}, u32[]{:S(2)}, u32[]{:S(2)}) %collective-permute-start.1) | collective-permute-done | bytes 262176 | tf_op jit(solution)/shard_map/ppermute | solution.py:431
  24.9 0.3 state_step.6
  25.2 2.1 %collective-permute-start.2 = (f32[4,128,128]{2,1,0:T(8,128)S(1)}, f32[4,128,128]{2,1,0:T(8,128)S(1)}, u32[]{:S(2)}, u32[]{:S(2)}) collective-permute-start(f32[4,128,128]{2,1,0:T(8,128)S(1)} %get-tuple-element.94), channel_id=1, source_target_pairs={{0,4},{4,8},{8,12},{1,5},{5,9},{9,13},{2,6},{6,10},{10,14},{3,7},{... | collective-permute-start | bytes 786440 | tf_op jit(solution)/shard_map/ppermute | solution.py:431
  27.3 5.8 %local_terms.7 = (f32[4,128,128]{2,1,0:T(8,128)S(1)}, f32[4,128,128]{2,1,0:T(8,128)S(1)}, f32[4,128,128]{2,1,0:T(8,128)}, f32[4,128,128]{2,1,0:T(8,128)}) custom-call(s32[1]{0:T(128)S(6)} %mul.3.offset_ref, s32[4,3]{1,0:T(4,128)} %resets_ref.7, bf16[128,512]{1,0:T(8,128)(2,1)S(1)} %get-tuple-element.81.refs_0_, ...), custom_call_target="tpu_custom_call" | custom-call | tf_op jit(solution)/shard_map/local_terms/pallas_call | solution.py:285
  33.1 0.6 collective-permute-done.2.refs_6_.refs_2_.refs_1_.refs_0_
  33.7 1.0 %state_step.7 = (f32[4,128,128]{2,1,0:T(8,128)}, f32[8,128]{1,0:T(8,128)S(1)}) custom-call(s32[1]{0:T(128)} %bitcast.here_ref, f32[4,128,128]{2,1,0:T(8,128)S(1)} %get-tuple-element.92.refs_0_, f32[4,128,128]{2,1,0:T(8,128)S(1)} %get-tuple-element.86.refs_0_.refs_1_, f32[4,128,128]{2,1,0:T(8,128)S(1)} %get-tuple-element.77.refs_0_.refs_1_.refs_2_, ...), custom_call_target="tpu_custom_call" | custom-call | flops 1048576 | bytes 1024 | tf_op jit(solution)/shard_map/state_step/pallas_call | solution.py:325
  34.7 1.9 %collective-permute-start.3 = (f32[4,128,128]{2,1,0:T(8,128)}, f32[4,128,128]{2,1,0:T(8,128)S(1)}, u32[]{:S(2)}, u32[]{:S(2)}) collective-permute-start(f32[4,128,128]{2,1,0:T(8,128)} %get-tuple-element.95), channel_id=1, source_target_pairs={{0,4},{4,8},{8,12},{1,5},{5,9},{9,13},{2,6},{6,10},{10,14},{3,7},{... | collective-permute-start | bytes 786440 | tf_op jit(solution)/shard_map/ppermute | solution.py:431
  36.7 1.0 %copy-done.6 = f32[4,128,128]{2,1,0:T(8,128)S(1)} copy-done((f32[4,128,128]{2,1,0:T(8,128)S(1)}, f32[4,128,128]{2,1,0:T(8,128)}, u32[]{:S(2)}) %copy-start.6) | copy-done | bytes 262168
  37.7 0.9 %copy-done.11 = f32[4,128,128]{2,1,0:T(8,128)S(1)} copy-done((f32[4,128,128]{2,1,0:T(8,128)S(1)}, f32[4,128,128]{2,1,0:T(8,128)}, u32[]{:S(2)}) %copy-start.11) | copy-done | bytes 262168
  38.7 0.9 %copy-done.12 = f32[4,128,128]{2,1,0:T(8,128)S(1)} copy-done((f32[4,128,128]{2,1,0:T(8,128)S(1)}, f32[4,128,128]{2,1,0:T(8,128)}, u32[]{:S(2)}) %copy-start.12) | copy-done | bytes 262168
  39.6 0.7 project.4
  40.3 0.1 collective-permute-start.5
  40.4 0.5 collective-permute-start.6
  40.9 2.3 %collective-permute-done.3.refs_4_.refs_2_.refs_1_.refs_0_ = f32[4,128,128]{2,1,0:T(8,128)S(1)} collective-permute-done((f32[4,128,128]{2,1,0:T(8,128)}, f32[4,128,128]{2,1,0:T(8,128)S(1)}, u32[]{:S(2)}, u32[]{:S(2)}) %collective-permute-start.3) | collective-permute-done | bytes 262176 | tf_op jit(solution)/shard_map/ppermute | solution.py:431
  43.2 0.3 state_step.8
  43.5 1.9 %collective-permute-start.4 = (f32[4,128,128]{2,1,0:T(8,128)S(1)}, f32[4,128,128]{2,1,0:T(8,128)S(1)}, u32[]{:S(2)}, u32[]{:S(2)}) collective-permute-start(f32[4,128,128]{2,1,0:T(8,128)S(1)} %get-tuple-element.100), channel_id=1, source_target_pairs={{4,8},{8,12},{5,9},{9,13},{6,10},{10,14},{7,11},{11,15},{20,24},{2... | collective-permute-start | bytes 786440 | tf_op jit(solution)/shard_map/ppermute | solution.py:431
  45.4 0.8 project.5
  46.2 0.0 collective-permute-done.6.refs_1_
  46.2 0.1 add_parts.4
  46.3 0.6 collective-permute-start.10
  46.9 0.5 collective-permute-start.9
  47.4 4.3 %collective-permute-done.4.refs_2_.refs_1_ = f32[4,128,128]{2,1,0:T(8,128)S(1)} collective-permute-done((f32[4,128,128]{2,1,0:T(8,128)S(1)}, f32[4,128,128]{2,1,0:T(8,128)S(1)}, u32[]{:S(2)}, u32[]{:S(2)}) %collective-permute-start.4) | collective-permute-done | bytes 262176 | tf_op jit(solution)/shard_map/ppermute | solution.py:431
  51.7 0.3 state_step.9
  52.0 1.7 %collective-permute-start.7 = (f32[4,128,128]{2,1,0:T(8,128)S(1)}, f32[4,128,128]{2,1,0:T(8,128)S(1)}, u32[]{:S(2)}, u32[]{:S(2)}) collective-permute-start(f32[4,128,128]{2,1,0:T(8,128)S(1)} %get-tuple-element.108), channel_id=1, source_target_pairs={{8,12},{9,13},{10,14},{11,15},{24,28},{25,29},{26,30},{27,31}} | collective-permute-start | bytes 786440 | tf_op jit(solution)/shard_map/ppermute | solution.py:431
  53.7 0.7 project.6
  54.5 0.1 collective-permute-start.13
  54.6 0.5 collective-permute-start.14
  55.1 0.1 add_parts.5
  55.1 0.6 collective-permute-start.15
  55.8 1.8 %collective-permute-done.7.refs_2_ = f32[4,128,128]{2,1,0:T(8,128)S(1)} collective-permute-done((f32[4,128,128]{2,1,0:T(8,128)S(1)}, f32[4,128,128]{2,1,0:T(8,128)S(1)}, u32[]{:S(2)}, u32[]{:S(2)}) %collective-permute-start.7) | collective-permute-done | bytes 262176 | tf_op jit(solution)/shard_map/ppermute | solution.py:431
  57.6 0.7 project.7
  58.3 0.1 collective-permute-start.11
  58.4 0.5 collective-permute-start.12
  58.9 0.1 add_parts.6
  59.0 0.6 collective-permute-start.17
  59.5 4.8 %collective-permute-done.15 = f32[1,128,512]{2,1,0:T(8,128)S(1)} collective-permute-done((f32[1,128,512]{2,1,0:T(8,128)S(1)}, f32[1,128,512]{2,1,0:T(8,128)S(1)}, u32[]{:S(2)}, u32[]{:S(2)}) %collective-permute-start.15) | collective-permute-done | bytes 262176 | tf_op jit(solution)/shard_map/ppermute | solution.py:426
  64.4 0.1 add_parts.7
  64.5 0.6 collective-permute-start.16
  65.1 4.9 %collective-permute-done.17 = f32[1,128,512]{2,1,0:T(8,128)S(1)} collective-permute-done((f32[1,128,512]{2,1,0:T(8,128)S(1)}, f32[1,128,512]{2,1,0:T(8,128)S(1)}, u32[]{:S(2)}, u32[]{:S(2)}) %collective-permute-start.17) | collective-permute-done | bytes 262176 | tf_op jit(solution)/shard_map/ppermute | solution.py:426
  70.0 0.9 %finish.2.refs_2_ = f32[4,128,512]{2,1,0:T(8,128)} custom-call(f32[128,512]{1,0:T(8,128)S(1)} %bitcast.14, f32[128,512]{1,0:T(8,128)S(1)} %bitcast.11, f32[128,512]{1,0:T(8,128)S(1)} %bitcast.15, f32[128,512]{1,0:T(8,128)S(1)} %bitcast.13, f32[128,512]{1,0:T(8,128)S(1)} %bitcast.16, f32[128,512]{1,0:T(8,128)S(1)} %bitcast.17), custom_call_target="tpu_custom_call" | custom-call | flops 1048576 | bytes 1024 | tf_op jit(solution)/shard_map/finish/pallas_call | solution.py:411
  70.9 3.8 %collective-permute-done.16 = f32[1,128,512]{2,1,0:T(8,128)S(1)} collective-permute-done((f32[1,128,512]{2,1,0:T(8,128)S(1)}, f32[1,128,512]{2,1,0:T(8,128)S(1)}, u32[]{:S(2)}, u32[]{:S(2)}) %collective-permute-start.16) | collective-permute-done | bytes 262176 | tf_op jit(solution)/shard_map/ppermute | solution.py:426
  74.7 0.7 finish.3
  (37 shorter events, 0.1 us)
Async XLA Ops:
  6.9 6.6 %collective-permute-start = (f32[4,128,128]{2,1,0:T(8,128)S(1)}, f32[4,128,128]{2,1,0:T(8,128)S(1)}, u32[]{:S(2)}, u32[]{:S(2)}) collective-permute-start(f32[4,128,128]{2,1,0:T(8,128)S(1)} %get-tuple-element.71.refs_10_.refs_3_.refs_5_), channel_id=1, source_target_pairs={{0,4},{1,5},{2,6},{3,7},{16,20},{17,21},{18,22},{19,23}} | collective-permute-start | bytes 786440 | tf_op jit(solution)/shard_map/ppermute | solution.py:431
  13.5 1.5 %copy-start.5 = (f32[4,128,128]{2,1,0:T(8,128)}, f32[4,128,128]{2,1,0:T(8,128)S(1)}, u32[]{:S(2)}) copy-start(f32[4,128,128]{2,1,0:T(8,128)S(1)} %collective-permute-done.refs_4_.refs_0_) | copy-start | bytes 786436
  13.6 11.4 %collective-permute-start.1 = (f32[4,128,128]{2,1,0:T(8,128)S(1)}, f32[4,128,128]{2,1,0:T(8,128)S(1)}, u32[]{:S(2)}, u32[]{:S(2)}) collective-permute-start(f32[4,128,128]{2,1,0:T(8,128)S(1)} %get-tuple-element.88), channel_id=1, source_target_pairs={{0,4},{4,8},{1,5},{5,9},{2,6},{6,10},{3,7},{7,11},{16,20},{20,24},... | collective-permute-start | bytes 786440 | tf_op jit(solution)/shard_map/ppermute | solution.py:431
  20.9 13.8 %copy-start.1 = (f32[4,128,128]{2,1,0:T(8,128)}, f32[4,128,128]{2,1,0:T(8,128)S(1)}, u32[]{:S(2)}) copy-start(f32[4,128,128]{2,1,0:T(8,128)S(1)} %get-tuple-element.86.refs_0_.refs_1_) | copy-start | bytes 786436
  24.9 11.8 %copy-start = (bf16[512,2048]{1,0:T(8,128)(2,1)S(1)}, bf16[512,2048]{1,0:T(8,128)(2,1)}, u32[]{:S(2)}) copy-start(bf16[512,2048]{1,0:T(8,128)(2,1)} %refs_3_.9) | copy-start | bytes 6291460
  25.2 8.5 %collective-permute-start.2 = (f32[4,128,128]{2,1,0:T(8,128)S(1)}, f32[4,128,128]{2,1,0:T(8,128)S(1)}, u32[]{:S(2)}, u32[]{:S(2)}) collective-permute-start(f32[4,128,128]{2,1,0:T(8,128)S(1)} %get-tuple-element.94), channel_id=1, source_target_pairs={{0,4},{4,8},{8,12},{1,5},{5,9},{9,13},{2,6},{6,10},{10,14},{3,7},{... | collective-permute-start | bytes 786440 | tf_op jit(solution)/shard_map/ppermute | solution.py:431
  33.1 1.6 %copy-start.3 = (f32[4,128,128]{2,1,0:T(8,128)}, f32[4,128,128]{2,1,0:T(8,128)S(1)}, u32[]{:S(2)}) copy-start(f32[4,128,128]{2,1,0:T(8,128)S(1)} %get-tuple-element.92.refs_0_) | copy-start | bytes 786436
  34.7 8.5 %collective-permute-start.3 = (f32[4,128,128]{2,1,0:T(8,128)}, f32[4,128,128]{2,1,0:T(8,128)S(1)}, u32[]{:S(2)}, u32[]{:S(2)}) collective-permute-start(f32[4,128,128]{2,1,0:T(8,128)} %get-tuple-element.95), channel_id=1, source_target_pairs={{0,4},{4,8},{8,12},{1,5},{5,9},{9,13},{2,6},{6,10},{10,14},{3,7},{... | collective-permute-start | bytes 786440 | tf_op jit(solution)/shard_map/ppermute | solution.py:431
  36.7 6.5 %copy-start.2 = (f32[4,128,128]{2,1,0:T(8,128)S(1)}, f32[4,128,128]{2,1,0:T(8,128)}, u32[]{:S(2)}) copy-start(f32[4,128,128]{2,1,0:T(8,128)} %copy-done.1) | copy-start | bytes 786436
  36.7 6.5 %copy-start.4 = (f32[4,128,128]{2,1,0:T(8,128)S(1)}, f32[4,128,128]{2,1,0:T(8,128)}, u32[]{:S(2)}) copy-start(f32[4,128,128]{2,1,0:T(8,128)} %copy-done.3) | copy-start | bytes 786436
  36.7 1.0 %copy-start.6 = (f32[4,128,128]{2,1,0:T(8,128)S(1)}, f32[4,128,128]{2,1,0:T(8,128)}, u32[]{:S(2)}) copy-start(f32[4,128,128]{2,1,0:T(8,128)} %copy-done.5) | copy-start | bytes 786436
  37.7 0.9 %copy-start.11 = (f32[4,128,128]{2,1,0:T(8,128)S(1)}, f32[4,128,128]{2,1,0:T(8,128)}, u32[]{:S(2)}) copy-start(f32[4,128,128]{2,1,0:T(8,128)} %get-tuple-element.96.reach_ref) | copy-start | bytes 786436
  38.7 0.9 %copy-start.12 = (f32[4,128,128]{2,1,0:T(8,128)S(1)}, f32[4,128,128]{2,1,0:T(8,128)}, u32[]{:S(2)}) copy-start(f32[4,128,128]{2,1,0:T(8,128)} %get-tuple-element.97.own_ref) | copy-start | bytes 786436
  39.6 5.8 %copy-start.9 = (f32[4,128,128]{2,1,0:T(8,128)S(1)}, f32[4,128,128]{2,1,0:T(8,128)}, u32[]{:S(2)}) copy-start(f32[4,128,128]{2,1,0:T(8,128)} %get-tuple-element.103.reach_ref) | copy-start | bytes 786436
  39.6 5.8 %copy-start.10 = (f32[4,128,128]{2,1,0:T(8,128)S(1)}, f32[4,128,128]{2,1,0:T(8,128)}, u32[]{:S(2)}) copy-start(f32[4,128,128]{2,1,0:T(8,128)} %get-tuple-element.104.own_ref) | copy-start | bytes 786436
  40.3 5.9 %collective-permute-start.5 = (f32[128,512]{1,0:T(8,128)S(1)}, f32[128,512]{1,0:T(8,128)S(1)}, u32[]{:S(2)}, u32[]{:S(2)}) collective-permute-start(f32[128,512]{1,0:T(8,128)S(1)} %get-tuple-element.101), channel_id=1, source_target_pairs={{0,1},{1,0},{2,3},{3,2},{4,5},{5,4},{6,7},{7,6},{8,9},{9,8},{10,11... | collective-permute-start | bytes 786440 | tf_op jit(solution)/shard_map/ppermute | solution.py:426
  40.4 5.8 %collective-permute-start.6 = (f32[128,512]{1,0:T(8,128)S(1)}, f32[128,512]{1,0:T(8,128)S(1)}, u32[]{:S(2)}, u32[]{:S(2)}) collective-permute-start(f32[128,512]{1,0:T(8,128)S(1)} %get-tuple-element.102), channel_id=1, source_target_pairs={{0,1},{1,0},{2,3},{3,2},{4,5},{5,4},{6,7},{7,6},{8,9},{9,8},{10,11... | collective-permute-start | bytes 786440 | tf_op jit(solution)/shard_map/ppermute | solution.py:426
  43.5 8.3 %collective-permute-start.4 = (f32[4,128,128]{2,1,0:T(8,128)S(1)}, f32[4,128,128]{2,1,0:T(8,128)S(1)}, u32[]{:S(2)}, u32[]{:S(2)}) collective-permute-start(f32[4,128,128]{2,1,0:T(8,128)S(1)} %get-tuple-element.100), channel_id=1, source_target_pairs={{4,8},{8,12},{5,9},{9,13},{6,10},{10,14},{7,11},{11,15},{20,24},{2... | collective-permute-start | bytes 786440 | tf_op jit(solution)/shard_map/ppermute | solution.py:431
  46.2 7.5 %copy-start.7 = (f32[4,128,128]{2,1,0:T(8,128)S(1)}, f32[4,128,128]{2,1,0:T(8,128)}, u32[]{:S(2)}) copy-start(f32[4,128,128]{2,1,0:T(8,128)} %get-tuple-element.111.reach_ref) | copy-start | bytes 786436
  46.2 7.5 %copy-start.8 = (f32[4,128,128]{2,1,0:T(8,128)S(1)}, f32[4,128,128]{2,1,0:T(8,128)}, u32[]{:S(2)}) copy-start(f32[4,128,128]{2,1,0:T(8,128)} %get-tuple-element.112.own_ref) | copy-start | bytes 786436
  46.3 7.4 %collective-permute-start.10 = (f32[1,128,512]{2,1,0:T(8,128)S(1)}, f32[1,128,512]{2,1,0:T(8,128)S(1)}, u32[]{:S(2)}, u32[]{:S(2)}) collective-permute-start(f32[1,128,512]{2,1,0:T(8,128)S(1)} %get-tuple-element.107.refs_3_), channel_id=1, source_target_pairs={{0,2},{1,3},{2,0},{3,1},{4,6},{5,7},{6,4},{7,5},{8,10},{9,11},{10,... | collective-permute-start | bytes 786440 | tf_op jit(solution)/shard_map/ppermute | solution.py:426
  46.9 8.2 %collective-permute-start.8 = (f32[128,512]{1,0:T(8,128)S(1)}, f32[128,512]{1,0:T(8,128)S(1)}, u32[]{:S(2)}, u32[]{:S(2)}) collective-permute-start(f32[128,512]{1,0:T(8,128)S(1)} %get-tuple-element.109), channel_id=1, source_target_pairs={{0,1},{1,0},{2,3},{3,2},{4,5},{5,4},{6,7},{7,6},{8,9},{9,8},{10,11... | collective-permute-start | bytes 786440 | tf_op jit(solution)/shard_map/ppermute | solution.py:426
  46.9 8.2 %collective-permute-start.9 = (f32[128,512]{1,0:T(8,128)S(1)}, f32[128,512]{1,0:T(8,128)S(1)}, u32[]{:S(2)}, u32[]{:S(2)}) collective-permute-start(f32[128,512]{1,0:T(8,128)S(1)} %get-tuple-element.110), channel_id=1, source_target_pairs={{0,1},{1,0},{2,3},{3,2},{4,5},{5,4},{6,7},{7,6},{8,9},{9,8},{10,11... | collective-permute-start | bytes 786440 | tf_op jit(solution)/shard_map/ppermute | solution.py:426
  52.0 5.5 %collective-permute-start.7 = (f32[4,128,128]{2,1,0:T(8,128)S(1)}, f32[4,128,128]{2,1,0:T(8,128)S(1)}, u32[]{:S(2)}, u32[]{:S(2)}) collective-permute-start(f32[4,128,128]{2,1,0:T(8,128)S(1)} %get-tuple-element.108), channel_id=1, source_target_pairs={{8,12},{9,13},{10,14},{11,15},{24,28},{25,29},{26,30},{27,31}} | collective-permute-start | bytes 786440 | tf_op jit(solution)/shard_map/ppermute | solution.py:431
  53.7 3.8 %copy-start.13 = (f32[4,128,128]{2,1,0:T(8,128)S(1)}, f32[4,128,128]{2,1,0:T(8,128)}, u32[]{:S(2)}) copy-start(f32[4,128,128]{2,1,0:T(8,128)} %get-tuple-element.90.reach_ref) | copy-start | bytes 786436
  53.7 3.8 %copy-start.14 = (f32[4,128,128]{2,1,0:T(8,128)S(1)}, f32[4,128,128]{2,1,0:T(8,128)}, u32[]{:S(2)}) copy-start(f32[4,128,128]{2,1,0:T(8,128)} %get-tuple-element.91.own_ref) | copy-start | bytes 786436
  54.5 4.4 %collective-permute-start.13 = (f32[128,512]{1,0:T(8,128)S(1)}, f32[128,512]{1,0:T(8,128)S(1)}, u32[]{:S(2)}, u32[]{:S(2)}) collective-permute-start(f32[128,512]{1,0:T(8,128)S(1)} %get-tuple-element.119), channel_id=1, source_target_pairs={{0,1},{1,0},{2,3},{3,2},{4,5},{5,4},{6,7},{7,6},{8,9},{9,8},{10,11... | collective-permute-start | bytes 786440 | tf_op jit(solution)/shard_map/ppermute | solution.py:426
  54.6 4.3 %collective-permute-start.14 = (f32[128,512]{1,0:T(8,128)S(1)}, f32[128,512]{1,0:T(8,128)S(1)}, u32[]{:S(2)}, u32[]{:S(2)}) collective-permute-start(f32[128,512]{1,0:T(8,128)S(1)} %get-tuple-element.120), channel_id=1, source_target_pairs={{0,1},{1,0},{2,3},{3,2},{4,5},{5,4},{6,7},{7,6},{8,9},{9,8},{10,11... | collective-permute-start | bytes 786440 | tf_op jit(solution)/shard_map/ppermute | solution.py:426
  55.1 9.2 %collective-permute-start.15 = (f32[1,128,512]{2,1,0:T(8,128)S(1)}, f32[1,128,512]{2,1,0:T(8,128)S(1)}, u32[]{:S(2)}, u32[]{:S(2)}) collective-permute-start(f32[1,128,512]{2,1,0:T(8,128)S(1)} %get-tuple-element.115.refs_4_), channel_id=1, source_target_pairs={{0,2},{1,3},{2,0},{3,1},{4,6},{5,7},{6,4},{7,5},{8,10},{9,11},{10,... | collective-permute-start | bytes 786440 | tf_op jit(solution)/shard_map/ppermute | solution.py:426
  58.3 6.1 %collective-permute-start.11 = (f32[128,512]{1,0:T(8,128)S(1)}, f32[128,512]{1,0:T(8,128)S(1)}, u32[]{:S(2)}, u32[]{:S(2)}) collective-permute-start(f32[128,512]{1,0:T(8,128)S(1)} %get-tuple-element.117), channel_id=1, source_target_pairs={{0,1},{1,0},{2,3},{3,2},{4,5},{5,4},{6,7},{7,6},{8,9},{9,8},{10,11... | collective-permute-start | bytes 786440 | tf_op jit(solution)/shard_map/ppermute | solution.py:426
  58.4 6.0 %collective-permute-start.12 = (f32[128,512]{1,0:T(8,128)S(1)}, f32[128,512]{1,0:T(8,128)S(1)}, u32[]{:S(2)}, u32[]{:S(2)}) collective-permute-start(f32[128,512]{1,0:T(8,128)S(1)} %get-tuple-element.118), channel_id=1, source_target_pairs={{0,1},{1,0},{2,3},{3,2},{4,5},{5,4},{6,7},{7,6},{8,9},{9,8},{10,11... | collective-permute-start | bytes 786440 | tf_op jit(solution)/shard_map/ppermute | solution.py:426
  59.0 11.0 %collective-permute-start.17 = (f32[1,128,512]{2,1,0:T(8,128)S(1)}, f32[1,128,512]{2,1,0:T(8,128)S(1)}, u32[]{:S(2)}, u32[]{:S(2)}) collective-permute-start(f32[1,128,512]{2,1,0:T(8,128)S(1)} %get-tuple-element.121.refs_2_), channel_id=1, source_target_pairs={{0,2},{1,3},{2,0},{3,1},{4,6},{5,7},{6,4},{7,5},{8,10},{9,11},{10,... | collective-permute-start | bytes 786440 | tf_op jit(solution)/shard_map/ppermute | solution.py:426
  64.5 10.3 %collective-permute-start.16 = (f32[1,128,512]{2,1,0:T(8,128)S(1)}, f32[1,128,512]{2,1,0:T(8,128)S(1)}, u32[]{:S(2)}, u32[]{:S(2)}) collective-permute-start(f32[1,128,512]{2,1,0:T(8,128)S(1)} %get-tuple-element.123), channel_id=1, source_target_pairs={{0,2},{1,3},{2,0},{3,1},{4,6},{5,7},{6,4},{7,5},{8,10},{9,11},{10,... | collective-permute-start | bytes 786440 | tf_op jit(solution)/shard_map/ppermute | solution.py:426
